TPU v7x, 128 devices: a whole 4x4x4 slice. The times are simulated.
128 devices in a mesh: adapter: 32 (over y, x, core), mp: 4 (over z).
Axes of the slice: x: 4, y: 4, z: 4, core: 2. Of those that a mesh axis runs over, the one named last changes fastest.
Arguments:
- hidden: bfloat16 [8192, 4096], P('adapter', 'mp'), may hold values from -8 to 8
- subsets: int32 [8192, 8], P('adapter'), may hold values from 0 to 31, all different within a row; in each aligned block of 256 rows (0 to 255, 256 to 511, ...) at most 128 rows name the same one
- down_weight: bfloat16 [32, 4096, 256], P('adapter', 'mp'), may hold values from -0.09375 to 0.09375
- up_weight: bfloat16 [32, 256, 4096], P('adapter', None, 'mp'), may hold values from -0.375 to 0.375
- query_weight: bfloat16 [4096, 4096], P('mp'), may hold values from -0.08 to 2.08
- key_weight: bfloat16 [4096, 4096], P('mp'), may hold values from -0.08 to 2.08
Outputs:
- joined: bfloat16 [8192, 4096], P('adapter', 'mp')
Inputs may be any that keep to these rules, and one draw needn't show every extreme that they name: `subsets`: each row names 8 different adapters; within the rows of one index of the adapter axis no adapter is named by more than 128 rows.
All inputs are finite; a program needn't handle non-finite values.
Results may differ from a plain program's by a relative error of at most 0.025.
Values may be sent and summed in bfloat16 or wider, within the bound.
No kernel may reach another device: no remote copies, remote signals or barrier semaphores. Data moves between devices by JAX's collectives and lax.ppermute only.
A program may use at most 192 MiB of HBM per device.

v0:
```python
import jax
import jax.numpy as jnp
from jax import lax
from jax.sharding import PartitionSpec as P

D = 4096


def sent_to_all(x, axis):
    size = lax.axis_size(axis)
    return lax.all_to_all(jnp.broadcast_to(x[None], (size, *x.shape)), axis, 0, 0, tiled=True)


def over_copies(x, axis):
    return sent_to_all(x, axis).astype(jnp.float32).sum(axis=0)


def split_up(x, dim, size):
    before, after = (x.shape[:dim], x.shape[dim + 1 :])
    return jnp.moveaxis(x.reshape(*before, size, -1, *after), dim, 0)


def sent_and_summed(x, axis, dim):
    size = lax.axis_size(axis)
    parts = lax.all_to_all(split_up(x, dim, size), axis, 0, 0, tiled=True)
    return jnp.sum(parts.astype(jnp.float32), axis=0)


def in_order(parts, dim):
    parts = jnp.moveaxis(parts, 0, dim)
    shape = parts.shape
    return parts.reshape(*shape[:dim], shape[dim] * shape[dim + 1], *shape[dim + 2 :])


def collect(x, axis, dim):
    parts = sent_to_all(x, axis)
    return in_order(parts, dim)


def taken_together(x, axis):
    return sent_to_all(x, axis).sum(axis=0)


def tally(partial_sum):
    summed = over_copies(partial_sum.astype(jnp.bfloat16), "mp").astype(jnp.float32)
    return jnp.maximum(summed, 0.0).astype(jnp.bfloat16)


def per_device(hidden, subsets, down_weight, up_weight, query_weight, key_weight):
    row_count, width_local = hidden.shape
    fanout = subsets.shape[1]
    total_adapters = lax.axis_size("adapter") * down_weight.shape[0]
    capacity = min(row_count, 2 * row_count * fanout // total_adapters)
    labels = jnp.arange(total_adapters, dtype=jnp.int32)
    picks = (subsets[:, :, None] == labels[None, None, :]).astype(jnp.int32)
    chosen = jnp.sum(picks, axis=1)
    before = jnp.cumsum(chosen, axis=0) - chosen
    slot_rank = jnp.sum(picks * before[:, None, :], axis=2)
    flat_slot = subsets * capacity + slot_rank
    row_ids = jnp.broadcast_to(jnp.arange(row_count, dtype=jnp.int32)[:, None], flat_slot.shape)
    source_row = (
        jnp.zeros((total_adapters * capacity,), jnp.int32)
        .at[flat_slot.reshape(-1)]
        .set(row_ids.reshape(-1))
    )
    filled = jnp.zeros((total_adapters * capacity,), jnp.bool_).at[flat_slot.reshape(-1)].set(True)
    outgoing = jnp.where(
        filled[:, None], jnp.take(hidden, source_row, axis=0), jnp.zeros((), jnp.bfloat16)
    )
    outgoing = outgoing.reshape(total_adapters, capacity, width_local)
    query_part = jnp.dot(hidden, query_weight, preferred_element_type=jnp.float32)
    query_piece = sent_and_summed(query_part.astype(jnp.bfloat16), "mp", 1).astype(jnp.bfloat16)
    query = collect(query_piece, "mp", 1)
    probe = lax.dot_general(
        query, key_weight, (((1,), (1,)), ((), ())), preferred_element_type=jnp.float32
    ).astype(jnp.bfloat16)
    block = outgoing
    bottle = tally(
        jnp.einsum(
            "ncd,ndb->ncb",
            block,
            lax.all_gather(down_weight, "adapter", axis=0, tiled=True),
            preferred_element_type=jnp.float32,
        )
    )
    block = bottle
    returned = jnp.einsum(
        "ncb,nbd->ncd",
        block,
        lax.all_gather(up_weight, "adapter", axis=0, tiled=True),
        preferred_element_type=jnp.float32,
    ).astype(jnp.bfloat16)
    picked = jnp.take(returned.reshape(total_adapters * capacity, width_local), flat_slot, axis=0)
    widened = picked.astype(jnp.float32)
    base = hidden.astype(jnp.float32)
    probe_wide = probe.astype(jnp.float32)
    own_term = jnp.sum(base * probe_wide, axis=1)
    partial_logit = (
        jnp.einsum("rkd,rd->rk", widened, probe_wide, precision=lax.Precision.HIGHEST)
        + own_term[:, None]
    )
    logits = taken_together(partial_logit, "mp") * D ** (-0.5)
    share = jax.nn.softmax(logits, axis=-1)
    joined = base + jnp.einsum("rk,rkd->rd", share, widened, precision=lax.Precision.HIGHEST)
    return joined.astype(jnp.bfloat16)


def solution(mesh):
    return jax.shard_map(
        per_device,
        mesh=mesh,
        in_specs=(
            P("adapter", "mp"),
            P("adapter", None),
            P("adapter", "mp", None),
            P("adapter", None, "mp"),
            P("mp", None),
            P("mp", None),
        ),
        out_specs=P("adapter", "mp"),
        check_vma=False,
    )
```

profile of v0, /device:TPU:0, one launch (start us, length us, event | category | flops | bytes accessed | tf_op | source)
XLA Modules:
  0.0 257.7 jit_solution(9191249026218513655)
XLA Ops:
  6.5 0.0 all-gather.3.cloned.1.call-start
  6.5 0.7 all-gather.3.cloned.1.call-update
  7.3 0.0 all-gather.5.cloned.1.call-start
  7.3 0.7 all-gather.5.cloned.1.call-update
  8.0 5.9 %convolution_convert_fusion.1 = bf16[256,4096]{1,0:T(8,128)(2,1)S(1)} fusion(bf16[256,1024]{1,0:T(8,128)(2,1)} %param.6, bf16[1024,4096]{1,0:T(8,128)(2,1)} %param.10), kind=kOutput, calls=%fused_computation.11 | convolution fusion | flops 2148532224 | bytes 11010048 | tf_op jit(solution)/shard_map/dot_general | solution.py:71
  13.9 0.0 copy-start.1
  13.9 0.0 copy-start
  13.9 1.6 copy.58
  15.5 5.4 %all-to-all-start.1 = ((bf16[4,256,1024]{2,1,0:T(8,128)(2,1)}), bf16[4,256,1024]{2,1,0:T(8,128)(2,1)S(1)}, u32[]{:S(2)}, u32[]{:S(2)}) async-start(bf16[4,256,1024]{2,1,0:T(8,128)(2,1)} %bitcast.53), calls=%async_computation.1 | async-start | bytes 4194304 | tf_op jit(solution)/shard_map/all_to_all | solution.py:25
  20.9 0.0 copy-done.1
  21.0 0.6 reduce-window.6
  21.5 0.2 slice_reduce_fusion
  21.8 0.1 fusion.18
  21.9 0.1 select_reduce_fusion
  21.9 0.1 copy.39
  22.1 0.1 reshape.87
  22.2 0.1 reshape.120
  22.3 8.1 %scatter_custom_fusion.1 = s32[4096]{0:T(1024)S(1)} fusion(s32[2048]{0:T(1024)S(1)} %bitcast.55, s32[2048]{0:T(1024)S(1)} %reshape.120, s32[]{:T(128)} %constant.18.clone.1), kind=kCustom, calls=%fused_computation.45 | custom fusion | bytes 16388 | tf_op jit(solution)/shard_map/scatter | solution.py:64
  30.4 0.0 copy-done
  30.4 18.2 %gather_fusion = bf16[4096,1024]{1,0:T(8,128)(2,1)} fusion(bf16[256,1024]{1,0:T(8,128)(2,1)S(1)} %copy-done, s32[4096]{0:T(1024)S(1)} %fusion.19), kind=kCustom, calls=%fused_computation | custom fusion | bytes 16793600 | tf_op jit(solution)/shard_map/jit(_take)/gather | solution.py:68
  48.7 9.1 %scatter_custom_fusion = pred[4096]{0:T(1024)(128)(4,1)S(1)} fusion(s32[2048]{0:T(1024)S(1)} %bitcast.56, pred[2048]{0:T(1024)(128)(4,1)S(1)} %broadcast.50, pred[]{:T(512)} %constant.27.clone.1), kind=kCustom, calls=%fused_computation.48 | custom fusion | bytes 4097 | tf_op jit(solution)/shard_map/scatter | solution.py:66
  57.8 0.0 all-to-all-done.1
  57.8 0.4 reduce_sum.69
  58.2 0.2 copy.43
  58.4 1.4 broadcast_in_dim.97
  59.9 4.8 %all-to-all-start.2 = ((bf16[4,256,1024]{1,2,0:T(8,128)(2,1)}), bf16[4,256,1024]{1,2,0:T(8,128)(2,1)}, u32[]{:S(2)}, u32[]{:S(2)}) async-start(bf16[4,256,1024]{1,2,0:T(8,128)(2,1)} %broadcast_in_dim.97), calls=%async_computation.2 | async-start | bytes 4194304 | tf_op jit(solution)/shard_map/all_to_all | solution.py:11
  64.7 19.8 %all-gather.3.cloned.1.call-done = bf16[32,1024,256]{2,1,0:T(8,128)(2,1)} async-done(((bf16[1,1024,256]{2,1,0:T(8,128)(2,1)}), bf16[32,1024,256]{2,1,0:T(8,128)(2,1)}) %all-gather.3.cloned.1.call-update) | async-done | bytes 16777232 | tf_op jit(solution)/shard_map/all_gather | solution.py:82
  84.5 9.7 %fusion.12 = bf16[32,128,256]{2,1,0:T(8,128)(2,1)S(1)} fusion(bf16[32,1024,256]{2,1,0:T(8,128)(2,1)} %all-gather.3.cloned.1.call-done, bf16[32,128,1024]{2,1,0:T(8,128)(2,1)} %bitcast.52, pred[32,128]{1,0:T(8,128)(4,1)S(1)} %and_bitcast_fusion, pred[32,128]{1,0:T(8,128)(4,1)S(1)} %bitcast.57), kind=kOutput, calls=%fused_computation.22 | convolution fusion | flops 2156920832 | bytes 27271168 | tf_op jit(solution)/shard_map/ncd,ndb->ncb/dot_general | solution.py:79
  94.2 0.0 all-to-all-done.2
  94.2 4.3 %broadcast_in_dim.94 = bf16[4,32,128,256]{3,2,1,0:T(8,128)(2,1)} broadcast(bf16[32,128,256]{2,1,0:T(8,128)(2,1)S(1)} %fusion.12), dimensions={1,2,3} | broadcast | bytes 10485760 | tf_op jit(solution)/shard_map/broadcast_in_dim | solution.py:11
  98.4 5.8 %all-to-all-start = ((bf16[4,32,128,256]{3,2,1,0:T(8,128)(2,1)}), bf16[4,32,128,256]{3,2,1,0:T(8,128)(2,1)}, u32[]{:S(2)}, u32[]{:S(2)}) async-start(bf16[4,32,128,256]{3,2,1,0:T(8,128)(2,1)} %broadcast_in_dim.94), calls=%async_computation | async-start | bytes 16777216 | tf_op jit(solution)/shard_map/all_to_all | solution.py:11
  104.3 0.1 copy.40
  104.4 0.1 reshape.102
  104.5 0.2 copy.38
  104.7 6.5 %fusion.15 = (f32[256]{0:T(256)S(1)}, bf16[256,1024]{1,0:T(8,128)(2,1)S(1)}) fusion(bf16[256,1024]{1,0:T(8,128)(2,1)S(1)} %copy-done, bf16[256,4096]{0,1:T(8,128)(2,1)} %bitcast.10, bf16[1024,4096]{1,0:T(8,128)(2,1)} %param.11), kind=kOutput, calls=%fused_computation.26 | convolution fusion | flops 2148794112 | bytes 11535360 | tf_op jit(solution)/shard_map/dot_general | solution.py:74
  111.3 87.5 %all-to-all-done = bf16[4,32,128,256]{3,2,1,0:T(8,128)(2,1)} async-done(((bf16[4,32,128,256]{3,2,1,0:T(8,128)(2,1)}), bf16[4,32,128,256]{3,2,1,0:T(8,128)(2,1)}, u32[]{:S(2)}, u32[]{:S(2)}) %all-to-all-start) | async-done | bytes 8388640 | tf_op jit(solution)/shard_map/all_to_all | solution.py:11
  198.8 4.9 %convert_reduce_fusion = bf16[32,128,256]{2,1,0:T(8,128)(2,1)S(1)} fusion(bf16[4,32,128,256]{3,2,1,0:T(8,128)(2,1)} %all-to-all-done), kind=kLoop, calls=%fused_computation.4 | loop fusion | flops 7340032 | bytes 10485760 | tf_op jit(solution)/shard_map/reduce_sum | solution.py:15
  203.7 0.0 all-gather.5.cloned.1.call-done
  203.8 11.4 %convolution_convert_fusion = bf16[32,128,1024]{2,1,0:T(8,128)(2,1)} fusion(bf16[32,256,1024]{2,1,0:T(8,128)(2,1)} %all-gather.5.cloned.1.call-done, bf16[32,128,256]{2,1,0:T(8,128)(2,1)S(1)} %convert_reduce_fusion), kind=kOutput, calls=%fused_computation.10 | convolution fusion | flops 2154823680 | bytes 27262976 | tf_op jit(solution)/shard_map/ncb,nbd->ncd/dot_general | solution.py:87
  215.1 15.4 %gather_fusion.1 = bf16[2048,1024]{1,0:T(8,128)(2,1)} fusion(bf16[4096,1024]{1,0:T(8,128)(2,1)} %bitcast.51, s32[2048]{0:T(1024)S(1)} %broadcast_clamp_fusion), kind=kCustom, calls=%fused_computation.1 | custom fusion | bytes 8396800 | tf_op jit(solution)/shard_map/jit(_take)/gather | solution.py:93
  230.6 5.3 %fusion.8 = f32[256,1,8]{2,1,0:T(1,128)S(1)} fusion(bf16[2048,1024]{1,0:T(8,128)(2,1)} %gather_fusion.1, pred[256,8]{1,0:T(8,128)(4,1)S(1)} %copy.38, bf16[256,1024,1]{1,0,2:T(8,128)(2,1)S(1)} %bitcast.58), kind=kOutput, calls=%fused_computation.17 | convolution fusion | flops 6291456 | bytes 4728832 | tf_op jit(solution)/shard_map/rkd,rd->rk/dot_general | solution.py:99
  235.9 0.1 copy.45
  236.0 7.8 %all_to_all.20 = f32[4,256,8]{1,2,0:T(8,128)S(1)} all-to-all(f32[4,256,8]{1,2,0:T(8,128)S(1)} %broadcast_in_dim.98), channel_id=1, replica_groups=mesh['adapter'=32,'mp'=4] {'mp'}, dimensions={0} | all-to-all | bytes 65536 | tf_op jit(solution)/shard_map/all_to_all | solution.py:11
  243.8 0.1 copy.46
  244.0 5.8 %fusion.7 = f32[256,1,1024]{2,1,0:T(1,128)S(1)} fusion(f32[256,8,1]{1,2,0:T(1,128)S(1)} %copy.46, bf16[2048,1024]{1,0:T(8,128)(2,1)} %gather_fusion.1, pred[256,8]{1,0:T(8,128)(4,1)S(1)} %copy.38), kind=kOutput, calls=%fused_computation.16 | convolution fusion | flops 27262976 | bytes 5253120 | tf_op jit(solution)/shard_map/rk,rkd->rd/dot_general | solution.py:104
  249.8 1.1 fusion.16
  (18 shorter events, 0.2 us)
Async XLA Ops:
  6.5 77.9 %all-gather.3.cloned.1.call-start = ((), (), s32[]{:S(2)}) async-start(), calls=%async_computation.4 | async-start | bytes 17301504 | tf_op jit(solution)/shard_map/all_gather | solution.py:82
  7.3 196.5 %all-gather.5.cloned.1.call-start = ((), (), s32[]{:S(2)}) async-start(), calls=%async_computation.5 | async-start | bytes 17301504 | tf_op jit(solution)/shard_map/all_gather | solution.py:90
  13.9 7.0 %copy-start.1 = (s32[256,8]{0,1:T(8,128)S(1)}, s32[256,8]{0,1:T(8,128)}, u32[]{:S(2)}) copy-start(s32[256,8]{0,1:T(8,128)} %param.7) | copy-start | bytes 24580
  13.9 16.5 %copy-start = (bf16[256,1024]{1,0:T(8,128)(2,1)S(1)}, bf16[256,1024]{1,0:T(8,128)(2,1)}, u32[]{:S(2)}) copy-start(bf16[256,1024]{1,0:T(8,128)(2,1)} %param.6) | copy-start | bytes 1572868
  15.5 42.3 %all-to-all-start.1 = ((bf16[4,256,1024]{2,1,0:T(8,128)(2,1)}), bf16[4,256,1024]{2,1,0:T(8,128)(2,1)S(1)}, u32[]{:S(2)}, u32[]{:S(2)}) async-start(bf16[4,256,1024]{2,1,0:T(8,128)(2,1)} %bitcast.53), calls=%async_computation.1 | async-start | bytes 4194304 | tf_op jit(solution)/shard_map/all_to_all | solution.py:25
  59.9 34.3 %all-to-all-start.2 = ((bf16[4,256,1024]{1,2,0:T(8,128)(2,1)}), bf16[4,256,1024]{1,2,0:T(8,128)(2,1)}, u32[]{:S(2)}, u32[]{:S(2)}) async-start(bf16[4,256,1024]{1,2,0:T(8,128)(2,1)} %broadcast_in_dim.97), calls=%async_computation.2 | async-start | bytes 4194304 | tf_op jit(solution)/shard_map/all_to_all | solution.py:11
  98.4 100.4 %all-to-all-start = ((bf16[4,32,128,256]{3,2,1,0:T(8,128)(2,1)}), bf16[4,32,128,256]{3,2,1,0:T(8,128)(2,1)}, u32[]{:S(2)}, u32[]{:S(2)}) async-start(bf16[4,32,128,256]{3,2,1,0:T(8,128)(2,1)} %broadcast_in_dim.94), calls=%async_computation | async-start | bytes 16777216 | tf_op jit(solution)/shard_map/all_to_all | solution.py:11
Sparse Core Ops, SparseCore 0:
  9.6 74.8 all-gather.2
  86.7 71.8 all-gather.4
where the time goes:
time: 258 us
  waiting for transfers between devices  109 us (42%)
  local copies, waits for them, and re-layouts  59.5 us (23%)
  matrix products  44.6 us (17%)
  starting transfers between devices  16.1 us (6%)
  between operations  13.6 us (5%)
  blocking collectives  7.81 us (3%)
  other arithmetic  7.31 us (3%)
    all_to_all x2, waiting for transfers between devices, sent_to_all(): lax.all_to_all(jnp.broadcast_to(x[None], (size, *x.shape)), axis, 0, 0, t...  87.5 us
    all_gather x1, waiting for transfers between devices, per_device(): lax.all_gather(down_weight, 'adapter', axis=0, tiled=True)  19.8 us
    gather x1, local copies, waits for them, and re-layouts, per_device(): jnp.take(hidden, source_row, axis=0)  18.2 us
    gather x1, local copies, waits for them, and re-layouts, per_device(): jnp.take(returned.reshape(total_adapters * capacity, width_local), flat_s...  15.4 us
    dot_general x1, matrix products, per_device(): jnp.einsum('ncb,nbd->ncd', block, lax.all_gather(up_weight, 'adapter', ax...  11.4 us
    all_to_all x2, starting transfers between devices, sent_to_all(): lax.all_to_all(jnp.broadcast_to(x[None], (size, *x.shape)), axis, 0, 0, t...  10.6 us
    dot_general x1, matrix products, per_device(): jnp.einsum('ncd,ndb->ncb', block, lax.all_gather(down_weight, 'adapter',...  9.7 us
    scatter x1, local copies, waits for them, and re-layouts, per_device(): jnp.zeros((total_adapters * capacity,), jnp.bool_).at[flat_slot.reshape(-1)]  9.12 us
  transfers between devices with their start and end apart: 5, of which 2 were waited for; matrix products, arithmetic and copies ran while one was open for 28% of the time, Pallas kernels for 0%

commit v1 on v0

v1 whole, which is shorter than its diff:
```python
import jax
import jax.numpy as jnp
from jax import lax
from jax.experimental import pallas as pl
from jax.experimental.pallas import tpu as pltpu
from jax.sharding import Mesh, PartitionSpec as P

D = 4096
ADAPTERS = 32
B = 256
CAP = 128
ROWS = 256
WIDTH = 1024
TILE = 16
PAIRS = 2560
PIECE = PAIRS // 4
BUF = PAIRS + CAP
BF16 = jnp.bfloat16
F32 = jnp.float32
VMEM = 56 * 1024 * 1024


def params(**kw):
    return pltpu.CompilerParams(vmem_limit_bytes=VMEM, **kw)


def dot(a, b, ca, cb):
    return lax.dot_general(a, b, (((ca,), (cb,)), ((), ())), preferred_element_type=F32)


def iota(shape, dim):
    return lax.broadcasted_iota(jnp.int32, shape, dim)


def whole():
    return pl.BlockSpec(memory_space=pltpu.VMEM)


def plan_kernel(sub_ref, hid_ref, ext_ref, rank_ref, off_ref):
    ids = iota((ADAPTERS, ROWS), 0)
    chosen = jnp.zeros((ADAPTERS, ROWS), F32)
    for k in range(sub_ref.shape[0]):
        chosen = chosen + jnp.where(sub_ref[k : k + 1, :] == ids, 1.0, 0.0)
    named = chosen.astype(BF16)
    earlier = jnp.where(iota((ROWS, ROWS), 0) < iota((ROWS, ROWS), 1), 1.0, 0.0)
    before = dot(named, earlier.astype(BF16), 1, 0)
    rank = jnp.where(chosen > 0.5, before, -1.0)
    rank_ref[...] = rank
    ext_ref[0:ROWS, :] = hid_ref[...]
    ext_ref[ROWS:, 0:ROWS] = rank.astype(BF16)
    ext_ref[ROWS:, ROWS:] = jnp.zeros((ADAPTERS, WIDTH - ROWS), BF16)
    count = jnp.sum(chosen, axis=1, keepdims=True)
    padded = jnp.broadcast_to(jnp.floor((count + (TILE - 1)) * (1.0 / TILE)) * TILE, (ADAPTERS, 128))
    lower = jnp.where(iota((ADAPTERS, ADAPTERS), 1) < iota((ADAPTERS, ADAPTERS), 0), 1.0, 0.0)
    off_ref[...] = dot(lower.astype(BF16), padded.astype(BF16), 1, 0).astype(jnp.int32)


def plan(subsets, hidden):
    return pl.pallas_call(
        plan_kernel,
        out_shape=(
            jax.ShapeDtypeStruct((ROWS + ADAPTERS, WIDTH), BF16),
            jax.ShapeDtypeStruct((ADAPTERS, ROWS), F32),
            jax.ShapeDtypeStruct((ADAPTERS, 128), jnp.int32),
        ),
        in_specs=[whole(), whole()],
        out_specs=(whole(), whole(), whole()),
        compiler_params=params(),
        name="plan",
    )(subsets.T, hidden)


def query_kernel(hid_ref, w_ref, out_ref):
    out_ref[0] = dot(hid_ref[...], w_ref[...], 1, 0).astype(BF16)


def query_parts(hidden, weight):
    return pl.pallas_call(
        query_kernel,
        out_shape=jax.ShapeDtypeStruct((4, ROWS, WIDTH), BF16),
        grid=(4,),
        in_specs=[
            pl.BlockSpec((ROWS, WIDTH), lambda j: (0, 0)),
            pl.BlockSpec((WIDTH, WIDTH), lambda j: (0, j)),
        ],
        out_specs=pl.BlockSpec((1, ROWS, WIDTH), lambda j: (j, 0, 0)),
        compiler_params=params(),
        name="query_parts",
    )(hidden, weight)


def probe_kernel(q_ref, w_ref, hid_ref, probe_ref, own_ref, acc):
    j = pl.program_id(0)

    @pl.when(j == 0)
    def _():
        acc[...] = jnp.zeros_like(acc)

    acc[...] += dot(q_ref[0], w_ref[...], 1, 1)

    @pl.when(j == 3)
    def _():
        probe = acc[...].astype(BF16)
        probe_ref[...] = probe
        own = jnp.sum(probe.astype(F32) * hid_ref[...].astype(F32), axis=1, keepdims=True)
        own_ref[...] = jnp.broadcast_to(own, (ROWS, 128)).T[0:8, :]


def probe_of(query, weight, hidden):
    return pl.pallas_call(
        probe_kernel,
        out_shape=(
            jax.ShapeDtypeStruct((ROWS, WIDTH), BF16),
            jax.ShapeDtypeStruct((8, ROWS), F32),
        ),
        grid=(4,),
        in_specs=[
            pl.BlockSpec((1, ROWS, WIDTH), lambda j: (j, 0, 0)),
            pl.BlockSpec((WIDTH, WIDTH), lambda j: (0, j)),
            pl.BlockSpec((ROWS, WIDTH), lambda j: (0, 0)),
        ],
        out_specs=(
            pl.BlockSpec((ROWS, WIDTH), lambda j: (0, 0)),
            pl.BlockSpec((8, ROWS), lambda j: (0, 0)),
        ),
        scratch_shapes=[pltpu.VMEM((ROWS, WIDTH), F32)],
        compiler_params=params(),
        name="probe",
    )(query, weight, hidden)


def adapter_of(pos_ref, sx, sy, rc):
    y = (pos_ref[0] + (4 - sy)) & 3
    x = (pos_ref[1] + (4 - sx)) & 3
    return (y * 4 + x) * 2 + (pos_ref[2] ^ rc)


def squeeze_kernel(pos_ref, *refs):
    exts, weights, outs, rows = refs[:4], refs[4:12], refs[12:16], refs[16]
    for s in range(4):
        rows[s * ROWS : (s + 1) * ROWS, :] = exts[s][0:ROWS, :]
    ids = iota((ADAPTERS, ROWS), 0)
    slots = iota((CAP, ROWS), 0).astype(F32)
    for i in range(8):
        a = adapter_of(pos_ref, 0, i // 2, i % 2)
        part = dot(rows[...], weights[i][...], 1, 0).astype(BF16)
        for s in range(4):
            ranks = exts[s][ROWS:, 0:ROWS].astype(F32)
            mine = jnp.sum(jnp.where(ids == a, ranks, 0.0), axis=0, keepdims=True)
            pick = jnp.where(slots == mine, 1.0, 0.0).astype(BF16)
            outs[s][i] = dot(pick, part[s * ROWS : (s + 1) * ROWS, :], 1, 0).astype(BF16)


def squeeze(pos, exts, weights):
    return pl.pallas_call(
        squeeze_kernel,
        out_shape=[jax.ShapeDtypeStruct((8, CAP, B), BF16)] * 4,
        in_specs=[pl.BlockSpec(memory_space=pltpu.SMEM)] + [whole()] * 12,
        out_specs=[whole()] * 4,
        scratch_shapes=[pltpu.VMEM((4 * ROWS, WIDTH), BF16)],
        compiler_params=params(),
        name="squeeze",
    )(pos, *exts, *weights)


def pack_kernel(pos_ref, off_ref, *refs):
    blocks, outs, buf = refs[:4], refs[4:8], refs[8]
    buf[...] = jnp.zeros_like(buf)
    for t in range(4):
        for i in range(8):
            a = adapter_of(pos_ref, t, i // 2, i % 2)
            at = pl.ds(pl.multiple_of(off_ref[a], TILE), CAP)
            buf[at, :] = buf[at, :] + blocks[t][i]
    for s in range(4):
        p = (pos_ref[3] + s) & 3
        outs[s][...] = buf[pl.ds(pl.multiple_of(p * PIECE, TILE), PIECE), :]


def pack(pos, off, blocks):
    return pl.pallas_call(
        pack_kernel,
        out_shape=[jax.ShapeDtypeStruct((PIECE, B), BF16)] * 4,
        in_specs=[pl.BlockSpec(memory_space=pltpu.SMEM)] * 2 + [whole()] * 4,
        out_specs=[whole()] * 4,
        scratch_shapes=[pltpu.VMEM((BUF, B), BF16)],
        compiler_params=params(),
        name="pack",
    )(pos, off, *blocks)


def unpack_into(buf, pos_ref, pieces):
    for s in range(4):
        p = (pos_ref[3] + (4 - s)) & 3
        buf[pl.ds(pl.multiple_of(p * PIECE, TILE), PIECE), :] = pieces[s][...]
    buf[PAIRS:, :] = jnp.zeros((CAP, B), BF16)


PER = 4


def logits_kernel(pos_ref, off_ref, g0, g1, g2, g3, rank_ref, probe_ref, own_ref, up_ref, out_ref, buf):
    step = pl.program_id(0)

    @pl.when(step == 0)
    def _():
        unpack_into(buf, pos_ref, (g0, g1, g2, g3))
        out_ref[ADAPTERS:, :] = own_ref[...]

    slots = iota((CAP, ROWS), 0).astype(F32)
    for k in range(PER):
        a = step * PER + k
        seg = buf[pl.ds(pl.multiple_of(off_ref[a], TILE), CAP), :]
        pick = jnp.where(slots == rank_ref[pl.ds(a, 1), :], 1.0, 0.0).astype(BF16)
        spread = dot(seg, pick, 0, 0)
        turned = dot(up_ref[k], probe_ref[...], 1, 1)
        out_ref[pl.ds(a, 1), :] = jnp.sum(spread * turned, axis=0, keepdims=True)


def smem():
    return pl.BlockSpec(memory_space=pltpu.SMEM)


def const(shape):
    return pl.BlockSpec(shape, lambda i: (0,) * len(shape))


def logits_of(pos, off, pieces, rank, probe, own, up):
    return pl.pallas_call(
        logits_kernel,
        out_shape=jax.ShapeDtypeStruct((ADAPTERS + 8, ROWS), F32),
        grid=(ADAPTERS // PER,),
        in_specs=[smem(), smem()]
        + [const((PIECE, B))] * 4
        + [const((ADAPTERS, ROWS)), const((ROWS, WIDTH)), const((8, ROWS))]
        + [pl.BlockSpec((PER, B, WIDTH), lambda i: (i, 0, 0))],
        out_specs=const((ADAPTERS + 8, ROWS)),
        scratch_shapes=[pltpu.VMEM((BUF, B), BF16)],
        compiler_params=params(),
        name="logits",
    )(pos, off, *pieces, rank, probe, own, up)


def join_kernel(
    pos_ref, off_ref, g0, g1, g2, g3, l0, l1, l2, l3, rank_ref, hid_ref, up_ref, out_ref, buf, share, mix, acc
):
    step = pl.program_id(0)

    @pl.when(step == 0)
    def _():
        unpack_into(buf, pos_ref, (g0, g1, g2, g3))
        total = (l0[...] + l1[...]) + (l2[...] + l3[...])
        logits = (total[0:ADAPTERS] + total[ADAPTERS : ADAPTERS + 1]) * D ** (-0.5)
        chosen = rank_ref[...] >= 0.0
        logits = jnp.where(chosen, logits, -jnp.inf)
        e = jnp.where(chosen, jnp.exp(logits - jnp.max(logits, axis=0, keepdims=True)), 0.0)
        share[...] = e / jnp.sum(e, axis=0, keepdims=True)
        acc[...] = hid_ref[...].astype(F32)

    slots = iota((CAP, ROWS), 0).astype(F32)
    for k in range(PER):
        a = step * PER + k
        seg = buf[pl.ds(pl.multiple_of(off_ref[a], TILE), CAP), :]
        pick = jnp.where(slots == rank_ref[pl.ds(a, 1), :], share[pl.ds(a, 1), :], 0.0).astype(BF16)
        mix[:, k * B : (k + 1) * B] = dot(pick, seg, 0, 0).astype(BF16)
    acc[...] += dot(mix[...], up_ref[...].reshape(PER * B, WIDTH), 1, 0)

    @pl.when(step == ADAPTERS // PER - 1)
    def _():
        out_ref[...] = acc[...].astype(BF16)


def join(pos, off, pieces, parts, rank, hidden, up):
    return pl.pallas_call(
        join_kernel,
        out_shape=jax.ShapeDtypeStruct((ROWS, WIDTH), BF16),
        grid=(ADAPTERS // PER,),
        in_specs=[smem(), smem()]
        + [const((PIECE, B))] * 4
        + [const((ADAPTERS + 8, ROWS))] * 4
        + [const((ADAPTERS, ROWS)), const((ROWS, WIDTH))]
        + [pl.BlockSpec((PER, B, WIDTH), lambda i: (i, 0, 0))],
        out_specs=const((ROWS, WIDTH)),
        scratch_shapes=[
            pltpu.VMEM((BUF, B), BF16),
            pltpu.VMEM((ADAPTERS, ROWS), F32),
            pltpu.VMEM((ROWS, PER * B), BF16),
            pltpu.VMEM((ROWS, WIDTH), F32),
        ],
        compiler_params=params(),
        name="join",
    )(pos, off, *pieces, *parts, rank, hidden, up)


def shifted(x, axis, s):
    return lax.ppermute(x, axis, [(i, (i + s) % 4) for i in range(4)])


def round_trip(x, axis):
    return [x] + [shifted(x, axis, s) for s in (1, 2, 3)]


def per_device(hidden, subsets, down_weight, up_weight, query_weight, key_weight):
    pos = jnp.stack([lax.axis_index(n) for n in ("y", "x", "core", "mp")]).astype(jnp.int32)
    up = lax.all_gather(up_weight, ("y", "x", "core"), axis=0, tiled=True)
    ext, rank, off = plan(subsets, hidden)
    off = off[:, 0]

    downs = round_trip(down_weight[0], "y")
    swap = [(0, 1), (1, 0)]
    weights = []
    for w in downs:
        weights += [w, lax.ppermute(w, "core", swap)]
    exts = round_trip(ext, "x")

    parts = query_parts(hidden, query_weight)
    parts = lax.all_to_all(parts, "mp", 0, 0, tiled=True)
    query = jnp.sum(parts.astype(F32), axis=0).astype(BF16)
    query = lax.all_to_all(jnp.broadcast_to(query[None], (4, ROWS, WIDTH)), "mp", 0, 0, tiled=True)
    probe, own = probe_of(query, key_weight, hidden)

    made = squeeze(pos, exts, weights)
    back = [made[0]] + [shifted(made[4 - t], "x", t) for t in (1, 2, 3)]
    sent = pack(pos, off, back)
    got = [sent[0]] + [shifted(sent[s], "mp", s) for s in (1, 2, 3)]
    total = (got[0].astype(F32) + got[1].astype(F32)) + (got[2].astype(F32) + got[3].astype(F32))
    bottle = jnp.maximum(total, 0.0).astype(BF16)
    pieces = round_trip(bottle, "mp")

    partial = logits_of(pos, off, pieces, rank, probe, own, up)
    partials = round_trip(partial, "mp")
    return join(pos, off, pieces, partials, rank, hidden, up)


def solution(mesh):
    split = Mesh(mesh.devices.reshape(4, 4, 2, 4), ("y", "x", "core", "mp"))
    rows = ("y", "x", "core")
    return jax.shard_map(
        per_device,
        mesh=split,
        in_specs=(
            P(rows, "mp"),
            P(rows, None),
            P(rows, "mp", None),
            P(rows, None, "mp"),
            P("mp", None),
            P("mp", None),
        ),
        out_specs=P(rows, "mp"),
        check_vma=False,
    )
```

time: 258 us -> 209 us (0.81); the launches traced: 258 us -> 206 us
  Pallas kernels: 0 us -> 58.9 us
  local copies, waits for them, and re-layouts: 59.5 us -> 6.49 us
  matrix products: 44.6 us -> 0 us
  waiting for transfers between devices: 109 us -> 78.8 us
  starting transfers between devices: 16.1 us -> 45.6 us
  blocking collectives: 7.81 us -> 0 us
  other arithmetic: 7.31 us -> 2.23 us
    all_to_all x3 -> x2, waiting for transfers between devices: 87.5 us -> 0.01 us  [the longest x1 0.01 us: per_device(): parts = lax.all_to_all(parts, 'mp', 0, 0, tiled=True)]
    ppermute x0 -> x22, waiting for transfers between devices: none -> 78.1 us  [the longest x18 78.1 us: shifted(): return lax.ppermute(x, axis, [(i, (i + s) % 4) for i in range(4)])]
    pallas_call x0 -> x7, Pallas kernels: none -> 58.9 us  [the longest x1 14.4 us: squeeze(): pl.pallas_call(squeeze_kernel, out_shape=[jax.ShapeDtypeStruct((8, CAP, B...]
    dot_general x6 -> x0, matrix products: 44.6 us -> none  [the longest x1 11.4 us: per_device(): jnp.einsum('ncb,nbd->ncd', block, lax.all_gather(up_weight, 'adapter', ax...]
    ppermute x0 -> x22, starting transfers between devices: none -> 35.6 us  [the longest x18 34.6 us: shifted(): return lax.ppermute(x, axis, [(i, (i + s) % 4) for i in range(4)])]
    gather x2 -> x0, local copies, waits for them, and re-layouts: 33.7 us -> none  [the longest x1 18.2 us: per_device(): jnp.take(hidden, source_row, axis=0)]
    all_gather x2 -> x1, waiting for transfers between devices: 19.8 us -> 0.02 us  [per_device(): up = lax.all_gather(up_weight, ('y', 'x', 'core'), axis=0, tiled=True)]
    scatter x2 -> x0, local copies, waits for them, and re-layouts: 17.2 us -> none  [the longest x1 9.12 us: per_device(): jnp.zeros((total_adapters * capacity,), jnp.bool_).at[flat_slot.reshape(-1)]]
  transfers between devices with their start and end apart: 5 -> 25, of which waited for: 2 -> 11; matrix products, arithmetic and copies ran while one was open for 28% -> 2% of each run, Pallas kernels for 0% -> 16%
where the time goes in v1:
time: 209 us; the launch traced here: 206 us
  waiting for transfers between devices  78.8 us (38%)
  Pallas kernels  58.9 us (28%)
  starting transfers between devices  45.6 us (22%)
  between operations  13.5 us (6%)
  local copies, waits for them, and re-layouts  6.49 us (3%)
  other arithmetic  2.23 us (1%)
    ppermute x18, waiting for transfers between devices, shifted(): return lax.ppermute(x, axis, [(i, (i + s) % 4) for i in range(4)])  78.1 us
    ppermute x18, starting transfers between devices, shifted(): return lax.ppermute(x, axis, [(i, (i + s) % 4) for i in range(4)])  34.6 us
    pallas_call x1, Pallas kernels, squeeze(): pl.pallas_call(squeeze_kernel, out_shape=[jax.ShapeDtypeStruct((8, CAP, B...  14.4 us
    pallas_call x1, Pallas kernels, join(): pl.pallas_call(join_kernel, out_shape=jax.ShapeDtypeStruct((ROWS, WIDTH),...  12.9 us
    pallas_call x1, Pallas kernels, logits_of(): pl.pallas_call(logits_kernel, out_shape=jax.ShapeDtypeStruct((ADAPTERS +...  12.6 us
    pallas_call x1, Pallas kernels, probe_of(): pl.pallas_call(probe_kernel, out_shape=(jax.ShapeDtypeStruct((ROWS, WIDTH...  7.37 us
    pallas_call x1, Pallas kernels, query_parts(): pl.pallas_call(query_kernel, out_shape=jax.ShapeDtypeStruct((4, ROWS, WID...  6.63 us
    all_to_all x1, starting transfers between devices, per_device(): parts = lax.all_to_all(parts, 'mp', 0, 0, tiled=True)  5.52 us
  transfers between devices with their start and end apart: 25, of which 11 were waited for; matrix products, arithmetic and copies ran while one was open for 2% of the time, Pallas kernels for 16%

profile of v1, /device:TPU:0, one launch (start us, length us, event | category | flops | bytes accessed | tf_op | source)
XLA Modules:
  0.0 205.6 jit_solution(15942217055727304453)
XLA Ops:
  6.5 0.7 all-gather.2.cloned.1.call-update
  7.3 6.6 %query_parts.1 = bf16[4,256,1024]{2,1,0:T(8,128)(2,1)} custom-call(bf16[256,1024]{1,0:T(8,128)(2,1)} %hid_ref.7, bf16[1024,4096]{1,0:T(8,128)(2,1)} %w_ref.2), custom_call_target="tpu_custom_call" | custom-call | tf_op jit(solution)/shard_map/query_parts/pallas_call | solution.py:78
  13.9 5.5 %all-to-all-start = ((bf16[4,256,1024]{2,1,0:T(8,128)(2,1)}), bf16[4,256,1024]{2,1,0:T(8,128)(2,1)S(1)}, u32[]{:S(2)}, u32[]{:S(2)}) async-start(bf16[4,256,1024]{2,1,0:T(8,128)(2,1)} %query_parts.1), calls=%async_computation | async-start | bytes 4194304 | tf_op jit(solution)/shard_map/all_to_all | solution.py:316
  19.4 1.6 collective-permute-start.4
  21.0 2.9 %collective-permute-start.6 = (bf16[1024,256]{1,0:T(8,128)(2,1)S(1)}, bf16[1024,256]{1,0:T(8,128)(2,1)}, u32[]{:S(2)}, u32[]{:S(2)}) collective-permute-start(bf16[1024,256]{1,0:T(8,128)(2,1)S(1)} %bitcast.8), channel_id=1, source_target_pairs={{0,64},{32,96},{64,0},{96,32},{1,65},{33,97},{65,1},{97,33},{2,66}... | collective-permute-start | bytes 1572872 | tf_op jit(solution)/shard_map/ppermute | solution.py:295
  23.9 2.1 %plan.1 = (bf16[288,1024]{1,0:T(8,128)(2,1)}, f32[32,256]{1,0:T(8,128)}, s32[32,128]{1,0:T(8,128)}) custom-call(s32[8,256]{1,0:T(8,128)} %bitcast.11, bf16[256,1024]{1,0:T(8,128)(2,1)} %hid_ref.7), custom_call_target="tpu_custom_call" | custom-call | tf_op jit(solution)/shard_map/plan/pallas_call | solution.py:59
  26.0 1.5 collective-permute-start
  27.5 1.4 collective-permute-start.8
  28.8 13.0 %collective-permute-done.4.refs_6_ = bf16[1024,256]{1,0:T(8,128)(2,1)} collective-permute-done((bf16[1024,256]{1,0:T(8,128)(2,1)S(1)}, bf16[1024,256]{1,0:T(8,128)(2,1)}, u32[]{:S(2)}, u32[]{:S(2)}) %collective-permute-start.4) | collective-permute-done | bytes 524320 | tf_op jit(solution)/shard_map/ppermute | solution.py:295
  41.8 3.0 %collective-permute-start.1 = (bf16[288,1024]{1,0:T(8,128)(2,1)}, bf16[288,1024]{1,0:T(8,128)(2,1)}, u32[]{:S(2)}, u32[]{:S(2)}) collective-permute-start(bf16[288,1024]{1,0:T(8,128)(2,1)} %get-tuple-element.19.refs_0_), channel_id=1, source_target_pairs={{0,16},{8,24},{16,0},{24,8},{1,17},{9,25},{17,1},{25,9},{2,18},{10... | collective-permute-start | bytes 1769480 | tf_op jit(solution)/shard_map/ppermute | solution.py:295
  44.8 10.3 %collective-permute-done.6.refs_8_ = bf16[1024,256]{1,0:T(8,128)(2,1)} collective-permute-done((bf16[1024,256]{1,0:T(8,128)(2,1)S(1)}, bf16[1024,256]{1,0:T(8,128)(2,1)}, u32[]{:S(2)}, u32[]{:S(2)}) %collective-permute-start.6) | collective-permute-done | bytes 524320 | tf_op jit(solution)/shard_map/ppermute | solution.py:295
  55.1 2.8 %collective-permute-start.2 = (bf16[288,1024]{1,0:T(8,128)(2,1)}, bf16[288,1024]{1,0:T(8,128)(2,1)}, u32[]{:S(2)}, u32[]{:S(2)}) collective-permute-start(bf16[288,1024]{1,0:T(8,128)(2,1)} %get-tuple-element.19.refs_0_), channel_id=1, source_target_pairs={{0,24},{8,0},{16,8},{24,16},{1,25},{9,1},{17,9},{25,17},{2,26},{10... | collective-permute-start | bytes 1769480 | tf_op jit(solution)/shard_map/ppermute | solution.py:295
  57.9 0.0 collective-permute-done.8.refs_10_
  57.9 0.0 collective-permute-start.5
  57.9 0.0 collective-permute-done.3.refs_5_
  57.9 0.0 copy-start.10
  57.9 0.5 collective-permute-start.7
  58.4 0.3 copy-done.10
  58.7 0.5 collective-permute-start.9
  59.2 0.0 all-to-all-done
  59.2 0.4 reduce_sum.12
  59.6 1.6 broadcast_in_dim.2
  61.3 4.5 %all-to-all-start.1 = ((bf16[4,256,1024]{2,1,0:T(8,128)(2,1)}), bf16[4,256,1024]{2,1,0:T(8,128)(2,1)S(1)}, u32[]{:S(2)}, u32[]{:S(2)}) async-start(bf16[4,256,1024]{2,1,0:T(8,128)(2,1)} %broadcast_in_dim.2), calls=%async_computation.1 | async-start | bytes 4194304 | tf_op jit(solution)/shard_map/all_to_all | solution.py:318
  65.8 0.7 pad_add_fusion.pos_ref
  66.4 0.0 collective-permute-done.1.refs_2_
  66.4 9.1 %collective-permute-done.2.refs_3_ = bf16[288,1024]{1,0:T(8,128)(2,1)} collective-permute-done((bf16[288,1024]{1,0:T(8,128)(2,1)}, bf16[288,1024]{1,0:T(8,128)(2,1)}, u32[]{:S(2)}, u32[]{:S(2)}) %collective-permute-start.2) | collective-permute-done | bytes 589856 | tf_op jit(solution)/shard_map/ppermute | solution.py:295
  75.5 0.0 collective-permute-done.5.refs_7_
  75.5 0.0 collective-permute-done.7.refs_9_
  75.5 14.4 %squeeze.9 = (bf16[8,128,256]{2,1,0:T(8,128)(2,1)}, bf16[8,128,256]{2,1,0:T(8,128)(2,1)}, bf16[8,128,256]{2,1,0:T(8,128)(2,1)}, bf16[8,128,256]{2,1,0:T(8,128)(2,1)}) custom-call(s32[4]{0:T(128)} %pad_add_fusion.pos_ref, bf16[288,1024]{1,0:T(8,128)(2,1)} %get-tuple-element.19.refs_0_, bf16[288,1024]{1,0:T(8,128)(2,1)} %copy-done.5, ...), custom_call_target="tpu_custom_call" | custom-call | tf_op jit(solution)/shard_map/squeeze/pallas_call | solution.py:155
  90.0 0.0 collective-permute-start.10
  90.0 5.1 %collective-permute-start.11 = (bf16[8,128,256]{2,1,0:T(8,128)(2,1)}, bf16[8,128,256]{2,1,0:T(8,128)(2,1)S(1)}, u32[]{:S(2)}, u32[]{:S(2)}) collective-permute-start(bf16[8,128,256]{2,1,0:T(8,128)(2,1)} %get-tuple-element.22), channel_id=1, source_target_pairs={{0,16},{8,24},{16,0},{24,8},{1,17},{9,25},{17,1},{25,9},{2,18},{10... | collective-permute-start | bytes 1572872 | tf_op jit(solution)/shard_map/ppermute | solution.py:295
  95.1 0.0 collective-permute-start.12
  95.1 0.6 slice_reduce_fusion.off_ref
  95.7 20.9 %collective-permute-done.10.refs_1_ = bf16[8,128,256]{2,1,0:T(8,128)(2,1)S(1)} collective-permute-done((bf16[8,128,256]{2,1,0:T(8,128)(2,1)}, bf16[8,128,256]{2,1,0:T(8,128)(2,1)S(1)}, u32[]{:S(2)}, u32[]{:S(2)}) %collective-permute-start.10) | collective-permute-done | bytes 524320 | tf_op jit(solution)/shard_map/ppermute | solution.py:295
  116.6 9.0 %collective-permute-done.11.refs_2_ = bf16[8,128,256]{2,1,0:T(8,128)(2,1)S(1)} collective-permute-done((bf16[8,128,256]{2,1,0:T(8,128)(2,1)}, bf16[8,128,256]{2,1,0:T(8,128)(2,1)S(1)}, u32[]{:S(2)}, u32[]{:S(2)}) %collective-permute-start.11) | collective-permute-done | bytes 524320 | tf_op jit(solution)/shard_map/ppermute | solution.py:295
  125.6 0.8 copy-done.7
  126.4 0.2 copy-done.8
  126.6 3.0 %pack.1 = (bf16[640,256]{1,0:T(8,128)(2,1)}, bf16[640,256]{1,0:T(8,128)(2,1)}, bf16[640,256]{1,0:T(8,128)(2,1)}, bf16[640,256]{1,0:T(8,128)(2,1)}) custom-call(s32[4]{0:T(128)} %pad_add_fusion.pos_ref, s32[32]{0:T(128)} %slice_reduce_fusion.off_ref, bf16[8,128,256]{2,1,0:T(8,128)(2,1)} %get-tuple-element.20.refs_0_, bf16[8,128,256]{2,1,0:T(8,128)(2,1)} %copy-done.6, ...), custom_call_target="tpu_custom_call" | custom-call | tf_op jit(solution)/shard_map/pack/pallas_call | solution.py:180
  129.6 1.6 collective-permute-start.13
  131.1 2.9 %collective-permute-start.14 = (bf16[640,256]{1,0:T(8,128)(2,1)}, bf16[640,256]{1,0:T(8,128)(2,1)S(1)}, u32[]{:S(2)}, u32[]{:S(2)}) collective-permute-start(bf16[640,256]{1,0:T(8,128)(2,1)} %get-tuple-element.26), channel_id=1, source_target_pairs={{0,2},{1,3},{2,0},{3,1},{4,6},{5,7},{6,4},{7,5},{8,10},{9,11},{10,... | collective-permute-start | bytes 983048 | tf_op jit(solution)/shard_map/ppermute | solution.py:295
  134.0 1.4 collective-permute-start.15
  135.4 6.0 %collective-permute-done.13 = bf16[640,256]{1,0:T(8,128)(2,1)S(1)} collective-permute-done((bf16[640,256]{1,0:T(8,128)(2,1)}, bf16[640,256]{1,0:T(8,128)(2,1)S(1)}, u32[]{:S(2)}, u32[]{:S(2)}) %collective-permute-start.13) | collective-permute-done | bytes 327712 | tf_op jit(solution)/shard_map/ppermute | solution.py:295
  141.3 4.5 %collective-permute-done.14 = bf16[640,256]{1,0:T(8,128)(2,1)S(1)} collective-permute-done((bf16[640,256]{1,0:T(8,128)(2,1)}, bf16[640,256]{1,0:T(8,128)(2,1)S(1)}, u32[]{:S(2)}, u32[]{:S(2)}) %collective-permute-start.14) | collective-permute-done | bytes 327712 | tf_op jit(solution)/shard_map/ppermute | solution.py:295
  145.8 1.2 maximum_convert_fusion.g0
  147.0 1.5 collective-permute-start.16
  148.5 2.4 %collective-permute-start.17 = (bf16[640,256]{1,0:T(8,128)(2,1)S(1)}, bf16[640,256]{1,0:T(8,128)(2,1)S(1)}, u32[]{:S(2)}, u32[]{:S(2)}) collective-permute-start(bf16[640,256]{1,0:T(8,128)(2,1)S(1)} %maximum_convert_fusion.g0), channel_id=1, source_target_pairs={{0,2},{1,3},{2,0},{3,1},{4,6},{5,7},{6,4},{7,5},{8,10},{9,11},{10,... | collective-permute-start | bytes 983048 | tf_op jit(solution)/shard_map/ppermute | solution.py:295
  150.9 1.4 collective-permute-start.18
  152.3 0.0 all-to-all-done.1.q_ref
  152.3 1.4 copy-done
  153.7 7.4 %probe.1 = (bf16[256,1024]{1,0:T(8,128)(2,1)}, f32[8,256]{1,0:T(8,128)}) custom-call(bf16[4,256,1024]{2,1,0:T(8,128)(2,1)} %copy-done, bf16[1024,4096]{1,0:T(8,128)(2,1)} %w_ref.3, bf16[256,1024]{1,0:T(8,128)(2,1)} %hid_ref.7), custom_call_target="tpu_custom_call" | custom-call | tf_op jit(solution)/shard_map/probe/pallas_call | solution.py:110
  161.0 2.9 %collective-permute-done.17.g2 = bf16[640,256]{1,0:T(8,128)(2,1)S(1)} collective-permute-done((bf16[640,256]{1,0:T(8,128)(2,1)S(1)}, bf16[640,256]{1,0:T(8,128)(2,1)S(1)}, u32[]{:S(2)}, u32[]{:S(2)}) %collective-permute-start.17) | collective-permute-done | bytes 327712 | tf_op jit(solution)/shard_map/ppermute | solution.py:295
  163.9 0.0 all-gather.2.cloned.1.call-done.up_ref
  164.0 0.7 copy-done.3
  164.7 0.1 copy-done.4
  164.8 12.6 %logits.1.l0 = f32[40,256]{1,0:T(8,128)} custom-call(s32[4]{0:T(128)} %pad_add_fusion.pos_ref, s32[32]{0:T(128)} %slice_reduce_fusion.off_ref, bf16[640,256]{1,0:T(8,128)(2,1)} %copy-done.1, bf16[640,256]{1,0:T(8,128)(2,1)} %copy-done.2, bf16[640,256]{1,0:T(8,128)(2,1)} %copy-done.3, bf16[640,256]{1,0:T(8,128)(2,1)} %copy-done.4, ...), custom_call_target="tpu_custom_call" | custom-call | tf_op jit(solution)/shard_map/logits/pallas_call | solution.py:228
  177.3 1.6 collective-permute-start.19
  178.9 1.9 collective-permute-start.20
  180.9 1.8 collective-permute-start.21
  182.6 0.5 collective-permute-done.19.l1
  183.1 1.5 collective-permute-done.20.l2
  184.6 0.4 collective-permute-done.21.l3
  185.1 0.2 copy-done.12
  185.3 0.6 copy-done.13
  185.9 12.9 %join.1 = bf16[256,1024]{1,0:T(8,128)(2,1)} custom-call(s32[4]{0:T(128)} %pad_add_fusion.pos_ref, s32[32]{0:T(128)} %slice_reduce_fusion.off_ref, bf16[640,256]{1,0:T(8,128)(2,1)} %copy-done.1, bf16[640,256]{1,0:T(8,128)(2,1)} %copy-done.2, bf16[640,256]{1,0:T(8,128)(2,1)} %copy-done.3, bf16[640,256]{1,0:T(8,128)(2,1)} %copy-done.4, f32[40,256]{1,0:T(8,128)} %logits.1.l0, ...), custom_call_target="tpu_custom_call" | custom-call | tf_op jit(solution)/shard_map/join/pallas_call | solution.py:273
  (29 shorter events, 0.1 us)
Async XLA Ops:
  6.5 157.4 %all-gather.2.cloned.1.call-start = ((), (), s32[]{:S(2)}) async-start(), calls=%async_computation.2 | async-start | bytes 17301504 | tf_op jit(solution)/shard_map/all_gather | solution.py:304
  13.9 5.5 %copy-start.9 = (bf16[1,1024,256]{2,1,0:T(8,128)(2,1)S(1)}, bf16[1,1024,256]{2,1,0:T(8,128)(2,1)}, u32[]{:S(2)}) copy-start(bf16[1,1024,256]{2,1,0:T(8,128)(2,1)} %param.8) | copy-start | bytes 1572868
  13.9 45.3 %all-to-all-start = ((bf16[4,256,1024]{2,1,0:T(8,128)(2,1)}), bf16[4,256,1024]{2,1,0:T(8,128)(2,1)S(1)}, u32[]{:S(2)}, u32[]{:S(2)}) async-start(bf16[4,256,1024]{2,1,0:T(8,128)(2,1)} %query_parts.1), calls=%async_computation | async-start | bytes 4194304 | tf_op jit(solution)/shard_map/all_to_all | solution.py:316
  19.4 22.4 %collective-permute-start.4 = (bf16[1024,256]{1,0:T(8,128)(2,1)S(1)}, bf16[1024,256]{1,0:T(8,128)(2,1)}, u32[]{:S(2)}, u32[]{:S(2)}) collective-permute-start(bf16[1024,256]{1,0:T(8,128)(2,1)S(1)} %bitcast.7), channel_id=1, source_target_pairs={{0,32},{32,64},{64,96},{96,0},{1,33},{33,65},{65,97},{97,1},{2,34}... | collective-permute-start | bytes 1572872 | tf_op jit(solution)/shard_map/ppermute | solution.py:295
  21.0 34.1 %collective-permute-start.6 = (bf16[1024,256]{1,0:T(8,128)(2,1)S(1)}, bf16[1024,256]{1,0:T(8,128)(2,1)}, u32[]{:S(2)}, u32[]{:S(2)}) collective-permute-start(bf16[1024,256]{1,0:T(8,128)(2,1)S(1)} %bitcast.8), channel_id=1, source_target_pairs={{0,64},{32,96},{64,0},{96,32},{1,65},{33,97},{65,1},{97,33},{2,66}... | collective-permute-start | bytes 1572872 | tf_op jit(solution)/shard_map/ppermute | solution.py:295
  26.0 32.4 %collective-permute-start = (bf16[288,1024]{1,0:T(8,128)(2,1)}, bf16[288,1024]{1,0:T(8,128)(2,1)S(1)}, u32[]{:S(2)}, u32[]{:S(2)}) collective-permute-start(bf16[288,1024]{1,0:T(8,128)(2,1)} %get-tuple-element.19.refs_0_), channel_id=1, source_target_pairs={{0,8},{8,16},{16,24},{24,0},{1,9},{9,17},{17,25},{25,1},{2,10},{10... | collective-permute-start | bytes 1769480 | tf_op jit(solution)/shard_map/ppermute | solution.py:295
  27.5 30.4 %collective-permute-start.8 = (bf16[1024,256]{1,0:T(8,128)(2,1)S(1)}, bf16[1024,256]{1,0:T(8,128)(2,1)}, u32[]{:S(2)}, u32[]{:S(2)}) collective-permute-start(bf16[1024,256]{1,0:T(8,128)(2,1)S(1)} %bitcast.9), channel_id=1, source_target_pairs={{0,96},{32,0},{64,32},{96,64},{1,97},{33,1},{65,33},{97,65},{2,98}... | collective-permute-start | bytes 1572872 | tf_op jit(solution)/shard_map/ppermute | solution.py:295
  28.8 29.1 %collective-permute-start.3 = (bf16[1024,256]{1,0:T(8,128)(2,1)S(1)}, bf16[1024,256]{1,0:T(8,128)(2,1)S(1)}, u32[]{:S(2)}, u32[]{:S(2)}) collective-permute-start(bf16[1024,256]{1,0:T(8,128)(2,1)S(1)} %bitcast.10), channel_id=1, source_target_pairs={{0,4},{4,0},{1,5},{5,1},{2,6},{6,2},{3,7},{7,3},{8,12},{12,8},{9,1... | collective-permute-start | bytes 1572872 | tf_op jit(solution)/shard_map/ppermute | solution.py:312
  41.8 24.7 %collective-permute-start.1 = (bf16[288,1024]{1,0:T(8,128)(2,1)}, bf16[288,1024]{1,0:T(8,128)(2,1)}, u32[]{:S(2)}, u32[]{:S(2)}) collective-permute-start(bf16[288,1024]{1,0:T(8,128)(2,1)} %get-tuple-element.19.refs_0_), channel_id=1, source_target_pairs={{0,16},{8,24},{16,0},{24,8},{1,17},{9,25},{17,1},{25,9},{2,18},{10... | collective-permute-start | bytes 1769480 | tf_op jit(solution)/shard_map/ppermute | solution.py:295
  55.1 20.4 %collective-permute-start.2 = (bf16[288,1024]{1,0:T(8,128)(2,1)}, bf16[288,1024]{1,0:T(8,128)(2,1)}, u32[]{:S(2)}, u32[]{:S(2)}) collective-permute-start(bf16[288,1024]{1,0:T(8,128)(2,1)} %get-tuple-element.19.refs_0_), channel_id=1, source_target_pairs={{0,24},{8,0},{16,8},{24,16},{1,25},{9,1},{17,9},{25,17},{2,26},{10... | collective-permute-start | bytes 1769480 | tf_op jit(solution)/shard_map/ppermute | solution.py:295
  57.9 17.6 %collective-permute-start.5 = (bf16[1024,256]{1,0:T(8,128)(2,1)}, bf16[1024,256]{1,0:T(8,128)(2,1)}, u32[]{:S(2)}, u32[]{:S(2)}) collective-permute-start(bf16[1024,256]{1,0:T(8,128)(2,1)} %collective-permute-done.4.refs_6_), channel_id=1, source_target_pairs={{0,4},{4,0},{1,5},{5,1},{2,6},{6,2},{3,7},{7,3},{8,12},{12,8},{9,1... | collective-permute-start | bytes 1572872 | tf_op jit(solution)/shard_map/ppermute | solution.py:312
  57.9 0.8 copy-start.10
  57.9 17.6 %collective-permute-start.7 = (bf16[1024,256]{1,0:T(8,128)(2,1)}, bf16[1024,256]{1,0:T(8,128)(2,1)}, u32[]{:S(2)}, u32[]{:S(2)}) collective-permute-start(bf16[1024,256]{1,0:T(8,128)(2,1)} %collective-permute-done.6.refs_8_), channel_id=1, source_target_pairs={{0,4},{4,0},{1,5},{5,1},{2,6},{6,2},{3,7},{7,3},{8,12},{12,8},{9,1... | collective-permute-start | bytes 1572872 | tf_op jit(solution)/shard_map/ppermute | solution.py:312
  58.7 2.6 %copy-start.5 = (bf16[288,1024]{1,0:T(8,128)(2,1)}, bf16[288,1024]{1,0:T(8,128)(2,1)S(1)}, u32[]{:S(2)}) copy-start(bf16[288,1024]{1,0:T(8,128)(2,1)S(1)} %collective-permute-done.refs_1_) | copy-start | bytes 1769476
  58.7 16.8 %collective-permute-start.9 = (bf16[1024,256]{1,0:T(8,128)(2,1)}, bf16[1024,256]{1,0:T(8,128)(2,1)}, u32[]{:S(2)}, u32[]{:S(2)}) collective-permute-start(bf16[1024,256]{1,0:T(8,128)(2,1)} %collective-permute-done.8.refs_10_), channel_id=1, source_target_pairs={{0,4},{4,0},{1,5},{5,1},{2,6},{6,2},{3,7},{7,3},{8,12},{12,8},{9,1... | collective-permute-start | bytes 1572872 | tf_op jit(solution)/shard_map/ppermute | solution.py:312
  61.3 91.0 %all-to-all-start.1 = ((bf16[4,256,1024]{2,1,0:T(8,128)(2,1)}), bf16[4,256,1024]{2,1,0:T(8,128)(2,1)S(1)}, u32[]{:S(2)}, u32[]{:S(2)}) async-start(bf16[4,256,1024]{2,1,0:T(8,128)(2,1)} %broadcast_in_dim.2), calls=%async_computation.1 | async-start | bytes 4194304 | tf_op jit(solution)/shard_map/all_to_all | solution.py:318
  66.4 28.7 %copy-start.14 = (s32[32,128]{1,0:T(8,128)S(1)}, s32[32,128]{1,0:T(8,128)}, u32[]{:S(2)}) copy-start(s32[32,128]{1,0:T(8,128)} %get-tuple-element.18) | copy-start | bytes 49156
  90.0 26.6 %collective-permute-start.10 = (bf16[8,128,256]{2,1,0:T(8,128)(2,1)}, bf16[8,128,256]{2,1,0:T(8,128)(2,1)S(1)}, u32[]{:S(2)}, u32[]{:S(2)}) collective-permute-start(bf16[8,128,256]{2,1,0:T(8,128)(2,1)} %get-tuple-element.21), channel_id=1, source_target_pairs={{0,8},{8,16},{16,24},{24,0},{1,9},{9,17},{17,25},{25,1},{2,10},{10... | collective-permute-start | bytes 1572872 | tf_op jit(solution)/shard_map/ppermute | solution.py:295
  90.0 35.6 %collective-permute-start.11 = (bf16[8,128,256]{2,1,0:T(8,128)(2,1)}, bf16[8,128,256]{2,1,0:T(8,128)(2,1)S(1)}, u32[]{:S(2)}, u32[]{:S(2)}) collective-permute-start(bf16[8,128,256]{2,1,0:T(8,128)(2,1)} %get-tuple-element.22), channel_id=1, source_target_pairs={{0,16},{8,24},{16,0},{24,8},{1,17},{9,25},{17,1},{25,9},{2,18},{10... | collective-permute-start | bytes 1572872 | tf_op jit(solution)/shard_map/ppermute | solution.py:295
  95.1 30.5 %collective-permute-start.12 = (bf16[8,128,256]{2,1,0:T(8,128)(2,1)}, bf16[8,128,256]{2,1,0:T(8,128)(2,1)S(1)}, u32[]{:S(2)}, u32[]{:S(2)}) collective-permute-start(bf16[8,128,256]{2,1,0:T(8,128)(2,1)} %get-tuple-element.23), channel_id=1, source_target_pairs={{0,24},{8,0},{16,8},{24,16},{1,25},{9,1},{17,9},{25,17},{2,26},{10... | collective-permute-start | bytes 1572872 | tf_op jit(solution)/shard_map/ppermute | solution.py:295
  116.6 9.0 %copy-start.6 = (bf16[8,128,256]{2,1,0:T(8,128)(2,1)}, bf16[8,128,256]{2,1,0:T(8,128)(2,1)S(1)}, u32[]{:S(2)}) copy-start(bf16[8,128,256]{2,1,0:T(8,128)(2,1)S(1)} %collective-permute-done.10.refs_1_) | copy-start | bytes 1572868
  125.6 0.8 copy-start.7
  125.6 1.0 copy-start.8
  129.6 11.8 %collective-permute-start.13 = (bf16[640,256]{1,0:T(8,128)(2,1)}, bf16[640,256]{1,0:T(8,128)(2,1)S(1)}, u32[]{:S(2)}, u32[]{:S(2)}) collective-permute-start(bf16[640,256]{1,0:T(8,128)(2,1)} %get-tuple-element.25), channel_id=1, source_target_pairs={{0,1},{1,2},{2,3},{3,0},{4,5},{5,6},{6,7},{7,4},{8,9},{9,10},{10,1... | collective-permute-start | bytes 983048 | tf_op jit(solution)/shard_map/ppermute | solution.py:295
  131.1 14.7 %collective-permute-start.14 = (bf16[640,256]{1,0:T(8,128)(2,1)}, bf16[640,256]{1,0:T(8,128)(2,1)S(1)}, u32[]{:S(2)}, u32[]{:S(2)}) collective-permute-start(bf16[640,256]{1,0:T(8,128)(2,1)} %get-tuple-element.26), channel_id=1, source_target_pairs={{0,2},{1,3},{2,0},{3,1},{4,6},{5,7},{6,4},{7,5},{8,10},{9,11},{10,... | collective-permute-start | bytes 983048 | tf_op jit(solution)/shard_map/ppermute | solution.py:295
  134.0 11.9 %collective-permute-start.15 = (bf16[640,256]{1,0:T(8,128)(2,1)}, bf16[640,256]{1,0:T(8,128)(2,1)S(1)}, u32[]{:S(2)}, u32[]{:S(2)}) collective-permute-start(bf16[640,256]{1,0:T(8,128)(2,1)} %get-tuple-element.27), channel_id=1, source_target_pairs={{0,3},{1,0},{2,1},{3,2},{4,7},{5,4},{6,5},{7,6},{8,11},{9,8},{10,9... | collective-permute-start | bytes 983048 | tf_op jit(solution)/shard_map/ppermute | solution.py:295
  147.0 17.0 %copy-start.1 = (bf16[640,256]{1,0:T(8,128)(2,1)}, bf16[640,256]{1,0:T(8,128)(2,1)S(1)}, u32[]{:S(2)}) copy-start(bf16[640,256]{1,0:T(8,128)(2,1)S(1)} %maximum_convert_fusion.g0) | copy-start | bytes 983044
  147.0 14.0 %collective-permute-start.16 = (bf16[640,256]{1,0:T(8,128)(2,1)S(1)}, bf16[640,256]{1,0:T(8,128)(2,1)S(1)}, u32[]{:S(2)}, u32[]{:S(2)}) collective-permute-start(bf16[640,256]{1,0:T(8,128)(2,1)S(1)} %maximum_convert_fusion.g0), channel_id=1, source_target_pairs={{0,1},{1,2},{2,3},{3,0},{4,5},{5,6},{6,7},{7,4},{8,9},{9,10},{10,1... | collective-permute-start | bytes 983048 | tf_op jit(solution)/shard_map/ppermute | solution.py:295
  148.5 15.4 %collective-permute-start.17 = (bf16[640,256]{1,0:T(8,128)(2,1)S(1)}, bf16[640,256]{1,0:T(8,128)(2,1)S(1)}, u32[]{:S(2)}, u32[]{:S(2)}) collective-permute-start(bf16[640,256]{1,0:T(8,128)(2,1)S(1)} %maximum_convert_fusion.g0), channel_id=1, source_target_pairs={{0,2},{1,3},{2,0},{3,1},{4,6},{5,7},{6,4},{7,5},{8,10},{9,11},{10,... | collective-permute-start | bytes 983048 | tf_op jit(solution)/shard_map/ppermute | solution.py:295
  150.9 13.1 %collective-permute-start.18 = (bf16[640,256]{1,0:T(8,128)(2,1)S(1)}, bf16[640,256]{1,0:T(8,128)(2,1)S(1)}, u32[]{:S(2)}, u32[]{:S(2)}) collective-permute-start(bf16[640,256]{1,0:T(8,128)(2,1)S(1)} %maximum_convert_fusion.g0), channel_id=1, source_target_pairs={{0,3},{1,0},{2,1},{3,2},{4,7},{5,4},{6,5},{7,6},{8,11},{9,8},{10,9... | collective-permute-start | bytes 983048 | tf_op jit(solution)/shard_map/ppermute | solution.py:295
  152.3 1.4 copy-start
  161.0 2.9 %copy-start.2 = (bf16[640,256]{1,0:T(8,128)(2,1)}, bf16[640,256]{1,0:T(8,128)(2,1)S(1)}, u32[]{:S(2)}) copy-start(bf16[640,256]{1,0:T(8,128)(2,1)S(1)} %collective-permute-done.16.g1) | copy-start | bytes 983044
  163.9 0.7 copy-start.3
  163.9 0.8 copy-start.4
  177.3 5.8 %collective-permute-start.19 = (f32[40,256]{1,0:T(8,128)}, f32[40,256]{1,0:T(8,128)S(1)}, u32[]{:S(2)}, u32[]{:S(2)}) collective-permute-start(f32[40,256]{1,0:T(8,128)} %logits.1.l0), channel_id=1, source_target_pairs={{0,1},{1,2},{2,3},{3,0},{4,5},{5,6},{6,7},{7,4},{8,9},{9,10},{10,1... | collective-permute-start | bytes 122888 | tf_op jit(solution)/shard_map/ppermute | solution.py:295
  178.9 5.7 %collective-permute-start.20 = (f32[40,256]{1,0:T(8,128)}, f32[40,256]{1,0:T(8,128)S(1)}, u32[]{:S(2)}, u32[]{:S(2)}) collective-permute-start(f32[40,256]{1,0:T(8,128)} %logits.1.l0), channel_id=1, source_target_pairs={{0,2},{1,3},{2,0},{3,1},{4,6},{5,7},{6,4},{7,5},{8,10},{9,11},{10,... | collective-permute-start | bytes 122888 | tf_op jit(solution)/shard_map/ppermute | solution.py:295
  180.9 4.2 %collective-permute-start.21 = (f32[40,256]{1,0:T(8,128)}, f32[40,256]{1,0:T(8,128)S(1)}, u32[]{:S(2)}, u32[]{:S(2)}) collective-permute-start(f32[40,256]{1,0:T(8,128)} %logits.1.l0), channel_id=1, source_target_pairs={{0,3},{1,0},{2,1},{3,2},{4,7},{5,4},{6,5},{7,6},{8,11},{9,8},{10,9... | collective-permute-start | bytes 122888 | tf_op jit(solution)/shard_map/ppermute | solution.py:295
  183.1 1.9 copy-start.11
  184.6 0.6 copy-start.12
  185.3 0.6 copy-start.13
Sparse Core Ops, SparseCore 0:
  9.6 116.0 all-gather.1

commit v2 on v1

v2 whole, which is shorter than its diff:
```python
import jax
import jax.numpy as jnp
from jax import lax
from jax.experimental import pallas as pl
from jax.experimental.pallas import tpu as pltpu
from jax.sharding import Mesh, PartitionSpec as P

D = 4096
ADAPTERS = 32
B = 256
CAP = 128
ROWS = 256
WIDTH = 1024
TILE = 16
PAIRS = 2560
PIECE = PAIRS // 4
BUF = PAIRS + CAP
BF16 = jnp.bfloat16
F32 = jnp.float32
VMEM = 56 * 1024 * 1024


def params(**kw):
    return pltpu.CompilerParams(vmem_limit_bytes=VMEM, **kw)


def dot(a, b, ca, cb):
    return lax.dot_general(a, b, (((ca,), (cb,)), ((), ())), preferred_element_type=F32)


def iota(shape, dim):
    return lax.broadcasted_iota(jnp.int32, shape, dim)


def whole():
    return pl.BlockSpec(memory_space=pltpu.VMEM)


def smem():
    return pl.BlockSpec(memory_space=pltpu.SMEM)


def anywhere():
    return pl.BlockSpec(memory_space=pl.ANY)


def plan_kernel(sub_ref, hid_ref, ext_ref, rank_ref, off_ref):
    ids = iota((ADAPTERS, ROWS), 0)
    chosen = jnp.zeros((ADAPTERS, ROWS), F32)
    for k in range(sub_ref.shape[0]):
        chosen = chosen + jnp.where(sub_ref[k : k + 1, :] == ids, 1.0, 0.0)
    named = chosen.astype(BF16)
    earlier = jnp.where(iota((ROWS, ROWS), 0) < iota((ROWS, ROWS), 1), 1.0, 0.0)
    before = dot(named, earlier.astype(BF16), 1, 0)
    rank = jnp.where(chosen > 0.5, before, -1.0)
    rank_ref[...] = rank
    ext_ref[0:ROWS, :] = hid_ref[...]
    ext_ref[ROWS:, 0:ROWS] = rank.astype(BF16)
    ext_ref[ROWS:, ROWS:] = jnp.zeros((ADAPTERS, WIDTH - ROWS), BF16)
    count = jnp.sum(chosen, axis=1, keepdims=True)
    padded = jnp.broadcast_to(jnp.floor((count + (TILE - 1)) * (1.0 / TILE)) * TILE, (ADAPTERS, 128))
    lower = jnp.where(iota((ADAPTERS, ADAPTERS), 1) < iota((ADAPTERS, ADAPTERS), 0), 1.0, 0.0)
    off_ref[...] = dot(lower.astype(BF16), padded.astype(BF16), 1, 0).astype(jnp.int32)


def plan(subsets, hidden):
    return pl.pallas_call(
        plan_kernel,
        out_shape=(
            jax.ShapeDtypeStruct((ROWS + ADAPTERS, WIDTH), BF16),
            jax.ShapeDtypeStruct((ADAPTERS, ROWS), F32),
            jax.ShapeDtypeStruct((ADAPTERS, 128), jnp.int32),
        ),
        in_specs=[whole(), whole()],
        out_specs=(whole(), whole(), whole()),
        compiler_params=params(),
        name="plan",
    )(subsets.T, hidden)


def spread_kernel(rank_ref, pick_ref):
    rest = jnp.full((CAP - ADAPTERS, ROWS), -1.0, F32)
    cols = jnp.concatenate([rank_ref[...], rest], axis=0).T.astype(BF16)
    slots = iota((ROWS, CAP), 1).astype(F32)
    for a in range(ADAPTERS):
        one = jnp.where(iota((CAP, CAP), 0) == a, 1.0, 0.0).astype(BF16)
        pick_ref[:, a * CAP : (a + 1) * CAP] = jnp.where(dot(cols, one, 1, 0) == slots, 1.0, 0.0).astype(BF16)


def spread(rank):
    return pl.pallas_call(
        spread_kernel,
        out_shape=jax.ShapeDtypeStruct((ROWS, ADAPTERS * CAP), BF16),
        in_specs=[whole()],
        out_specs=whole(),
        compiler_params=params(),
        name="spread",
    )(rank)


def block_copies(pos_ref, weight_ref, held, sems, sign):
    copies = []
    for s in range(4):
        p = (pos_ref[3] + (s if sign > 0 else 4 - s)) & 3
        cols = pl.ds(pl.multiple_of(p * WIDTH, WIDTH), WIDTH)
        copies.append(pltpu.make_async_copy(weight_ref.at[:, cols], held.at[s], sems.at[s]))
    for s in (2, 1, 3, 0):
        copies[s].start()
    return copies


def query_kernel(pos_ref, ext_ref, weight_ref, *refs):
    outs, held, sems = refs[:4], refs[4], refs[5]
    copies = block_copies(pos_ref, weight_ref, held, sems, 1)
    for s in (2, 1, 3, 0):
        copies[s].wait()
        outs[s][...] = dot(ext_ref[0:ROWS, :], held[s], 1, 0).astype(BF16)


def query_parts(pos, ext, weight):
    return pl.pallas_call(
        query_kernel,
        out_shape=[jax.ShapeDtypeStruct((ROWS, WIDTH), BF16)] * 4,
        in_specs=[smem(), whole(), anywhere()],
        out_specs=[whole()] * 4,
        scratch_shapes=[pltpu.VMEM((4, WIDTH, WIDTH), BF16), pltpu.SemaphoreType.DMA((4,))],
        compiler_params=params(),
        name="query_parts",
    )(pos, ext, weight)


def probe_kernel(pos_ref, q0, q1, q2, q3, hid_ref, weight_ref, probe_ref, own_ref, held, sems):
    copies = block_copies(pos_ref, weight_ref, held, sems, -1)
    total = jnp.zeros((ROWS, WIDTH), F32)
    for s, q in ((2, q2), (1, q1), (3, q3), (0, q0)):
        copies[s].wait()
        total = total + dot(q[...], held[s], 1, 1)
    probe = total.astype(BF16)
    probe_ref[...] = probe
    own = jnp.sum(probe.astype(F32) * hid_ref[...].astype(F32), axis=1, keepdims=True)
    own_ref[...] = jnp.broadcast_to(own, (ROWS, 128)).T[0:8, :]


def probe_of(pos, query, weight, hidden):
    return pl.pallas_call(
        probe_kernel,
        out_shape=(
            jax.ShapeDtypeStruct((ROWS, WIDTH), BF16),
            jax.ShapeDtypeStruct((8, ROWS), F32),
        ),
        in_specs=[smem()] + [whole()] * 5 + [anywhere()],
        out_specs=(whole(), whole()),
        scratch_shapes=[pltpu.VMEM((4, WIDTH, WIDTH), BF16), pltpu.SemaphoreType.DMA((4,))],
        compiler_params=params(),
        name="probe",
    )(pos, *query, hidden, weight)


def adapter_of(pos_ref, sx, i):
    return (i // 2 * 4 + ((pos_ref[1] + (4 - sx)) & 3)) * 2 + i % 2


def squeeze_kernel(pos_ref, *refs):
    exts, weights, outs = refs[:4], refs[4], refs[5:9]
    rows, ranks, held, row_sems, rank_sems, sems = refs[9:]
    row_copies, rank_copies = [], []
    for s in range(4):
        some = pl.ds(s * ROWS, ROWS)
        row_copies.append(pltpu.make_async_copy(exts[s].at[pl.ds(0, ROWS)], rows.at[some], row_sems.at[s]))
        rest = exts[s].at[pl.ds(ROWS, ADAPTERS), pl.ds(0, ROWS)]
        rank_copies.append(pltpu.make_async_copy(rest, ranks.at[s], rank_sems.at[s]))
    copies = [
        pltpu.make_async_copy(weights.at[i], held.at[:, pl.ds(i * B, B)], sems.at[i]) for i in range(8)
    ]
    for copy in row_copies + copies[:4] + rank_copies + copies[4:]:
        copy.start()
    ids = iota((ADAPTERS, ROWS), 0)
    slots = iota((CAP, ROWS), 0).astype(F32)
    for copy in row_copies:
        copy.wait()
    for j in range(2):
        for i in range(4 * j, 4 * j + 4):
            copies[i].wait()
        part = dot(rows[...], held[:, 4 * j * B : 4 * (j + 1) * B], 1, 0).astype(BF16)
        if j == 0:
            for copy in rank_copies:
                copy.wait()
        for i in range(4 * j, 4 * j + 4):
            a = adapter_of(pos_ref, 0, i)
            cols = slice((i - 4 * j) * B, (i - 4 * j + 1) * B)
            for s in range(4):
                mine = jnp.sum(jnp.where(ids == a, ranks[s].astype(F32), 0.0), axis=0, keepdims=True)
                pick = jnp.where(slots == mine, 1.0, 0.0).astype(BF16)
                outs[s][i] = dot(pick, part[s * ROWS : (s + 1) * ROWS, cols], 1, 0).astype(BF16)


def squeeze(pos, exts, weights):
    return pl.pallas_call(
        squeeze_kernel,
        out_shape=[jax.ShapeDtypeStruct((8, CAP, B), BF16)] * 4,
        in_specs=[smem()] + [anywhere()] * 5,
        out_specs=[whole()] * 4,
        scratch_shapes=[
            pltpu.VMEM((4 * ROWS, WIDTH), BF16),
            pltpu.VMEM((4, ADAPTERS, ROWS), BF16),
            pltpu.VMEM((WIDTH, 8 * B), BF16),
            pltpu.SemaphoreType.DMA((4,)),
            pltpu.SemaphoreType.DMA((4,)),
            pltpu.SemaphoreType.DMA((8,)),
        ],
        compiler_params=params(),
        name="squeeze",
    )(pos, *exts, weights)


def pack_kernel(pos_ref, off_ref, *refs):
    blocks, outs, buf = refs[:4], refs[4:8], refs[8]
    buf[...] = jnp.zeros_like(buf)
    for t in range(4):
        for i in range(8):
            a = adapter_of(pos_ref, t, i)
            at = pl.ds(pl.multiple_of(off_ref[a], TILE), CAP)
            buf[at, :] = buf[at, :] + blocks[t][i]
    for s in range(4):
        p = (pos_ref[3] + s) & 3
        outs[s][...] = buf[pl.ds(pl.multiple_of(p * PIECE, TILE), PIECE), :]


def pack(pos, off, blocks):
    return pl.pallas_call(
        pack_kernel,
        out_shape=[jax.ShapeDtypeStruct((PIECE, B), BF16)] * 4,
        in_specs=[pl.BlockSpec(memory_space=pltpu.SMEM)] * 2 + [whole()] * 4,
        out_specs=[whole()] * 4,
        scratch_shapes=[pltpu.VMEM((BUF, B), BF16)],
        compiler_params=params(),
        name="pack",
    )(pos, off, *blocks)


def unpack_into(buf, pos_ref, pieces):
    for s in range(4):
        p = (pos_ref[3] + (4 - s)) & 3
        buf[pl.ds(pl.multiple_of(p * PIECE, TILE), PIECE), :] = pieces[s][...]
    buf[PAIRS:, :] = jnp.zeros((CAP, B), BF16)


PER = 4
STEPS = ADAPTERS // PER
ORDER = list(range(ADAPTERS))


def step_copies(up_ref, held, bottle_ref, bottles, sems):
    copies = []
    for g in range(STEPS):
        some = pl.ds(g * PER, PER)
        cols = pl.ds(g * PER * B, PER * B)
        copies.append(
            (
                pltpu.make_async_copy(bottle_ref.at[:, cols], bottles.at[:, cols], sems.at[0, g]),
                pltpu.make_async_copy(up_ref.at[some], held.at[some], sems.at[1, g]),
            )
        )
        for copy in copies[g]:
            copy.start()

    def arrive(g):
        for copy in copies[g]:
            copy.wait()

    return arrive


def segment(buf, off_ref, a):
    return buf[pl.ds(pl.multiple_of(off_ref[a], TILE), CAP), :]


def expand_kernel(pos_ref, off_ref, g0, g1, g2, g3, pick_ref, out_ref, buf):
    unpack_into(buf, pos_ref, (g0, g1, g2, g3))
    for i, a in enumerate(ORDER):
        pick = pick_ref[:, a * CAP : (a + 1) * CAP]
        out_ref[:, i * B : (i + 1) * B] = dot(pick, segment(buf, off_ref, a), 1, 0).astype(BF16)


def expand(pos, off, pieces, pick):
    return pl.pallas_call(
        expand_kernel,
        out_shape=jax.ShapeDtypeStruct((ROWS, ADAPTERS * B), BF16),
        in_specs=[smem(), smem()] + [whole()] * 5,
        out_specs=whole(),
        scratch_shapes=[pltpu.VMEM((BUF, B), BF16)],
        compiler_params=params(),
        name="expand",
    )(pos, off, *pieces, pick)


def logits_kernel(bottle_ref, probe_ref, own_ref, up_ref, out_ref, held, bottles, sems):
    arrive = step_copies(up_ref, held, bottle_ref, bottles, sems)
    out_ref[ADAPTERS:, :] = own_ref[...]
    lane = iota((ROWS, 128), 1)
    found = jnp.zeros((ROWS, 128), F32)
    for g in range(STEPS):
        arrive(g)
        turned = dot(probe_ref[...], held[g * PER : (g + 1) * PER].reshape(PER * B, WIDTH), 1, 1)
        product = turned * bottles[:, g * PER * B : (g + 1) * PER * B].astype(F32)
        for k in range(PER):
            logit = jnp.sum(product[:, k * B : (k + 1) * B], axis=1, keepdims=True)
            found = jnp.where(lane == ORDER[g * PER + k], logit, found)
    out_ref[0:ADAPTERS, :] = found.T[0:ADAPTERS, :]


def logits_of(bottle, probe, own, up):
    return pl.pallas_call(
        logits_kernel,
        out_shape=jax.ShapeDtypeStruct((ADAPTERS + 8, ROWS), F32),
        in_specs=[anywhere()] + [whole()] * 2 + [anywhere()],
        out_specs=whole(),
        scratch_shapes=[
            pltpu.VMEM((ADAPTERS, B, WIDTH), BF16),
            pltpu.VMEM((ROWS, ADAPTERS * B), BF16),
            pltpu.SemaphoreType.DMA((2, STEPS)),
        ],
        compiler_params=params(),
        name="logits",
    )(bottle, probe, own, up)


def join_kernel(bottle_ref, l0, l1, l2, l3, rank_ref, hid_ref, up_ref, out_ref, held, bottles, sems):
    arrive = step_copies(up_ref, held, bottle_ref, bottles, sems)
    total = (l0[...] + l1[...]) + (l2[...] + l3[...])
    logits = (total[0:ADAPTERS] + total[ADAPTERS : ADAPTERS + 1]) * D ** (-0.5)
    chosen = rank_ref[...] >= 0.0
    logits = jnp.where(chosen, logits, -jnp.inf)
    e = jnp.where(chosen, jnp.exp(logits - jnp.max(logits, axis=0, keepdims=True)), 0.0)
    share = e / jnp.sum(e, axis=0, keepdims=True)
    share = jnp.concatenate([share, jnp.zeros((128 - ADAPTERS, ROWS), F32)], axis=0).T
    total = hid_ref[...].astype(F32)
    for g in range(STEPS):
        mix = []
        arrive(g)
        for i in range(g * PER, (g + 1) * PER):
            a = ORDER[i]
            bottle = bottles[:, i * B : (i + 1) * B].astype(F32)
            mix.append((bottle * share[:, a : a + 1]).astype(BF16))
        up = held[g * PER : (g + 1) * PER].reshape(PER * B, WIDTH)
        total = total + dot(jnp.concatenate(mix, axis=1), up, 1, 0)
    out_ref[...] = total.astype(BF16)


def join(bottle, parts, rank, hidden, up):
    return pl.pallas_call(
        join_kernel,
        out_shape=jax.ShapeDtypeStruct((ROWS, WIDTH), BF16),
        in_specs=[anywhere()] + [whole()] * 6 + [anywhere()],
        out_specs=whole(),
        scratch_shapes=[
            pltpu.VMEM((ADAPTERS, B, WIDTH), BF16),
            pltpu.VMEM((ROWS, ADAPTERS * B), BF16),
            pltpu.SemaphoreType.DMA((2, STEPS)),
        ],
        compiler_params=params(),
        name="join",
    )(bottle, *parts, rank, hidden, up)


def shifted(x, axis, s):
    return lax.ppermute(x, axis, [(i, (i + s) % 4) for i in range(4)])


def round_trip(x, axis):
    return [x] + [shifted(x, axis, s) for s in (1, 2, 3)]


def gathered(xs, axis):
    return [xs[0]] + [shifted(xs[s], axis, s) for s in (1, 2, 3)]


def summed(xs):
    xs = [x.astype(F32) for x in xs]
    return (xs[0] + xs[1]) + (xs[2] + xs[3])


def per_device(hidden, subsets, down_weight, up_weight, query_weight, key_weight):
    pos = jnp.stack([lax.axis_index(n) for n in ("y", "x", "core", "mp")]).astype(jnp.int32)
    ext, rank, off = plan(subsets, hidden)
    pick = spread(rank)
    off = off[:, 0]

    parts = query_parts(pos, ext, query_weight)
    downs = lax.all_gather(down_weight, ("y", "core"), axis=0, tiled=True)
    exts = round_trip(ext, "x")
    near = [parts[0]] + [shifted(parts[s], "mp", s) for s in (1, 3)]
    phase = (exts, downs, near, parts[2], pick, up_weight)
    exts, downs, near, far, pick, up_weight = lax.optimization_barrier(phase)
    parts = near + [shifted(far, "mp", 2)]

    up = lax.all_gather(up_weight, ("y", "x", "core"), axis=0, tiled=True)
    made = squeeze(pos, exts, downs)
    back = gathered([made[0], made[3], made[2], made[1]], "x")
    query = summed(parts).astype(BF16)
    query = round_trip(query, "mp")

    sent = pack(pos, off, back)
    probe, own = probe_of(pos, query, key_weight, hidden)
    got = gathered(sent, "mp")
    got, probe = lax.optimization_barrier((got, probe))
    pieces = round_trip(jnp.maximum(summed(got), 0.0).astype(BF16), "mp")

    bottle = expand(pos, off, pieces, pick)
    partial = logits_of(bottle, probe, own, up)
    partials = round_trip(partial, "mp")
    return join(bottle, partials, rank, hidden, up)


def solution(mesh):
    split = Mesh(mesh.devices.reshape(4, 4, 2, 4), ("y", "x", "core", "mp"))
    rows = ("y", "x", "core")
    return jax.shard_map(
        per_device,
        mesh=split,
        in_specs=(
            P(rows, "mp"),
            P(rows, None),
            P(rows, "mp", None),
            P(rows, None, "mp"),
            P("mp", None),
            P("mp", None),
        ),
        out_specs=P(rows, "mp"),
        check_vma=False,
    )
```

time: 209 us -> 175 us (0.84); the launches traced: 206 us -> 175 us
  waiting for transfers between devices: 78.8 us -> 61.1 us
  starting transfers between devices: 45.6 us -> 36.4 us
    ppermute x18 -> x21, waiting for transfers between devices: 78.1 us -> 56.3 us  [shifted(): return lax.ppermute(x, axis, [(i, (i + s) % 4) for i in range(4)])]
    all_to_all x2 -> x0, starting transfers between devices: 10 us -> none  [the longest x1 5.52 us: per_device(): parts = lax.all_to_all(parts, 'mp', 0, 0, tiled=True)]
    pallas_call x1 -> x3, Pallas kernels: 6.63 us -> 14.7 us  [the longest x1 6.36 us: query_parts(): pl.pallas_call(query_kernel, out_shape=[jax.ShapeDtypeStruct((ROWS, WIDTH...]
    pallas_call x1, Pallas kernels: 14.4 us -> 10.2 us  [squeeze(): pl.pallas_call(squeeze_kernel, out_shape=[jax.ShapeDtypeStruct((8, CAP, B...]
    all_gather x0 -> x1, waiting for transfers between devices: none -> 4.15 us  [per_device(): downs = lax.all_gather(down_weight, ('y', 'core'), axis=0, tiled=True)]
    pallas_call x1, Pallas kernels: 12.9 us -> 9.94 us  [join(): pl.pallas_call(join_kernel, out_shape=jax.ShapeDtypeStruct((ROWS, WIDTH),...]
    pallas_call x1, Pallas kernels: 12.6 us -> 10.2 us  [logits_of(): pl.pallas_call(logits_kernel, out_shape=jax.ShapeDtypeStruct((ADAPTERS +...]
    ppermute x18 -> x21, starting transfers between devices: 34.6 us -> 36.4 us  [shifted(): return lax.ppermute(x, axis, [(i, (i + s) % 4) for i in range(4)])]
  transfers between devices with their start and end apart: 25 -> 23, of which waited for: 11 -> 12; matrix products, arithmetic and copies ran while one was open for 2% -> 1% of each run, Pallas kernels for 16% -> 21%
where the time goes in v2:
time: 175 us
  waiting for transfers between devices  61.1 us (35%)
  Pallas kernels  57.4 us (33%)
  starting transfers between devices  36.4 us (21%)
  between operations  13.6 us (8%)
  local copies, waits for them, and re-layouts  4.92 us (3%)
    ppermute x21, waiting for transfers between devices, shifted(): return lax.ppermute(x, axis, [(i, (i + s) % 4) for i in range(4)])  56.3 us
    ppermute x21, starting transfers between devices, shifted(): return lax.ppermute(x, axis, [(i, (i + s) % 4) for i in range(4)])  36.4 us
    pallas_call x1, Pallas kernels, logits_of(): pl.pallas_call(logits_kernel, out_shape=jax.ShapeDtypeStruct((ADAPTERS +...  10.2 us
    pallas_call x1, Pallas kernels, squeeze(): pl.pallas_call(squeeze_kernel, out_shape=[jax.ShapeDtypeStruct((8, CAP, B...  10.2 us
    pallas_call x1, Pallas kernels, join(): pl.pallas_call(join_kernel, out_shape=jax.ShapeDtypeStruct((ROWS, WIDTH),...  9.94 us
    pallas_call x1, Pallas kernels, probe_of(): pl.pallas_call(probe_kernel, out_shape=(jax.ShapeDtypeStruct((ROWS, WIDTH...  7.33 us
    pallas_call x1, Pallas kernels, query_parts(): pl.pallas_call(query_kernel, out_shape=[jax.ShapeDtypeStruct((ROWS, WIDTH...  6.36 us
    pallas_call x1, Pallas kernels, expand(): pl.pallas_call(expand_kernel, out_shape=jax.ShapeDtypeStruct((ROWS, ADAPT...  5.5 us
  transfers between devices with their start and end apart: 23, of which 12 were waited for; matrix products, arithmetic and copies ran while one was open for 1% of the time, Pallas kernels for 21%

profile of v2, /device:TPU:0, one launch (start us, length us, event | category | flops | bytes accessed | tf_op | source)
XLA Modules:
  0.0 174.6 jit_solution(13210480494128019961)
XLA Ops:
  6.5 0.7 all-gather.3.cloned.1.call-update
  7.3 0.0 all-gather.5.cloned.1.call-start
  7.3 2.1 %plan.1 = (bf16[288,1024]{1,0:T(8,128)(2,1)}, f32[32,256]{1,0:T(8,128)}, s32[32,128]{1,0:T(8,128)}) custom-call(s32[8,256]{1,0:T(8,128)} %bitcast.5, bf16[256,1024]{1,0:T(8,128)(2,1)} %hid_ref.5), custom_call_target="tpu_custom_call" | custom-call | tf_op jit(solution)/shard_map/plan/pallas_call | solution.py:67
  9.4 1.6 collective-permute-start
  10.9 2.7 %collective-permute-start.1 = (bf16[288,1024]{1,0:T(8,128)(2,1)}, bf16[288,1024]{1,0:T(8,128)(2,1)S(1)}, u32[]{:S(2)}, u32[]{:S(2)}) collective-permute-start(bf16[288,1024]{1,0:T(8,128)(2,1)} %get-tuple-element.45.ext_ref.refs_0_), channel_id=1, source_target_pairs={{0,16},{8,24},{16,0},{24,8},{1,17},{9,25},{17,1},{25,9},{2,18},{10... | collective-permute-start | bytes 1769480 | tf_op jit(solution)/shard_map/ppermute | solution.py:367
  13.7 1.4 collective-permute-start.2
  15.1 0.6 pad_add_fusion.pos_ref
  15.7 6.4 %query_parts.1 = (bf16[256,1024]{1,0:T(8,128)(2,1)}, bf16[256,1024]{1,0:T(8,128)(2,1)}, bf16[256,1024]{1,0:T(8,128)(2,1)}, bf16[256,1024]{1,0:T(8,128)(2,1)}) custom-call(s32[4]{0:T(128)} %pad_add_fusion.pos_ref, bf16[288,1024]{1,0:T(8,128)(2,1)} %get-tuple-element.45.ext_ref.refs_0_, bf16[1024,4096]{1,0:T(8,128)(2,1)} %weight_ref.2), custom_call_target="tpu_custom_call" | custom-call | tf_op jit(solution)/shard_map/query_parts/pallas_call | solution.py:121
  22.1 2.0 %collective-permute-start.3 = (bf16[256,1024]{1,0:T(8,128)(2,1)}, bf16[256,1024]{1,0:T(8,128)(2,1)S(1)}, u32[]{:S(2)}, u32[]{:S(2)}) collective-permute-start(bf16[256,1024]{1,0:T(8,128)(2,1)} %get-tuple-element.41), channel_id=1, source_target_pairs={{0,1},{1,2},{2,3},{3,0},{4,5},{5,6},{6,7},{7,4},{8,9},{9,10},{10,1... | collective-permute-start | bytes 1572872 | tf_op jit(solution)/shard_map/ppermute | solution.py:367
  24.1 2.2 %collective-permute-start.4 = (bf16[256,1024]{1,0:T(8,128)(2,1)}, bf16[256,1024]{1,0:T(8,128)(2,1)S(1)}, u32[]{:S(2)}, u32[]{:S(2)}) collective-permute-start(bf16[256,1024]{1,0:T(8,128)(2,1)} %get-tuple-element.42), channel_id=1, source_target_pairs={{0,3},{1,0},{2,1},{3,2},{4,7},{5,4},{6,5},{7,6},{8,11},{9,8},{10,9... | collective-permute-start | bytes 1572872 | tf_op jit(solution)/shard_map/ppermute | solution.py:367
  26.3 2.9 %spread.1.pick_ref = bf16[256,4096]{1,0:T(8,128)(2,1)} custom-call(f32[32,256]{1,0:T(8,128)} %get-tuple-element.44.rank_ref), custom_call_target="tpu_custom_call" | custom-call | tf_op jit(solution)/shard_map/spread/pallas_call | solution.py:91
  29.1 8.3 %collective-permute-done.3 = bf16[256,1024]{1,0:T(8,128)(2,1)S(1)} collective-permute-done((bf16[256,1024]{1,0:T(8,128)(2,1)}, bf16[256,1024]{1,0:T(8,128)(2,1)S(1)}, u32[]{:S(2)}, u32[]{:S(2)}) %collective-permute-start.3) | collective-permute-done | bytes 524320 | tf_op jit(solution)/shard_map/ppermute | solution.py:367
  37.5 0.0 collective-permute-done.4
  37.5 2.1 %collective-permute-done.1.refs_2_ = bf16[288,1024]{1,0:T(8,128)(2,1)S(1)} collective-permute-done((bf16[288,1024]{1,0:T(8,128)(2,1)}, bf16[288,1024]{1,0:T(8,128)(2,1)S(1)}, u32[]{:S(2)}, u32[]{:S(2)}) %collective-permute-start.1) | collective-permute-done | bytes 589856 | tf_op jit(solution)/shard_map/ppermute | solution.py:367
  39.6 0.0 collective-permute-done.2.refs_3_
  39.6 4.1 %all-gather.3.cloned.1.call-done.refs_4_ = bf16[8,1024,256]{2,1,0:T(8,128)(2,1)} async-done(((bf16[1,1024,256]{2,1,0:T(8,128)(2,1)}), bf16[8,1024,256]{2,1,0:T(8,128)(2,1)}) %all-gather.3.cloned.1.call-update) | async-done | bytes 4194320 | tf_op jit(solution)/shard_map/all_gather | solution.py:390
  43.7 0.0 all-gather.5.cloned.1.call-update
  43.7 3.2 %collective-permute-start.11 = (bf16[256,1024]{1,0:T(8,128)(2,1)}, bf16[256,1024]{1,0:T(8,128)(2,1)S(1)}, u32[]{:S(2)}, u32[]{:S(2)}) collective-permute-start(bf16[256,1024]{1,0:T(8,128)(2,1)} %get-tuple-element.61), channel_id=1, source_target_pairs={{0,2},{1,3},{2,0},{3,1},{4,6},{5,7},{6,4},{7,5},{8,10},{9,11},{10,... | collective-permute-start | bytes 1572872 | tf_op jit(solution)/shard_map/ppermute | solution.py:367
  47.0 10.2 %squeeze.5 = (bf16[8,128,256]{2,1,0:T(8,128)(2,1)}, bf16[8,128,256]{2,1,0:T(8,128)(2,1)}, bf16[8,128,256]{2,1,0:T(8,128)(2,1)}, bf16[8,128,256]{2,1,0:T(8,128)(2,1)}) custom-call(s32[4]{0:T(128)} %pad_add_fusion.pos_ref, bf16[288,1024]{1,0:T(8,128)(2,1)} %get-tuple-element.45.ext_ref.refs_0_, bf16[288,1024]{1,0:T(8,128)(2,1)} %copy-done.2, ...), custom_call_target="tpu_custom_call" | custom-call | tf_op jit(solution)/shard_map/squeeze/pallas_call | solution.py:198
  57.1 1.6 collective-permute-start.5
  58.7 2.7 %collective-permute-start.6 = (bf16[8,128,256]{2,1,0:T(8,128)(2,1)}, bf16[8,128,256]{2,1,0:T(8,128)(2,1)S(1)}, u32[]{:S(2)}, u32[]{:S(2)}) collective-permute-start(bf16[8,128,256]{2,1,0:T(8,128)(2,1)} %get-tuple-element.52), channel_id=1, source_target_pairs={{0,16},{8,24},{16,0},{24,8},{1,17},{9,25},{17,1},{25,9},{2,18},{10... | collective-permute-start | bytes 1572872 | tf_op jit(solution)/shard_map/ppermute | solution.py:367
  61.4 1.5 collective-permute-start.7
  62.8 0.0 collective-permute-done.11
  62.8 0.4 add_convert_fusion.q0
  63.2 0.7 collective-permute-start.12
  63.9 1.9 %collective-permute-start.13 = (bf16[256,1024]{1,0:T(8,128)(2,1)S(1)}, bf16[256,1024]{1,0:T(8,128)(2,1)S(1)}, u32[]{:S(2)}, u32[]{:S(2)}) collective-permute-start(bf16[256,1024]{1,0:T(8,128)(2,1)S(1)} %add_convert_fusion.q0), channel_id=1, source_target_pairs={{0,2},{1,3},{2,0},{3,1},{4,6},{5,7},{6,4},{7,5},{8,10},{9,11},{10,... | collective-permute-start | bytes 1572872 | tf_op jit(solution)/shard_map/ppermute | solution.py:367
  65.8 13.8 %collective-permute-done.5.refs_1_ = bf16[8,128,256]{2,1,0:T(8,128)(2,1)S(1)} collective-permute-done((bf16[8,128,256]{2,1,0:T(8,128)(2,1)}, bf16[8,128,256]{2,1,0:T(8,128)(2,1)S(1)}, u32[]{:S(2)}, u32[]{:S(2)}) %collective-permute-start.5) | collective-permute-done | bytes 524320 | tf_op jit(solution)/shard_map/ppermute | solution.py:367
  79.6 1.6 collective-permute-start.14
  81.2 0.6 slice_reduce_fusion.off_ref
  81.9 9.2 %collective-permute-done.6.refs_2_ = bf16[8,128,256]{2,1,0:T(8,128)(2,1)S(1)} collective-permute-done((bf16[8,128,256]{2,1,0:T(8,128)(2,1)}, bf16[8,128,256]{2,1,0:T(8,128)(2,1)S(1)}, u32[]{:S(2)}, u32[]{:S(2)}) %collective-permute-start.6) | collective-permute-done | bytes 524320 | tf_op jit(solution)/shard_map/ppermute | solution.py:367
  91.1 0.8 copy-done.10
  91.9 0.3 copy-done.11
  92.2 3.0 %pack.1 = (bf16[640,256]{1,0:T(8,128)(2,1)}, bf16[640,256]{1,0:T(8,128)(2,1)}, bf16[640,256]{1,0:T(8,128)(2,1)}, bf16[640,256]{1,0:T(8,128)(2,1)}) custom-call(s32[4]{0:T(128)} %pad_add_fusion.pos_ref, s32[32]{0:T(128)} %slice_reduce_fusion.off_ref, bf16[8,128,256]{2,1,0:T(8,128)(2,1)} %get-tuple-element.50.refs_0_, bf16[8,128,256]{2,1,0:T(8,128)(2,1)} %copy-done.9, ...), custom_call_target="tpu_custom_call" | custom-call | tf_op jit(solution)/shard_map/pack/pallas_call | solution.py:230
  95.2 3.0 %collective-permute-start.10 = (bf16[640,256]{1,0:T(8,128)(2,1)}, bf16[640,256]{1,0:T(8,128)(2,1)S(1)}, u32[]{:S(2)}, u32[]{:S(2)}) collective-permute-start(bf16[640,256]{1,0:T(8,128)(2,1)} %get-tuple-element.57), channel_id=1, source_target_pairs={{0,3},{1,0},{2,1},{3,2},{4,7},{5,4},{6,5},{7,6},{8,11},{9,8},{10,9... | collective-permute-start | bytes 983048 | tf_op jit(solution)/shard_map/ppermute | solution.py:367
  98.2 0.0 collective-permute-start.8
  98.2 0.0 collective-permute-done.12.q1
  98.2 1.7 collective-permute-start.9
  99.9 0.0 collective-permute-done.13.q2
  99.9 0.8 copy-done.7
  100.7 0.8 copy-done.8
  101.5 7.3 %probe.1 = (bf16[256,1024]{1,0:T(8,128)(2,1)}, f32[8,256]{1,0:T(8,128)}) custom-call(s32[4]{0:T(128)} %pad_add_fusion.pos_ref, bf16[256,1024]{1,0:T(8,128)(2,1)} %copy-done, bf16[256,1024]{1,0:T(8,128)(2,1)} %copy-done.6, bf16[256,1024]{1,0:T(8,128)(2,1)} %copy-done.7, bf16[256,1024]{1,0:T(8,128)(2,1)} %copy-done.8, bf16[256,1024]{1,0:T(8,128)(2,1)} %hid_ref.5, ...), custom_call_target="tpu_custom_call" | custom-call | tf_op jit(solution)/shard_map/probe/pallas_call | solution.py:145
  108.8 3.6 %collective-permute-done.10 = bf16[640,256]{1,0:T(8,128)(2,1)S(1)} collective-permute-done((bf16[640,256]{1,0:T(8,128)(2,1)}, bf16[640,256]{1,0:T(8,128)(2,1)S(1)}, u32[]{:S(2)}, u32[]{:S(2)}) %collective-permute-start.10) | collective-permute-done | bytes 327712 | tf_op jit(solution)/shard_map/ppermute | solution.py:367
  112.5 3.3 %collective-permute-done.8 = bf16[640,256]{1,0:T(8,128)(2,1)S(1)} collective-permute-done((bf16[640,256]{1,0:T(8,128)(2,1)}, bf16[640,256]{1,0:T(8,128)(2,1)S(1)}, u32[]{:S(2)}, u32[]{:S(2)}) %collective-permute-start.8) | collective-permute-done | bytes 327712 | tf_op jit(solution)/shard_map/ppermute | solution.py:367
  115.8 0.0 collective-permute-done.9
  115.8 0.2 maximum_convert_fusion.g0
  116.0 0.0 copy-start.1
  116.0 0.1 collective-permute-start.15
  116.1 1.7 collective-permute-start.16
  117.8 1.5 collective-permute-start.17
  119.3 12.4 %collective-permute-done.15.g1 = bf16[640,256]{1,0:T(8,128)(2,1)S(1)} collective-permute-done((bf16[640,256]{1,0:T(8,128)(2,1)S(1)}, bf16[640,256]{1,0:T(8,128)(2,1)S(1)}, u32[]{:S(2)}, u32[]{:S(2)}) %collective-permute-start.15) | collective-permute-done | bytes 327712 | tf_op jit(solution)/shard_map/ppermute | solution.py:367
  131.7 0.6 collective-permute-done.17.g3
  132.3 0.1 copy-done.12
  132.4 0.1 copy-done.13
  132.5 0.8 copy-done.14
  133.2 5.5 %expand.1.bottle_ref = bf16[256,8192]{1,0:T(8,128)(2,1)} custom-call(s32[4]{0:T(128)} %pad_add_fusion.pos_ref, s32[32]{0:T(128)} %slice_reduce_fusion.off_ref, bf16[640,256]{1,0:T(8,128)(2,1)} %copy-done.1, bf16[640,256]{1,0:T(8,128)(2,1)} %copy-done.12, bf16[640,256]{1,0:T(8,128)(2,1)} %copy-done.13, bf16[640,256]{1,0:T(8,128)(2,1)} %copy-done.14, ...), custom_call_target="tpu_custom_call" | custom-call | tf_op jit(solution)/shard_map/expand/pallas_call | solution.py:286
  138.7 10.2 %logits.1.l0 = f32[40,256]{1,0:T(8,128)} custom-call(bf16[256,8192]{1,0:T(8,128)(2,1)} %expand.1.bottle_ref, bf16[256,1024]{1,0:T(8,128)(2,1)} %get-tuple-element.68.probe_ref, f32[8,256]{1,0:T(8,128)} %get-tuple-element.69.own_ref, bf16[32,256,1024]{2,1,0:T(8,128)(2,1)} %all-gather.5.cloned.1.call-done.up_ref), custom_call_target="tpu_custom_call" | custom-call | tf_op jit(solution)/shard_map/logits/pallas_call | solution.py:313
  149.0 1.2 collective-permute-start.18
  150.1 2.9 %collective-permute-start.19 = (f32[40,256]{1,0:T(8,128)}, f32[40,256]{1,0:T(8,128)S(1)}, u32[]{:S(2)}, u32[]{:S(2)}) collective-permute-start(f32[40,256]{1,0:T(8,128)} %logits.1.l0), channel_id=1, source_target_pairs={{0,2},{1,3},{2,0},{3,1},{4,6},{5,7},{6,4},{7,5},{8,10},{9,11},{10,... | collective-permute-start | bytes 122888 | tf_op jit(solution)/shard_map/ppermute | solution.py:367
  153.0 1.4 collective-permute-start.20
  154.4 0.1 collective-permute-done.18.l1
  154.5 1.4 collective-permute-done.19.l2
  155.8 1.4 collective-permute-done.20.l3
  157.2 0.6 copy-done.18
  157.8 9.9 %join.1 = bf16[256,1024]{1,0:T(8,128)(2,1)} custom-call(bf16[256,8192]{1,0:T(8,128)(2,1)} %expand.1.bottle_ref, f32[40,256]{1,0:T(8,128)} %logits.1.l0, f32[40,256]{1,0:T(8,128)} %copy-done.16, f32[40,256]{1,0:T(8,128)} %copy-done.17, f32[40,256]{1,0:T(8,128)} %copy-done.18, f32[32,256]{1,0:T(8,128)} %get-tuple-element.44.rank_ref, ...), custom_call_target="tpu_custom_call" | custom-call | tf_op jit(solution)/shard_map/join/pallas_call | solution.py:351
  (37 shorter events, 0.1 us)
Async XLA Ops:
  6.5 37.2 %all-gather.3.cloned.1.call-start = ((), (), s32[]{:S(2)}) async-start(), calls=%async_computation | async-start | bytes 4718592 | tf_op jit(solution)/shard_map/all_gather | solution.py:390
  7.3 131.5 %all-gather.5.cloned.1.call-start = ((), (), s32[]{:S(2)}) async-start(), calls=%async_computation.1 | async-start | bytes 17301504 | tf_op jit(solution)/shard_map/all_gather | solution.py:397
  9.4 28.1 %collective-permute-start = (bf16[288,1024]{1,0:T(8,128)(2,1)}, bf16[288,1024]{1,0:T(8,128)(2,1)S(1)}, u32[]{:S(2)}, u32[]{:S(2)}) collective-permute-start(bf16[288,1024]{1,0:T(8,128)(2,1)} %get-tuple-element.45.ext_ref.refs_0_), channel_id=1, source_target_pairs={{0,8},{8,16},{16,24},{24,0},{1,9},{9,17},{17,25},{25,1},{2,10},{10... | collective-permute-start | bytes 1769480 | tf_op jit(solution)/shard_map/ppermute | solution.py:367
  10.9 28.6 %collective-permute-start.1 = (bf16[288,1024]{1,0:T(8,128)(2,1)}, bf16[288,1024]{1,0:T(8,128)(2,1)S(1)}, u32[]{:S(2)}, u32[]{:S(2)}) collective-permute-start(bf16[288,1024]{1,0:T(8,128)(2,1)} %get-tuple-element.45.ext_ref.refs_0_), channel_id=1, source_target_pairs={{0,16},{8,24},{16,0},{24,8},{1,17},{9,25},{17,1},{25,9},{2,18},{10... | collective-permute-start | bytes 1769480 | tf_op jit(solution)/shard_map/ppermute | solution.py:367
  13.7 25.9 %collective-permute-start.2 = (bf16[288,1024]{1,0:T(8,128)(2,1)}, bf16[288,1024]{1,0:T(8,128)(2,1)S(1)}, u32[]{:S(2)}, u32[]{:S(2)}) collective-permute-start(bf16[288,1024]{1,0:T(8,128)(2,1)} %get-tuple-element.45.ext_ref.refs_0_), channel_id=1, source_target_pairs={{0,24},{8,0},{16,8},{24,16},{1,25},{9,1},{17,9},{25,17},{2,26},{10... | collective-permute-start | bytes 1769480 | tf_op jit(solution)/shard_map/ppermute | solution.py:367
  15.7 65.5 %copy-start.19 = (s32[32,128]{1,0:T(8,128)S(1)}, s32[32,128]{1,0:T(8,128)}, u32[]{:S(2)}) copy-start(s32[32,128]{1,0:T(8,128)} %get-tuple-element.38) | copy-start | bytes 49156
  22.1 40.8 %copy-start.5 = (bf16[256,1024]{1,0:T(8,128)(2,1)S(1)}, bf16[256,1024]{1,0:T(8,128)(2,1)}, u32[]{:S(2)}) copy-start(bf16[256,1024]{1,0:T(8,128)(2,1)} %get-tuple-element.58) | copy-start | bytes 1572868
  22.1 15.4 %collective-permute-start.3 = (bf16[256,1024]{1,0:T(8,128)(2,1)}, bf16[256,1024]{1,0:T(8,128)(2,1)S(1)}, u32[]{:S(2)}, u32[]{:S(2)}) collective-permute-start(bf16[256,1024]{1,0:T(8,128)(2,1)} %get-tuple-element.41), channel_id=1, source_target_pairs={{0,1},{1,2},{2,3},{3,0},{4,5},{5,6},{6,7},{7,4},{8,9},{9,10},{10,1... | collective-permute-start | bytes 1572872 | tf_op jit(solution)/shard_map/ppermute | solution.py:367
  24.1 13.4 %collective-permute-start.4 = (bf16[256,1024]{1,0:T(8,128)(2,1)}, bf16[256,1024]{1,0:T(8,128)(2,1)S(1)}, u32[]{:S(2)}, u32[]{:S(2)}) collective-permute-start(bf16[256,1024]{1,0:T(8,128)(2,1)} %get-tuple-element.42), channel_id=1, source_target_pairs={{0,3},{1,0},{2,1},{3,2},{4,7},{5,4},{6,5},{7,6},{8,11},{9,8},{10,9... | collective-permute-start | bytes 1572872 | tf_op jit(solution)/shard_map/ppermute | solution.py:367
  37.5 9.5 %copy-start.2 = (bf16[288,1024]{1,0:T(8,128)(2,1)}, bf16[288,1024]{1,0:T(8,128)(2,1)S(1)}, u32[]{:S(2)}) copy-start(bf16[288,1024]{1,0:T(8,128)(2,1)S(1)} %collective-permute-done.refs_1_) | copy-start | bytes 1769476
  39.6 7.4 %copy-start.3 = (bf16[288,1024]{1,0:T(8,128)(2,1)}, bf16[288,1024]{1,0:T(8,128)(2,1)S(1)}, u32[]{:S(2)}) copy-start(bf16[288,1024]{1,0:T(8,128)(2,1)S(1)} %collective-permute-done.1.refs_2_) | copy-start | bytes 1769476
  39.6 7.4 %copy-start.4 = (bf16[288,1024]{1,0:T(8,128)(2,1)}, bf16[288,1024]{1,0:T(8,128)(2,1)S(1)}, u32[]{:S(2)}) copy-start(bf16[288,1024]{1,0:T(8,128)(2,1)S(1)} %collective-permute-done.2.refs_3_) | copy-start | bytes 1769476
  43.7 19.1 %collective-permute-start.11 = (bf16[256,1024]{1,0:T(8,128)(2,1)}, bf16[256,1024]{1,0:T(8,128)(2,1)S(1)}, u32[]{:S(2)}, u32[]{:S(2)}) collective-permute-start(bf16[256,1024]{1,0:T(8,128)(2,1)} %get-tuple-element.61), channel_id=1, source_target_pairs={{0,2},{1,3},{2,0},{3,1},{4,6},{5,7},{6,4},{7,5},{8,10},{9,11},{10,... | collective-permute-start | bytes 1572872 | tf_op jit(solution)/shard_map/ppermute | solution.py:367
  57.1 22.5 %collective-permute-start.5 = (bf16[8,128,256]{2,1,0:T(8,128)(2,1)}, bf16[8,128,256]{2,1,0:T(8,128)(2,1)S(1)}, u32[]{:S(2)}, u32[]{:S(2)}) collective-permute-start(bf16[8,128,256]{2,1,0:T(8,128)(2,1)} %get-tuple-element.51), channel_id=1, source_target_pairs={{0,8},{8,16},{16,24},{24,0},{1,9},{9,17},{17,25},{25,1},{2,10},{10... | collective-permute-start | bytes 1572872 | tf_op jit(solution)/shard_map/ppermute | solution.py:367
  58.7 32.4 %collective-permute-start.6 = (bf16[8,128,256]{2,1,0:T(8,128)(2,1)}, bf16[8,128,256]{2,1,0:T(8,128)(2,1)S(1)}, u32[]{:S(2)}, u32[]{:S(2)}) collective-permute-start(bf16[8,128,256]{2,1,0:T(8,128)(2,1)} %get-tuple-element.52), channel_id=1, source_target_pairs={{0,16},{8,24},{16,0},{24,8},{1,17},{9,25},{17,1},{25,9},{2,18},{10... | collective-permute-start | bytes 1572872 | tf_op jit(solution)/shard_map/ppermute | solution.py:367
  61.4 29.8 %collective-permute-start.7 = (bf16[8,128,256]{2,1,0:T(8,128)(2,1)}, bf16[8,128,256]{2,1,0:T(8,128)(2,1)S(1)}, u32[]{:S(2)}, u32[]{:S(2)}) collective-permute-start(bf16[8,128,256]{2,1,0:T(8,128)(2,1)} %get-tuple-element.53), channel_id=1, source_target_pairs={{0,24},{8,0},{16,8},{24,16},{1,25},{9,1},{17,9},{25,17},{2,26},{10... | collective-permute-start | bytes 1572872 | tf_op jit(solution)/shard_map/ppermute | solution.py:367
  63.2 36.7 %copy-start = (bf16[256,1024]{1,0:T(8,128)(2,1)}, bf16[256,1024]{1,0:T(8,128)(2,1)S(1)}, u32[]{:S(2)}) copy-start(bf16[256,1024]{1,0:T(8,128)(2,1)S(1)} %add_convert_fusion.q0) | copy-start | bytes 1572868
  63.2 35.0 %collective-permute-start.12 = (bf16[256,1024]{1,0:T(8,128)(2,1)S(1)}, bf16[256,1024]{1,0:T(8,128)(2,1)S(1)}, u32[]{:S(2)}, u32[]{:S(2)}) collective-permute-start(bf16[256,1024]{1,0:T(8,128)(2,1)S(1)} %add_convert_fusion.q0), channel_id=1, source_target_pairs={{0,1},{1,2},{2,3},{3,0},{4,5},{5,6},{6,7},{7,4},{8,9},{9,10},{10,1... | collective-permute-start | bytes 1572872 | tf_op jit(solution)/shard_map/ppermute | solution.py:367
  63.9 36.0 %collective-permute-start.13 = (bf16[256,1024]{1,0:T(8,128)(2,1)S(1)}, bf16[256,1024]{1,0:T(8,128)(2,1)S(1)}, u32[]{:S(2)}, u32[]{:S(2)}) collective-permute-start(bf16[256,1024]{1,0:T(8,128)(2,1)S(1)} %add_convert_fusion.q0), channel_id=1, source_target_pairs={{0,2},{1,3},{2,0},{3,1},{4,6},{5,7},{6,4},{7,5},{8,10},{9,11},{10,... | collective-permute-start | bytes 1572872 | tf_op jit(solution)/shard_map/ppermute | solution.py:367
  79.6 11.5 %copy-start.9 = (bf16[8,128,256]{2,1,0:T(8,128)(2,1)}, bf16[8,128,256]{2,1,0:T(8,128)(2,1)S(1)}, u32[]{:S(2)}) copy-start(bf16[8,128,256]{2,1,0:T(8,128)(2,1)S(1)} %collective-permute-done.5.refs_1_) | copy-start | bytes 1572868
  79.6 20.2 %collective-permute-start.14 = (bf16[256,1024]{1,0:T(8,128)(2,1)S(1)}, bf16[256,1024]{1,0:T(8,128)(2,1)S(1)}, u32[]{:S(2)}, u32[]{:S(2)}) collective-permute-start(bf16[256,1024]{1,0:T(8,128)(2,1)S(1)} %add_convert_fusion.q0), channel_id=1, source_target_pairs={{0,3},{1,0},{2,1},{3,2},{4,7},{5,4},{6,5},{7,6},{8,11},{9,8},{10,9... | collective-permute-start | bytes 1572872 | tf_op jit(solution)/shard_map/ppermute | solution.py:367
  91.1 0.8 copy-start.10
  91.1 1.0 copy-start.11
  95.2 20.6 %copy-start.15 = (bf16[640,256]{1,0:T(8,128)(2,1)S(1)}, bf16[640,256]{1,0:T(8,128)(2,1)}, u32[]{:S(2)}) copy-start(bf16[640,256]{1,0:T(8,128)(2,1)} %get-tuple-element.63) | copy-start | bytes 983044
  95.2 17.3 %collective-permute-start.10 = (bf16[640,256]{1,0:T(8,128)(2,1)}, bf16[640,256]{1,0:T(8,128)(2,1)S(1)}, u32[]{:S(2)}, u32[]{:S(2)}) collective-permute-start(bf16[640,256]{1,0:T(8,128)(2,1)} %get-tuple-element.57), channel_id=1, source_target_pairs={{0,3},{1,0},{2,1},{3,2},{4,7},{5,4},{6,5},{7,6},{8,11},{9,8},{10,9... | collective-permute-start | bytes 983048 | tf_op jit(solution)/shard_map/ppermute | solution.py:367
  98.2 17.6 %collective-permute-start.8 = (bf16[640,256]{1,0:T(8,128)(2,1)}, bf16[640,256]{1,0:T(8,128)(2,1)S(1)}, u32[]{:S(2)}, u32[]{:S(2)}) collective-permute-start(bf16[640,256]{1,0:T(8,128)(2,1)} %get-tuple-element.55), channel_id=1, source_target_pairs={{0,1},{1,2},{2,3},{3,0},{4,5},{5,6},{6,7},{7,4},{8,9},{9,10},{10,1... | collective-permute-start | bytes 983048 | tf_op jit(solution)/shard_map/ppermute | solution.py:367
  98.2 1.7 copy-start.6
  98.2 17.6 %collective-permute-start.9 = (bf16[640,256]{1,0:T(8,128)(2,1)}, bf16[640,256]{1,0:T(8,128)(2,1)S(1)}, u32[]{:S(2)}, u32[]{:S(2)}) collective-permute-start(bf16[640,256]{1,0:T(8,128)(2,1)} %get-tuple-element.56), channel_id=1, source_target_pairs={{0,2},{1,3},{2,0},{3,1},{4,6},{5,7},{6,4},{7,5},{8,10},{9,11},{10,... | collective-permute-start | bytes 983048 | tf_op jit(solution)/shard_map/ppermute | solution.py:367
  99.9 0.8 copy-start.7
  100.7 0.8 copy-start.8
  116.0 16.3 %copy-start.1 = (bf16[640,256]{1,0:T(8,128)(2,1)}, bf16[640,256]{1,0:T(8,128)(2,1)S(1)}, u32[]{:S(2)}) copy-start(bf16[640,256]{1,0:T(8,128)(2,1)S(1)} %maximum_convert_fusion.g0) | copy-start | bytes 983044
  116.0 15.7 %collective-permute-start.15 = (bf16[640,256]{1,0:T(8,128)(2,1)S(1)}, bf16[640,256]{1,0:T(8,128)(2,1)S(1)}, u32[]{:S(2)}, u32[]{:S(2)}) collective-permute-start(bf16[640,256]{1,0:T(8,128)(2,1)S(1)} %maximum_convert_fusion.g0), channel_id=1, source_target_pairs={{0,1},{1,2},{2,3},{3,0},{4,5},{5,6},{6,7},{7,4},{8,9},{9,10},{10,1... | collective-permute-start | bytes 983048 | tf_op jit(solution)/shard_map/ppermute | solution.py:367
  116.1 15.6 %collective-permute-start.16 = (bf16[640,256]{1,0:T(8,128)(2,1)S(1)}, bf16[640,256]{1,0:T(8,128)(2,1)S(1)}, u32[]{:S(2)}, u32[]{:S(2)}) collective-permute-start(bf16[640,256]{1,0:T(8,128)(2,1)S(1)} %maximum_convert_fusion.g0), channel_id=1, source_target_pairs={{0,2},{1,3},{2,0},{3,1},{4,6},{5,7},{6,4},{7,5},{8,10},{9,11},{10,... | collective-permute-start | bytes 983048 | tf_op jit(solution)/shard_map/ppermute | solution.py:367
  117.8 14.5 %collective-permute-start.17 = (bf16[640,256]{1,0:T(8,128)(2,1)S(1)}, bf16[640,256]{1,0:T(8,128)(2,1)S(1)}, u32[]{:S(2)}, u32[]{:S(2)}) collective-permute-start(bf16[640,256]{1,0:T(8,128)(2,1)S(1)} %maximum_convert_fusion.g0), channel_id=1, source_target_pairs={{0,3},{1,0},{2,1},{3,2},{4,7},{5,4},{6,5},{7,6},{8,11},{9,8},{10,9... | collective-permute-start | bytes 983048 | tf_op jit(solution)/shard_map/ppermute | solution.py:367
  131.7 0.7 copy-start.12
  131.7 0.8 copy-start.13
  132.5 0.8 copy-start.14
  149.0 5.5 %collective-permute-start.18 = (f32[40,256]{1,0:T(8,128)}, f32[40,256]{1,0:T(8,128)S(1)}, u32[]{:S(2)}, u32[]{:S(2)}) collective-permute-start(f32[40,256]{1,0:T(8,128)} %logits.1.l0), channel_id=1, source_target_pairs={{0,1},{1,2},{2,3},{3,0},{4,5},{5,6},{6,7},{7,4},{8,9},{9,10},{10,1... | collective-permute-start | bytes 122888 | tf_op jit(solution)/shard_map/ppermute | solution.py:367
  150.1 5.7 %collective-permute-start.19 = (f32[40,256]{1,0:T(8,128)}, f32[40,256]{1,0:T(8,128)S(1)}, u32[]{:S(2)}, u32[]{:S(2)}) collective-permute-start(f32[40,256]{1,0:T(8,128)} %logits.1.l0), channel_id=1, source_target_pairs={{0,2},{1,3},{2,0},{3,1},{4,6},{5,7},{6,4},{7,5},{8,10},{9,11},{10,... | collective-permute-start | bytes 122888 | tf_op jit(solution)/shard_map/ppermute | solution.py:367
  153.0 4.2 %collective-permute-start.20 = (f32[40,256]{1,0:T(8,128)}, f32[40,256]{1,0:T(8,128)S(1)}, u32[]{:S(2)}, u32[]{:S(2)}) collective-permute-start(f32[40,256]{1,0:T(8,128)} %logits.1.l0), channel_id=1, source_target_pairs={{0,3},{1,0},{2,1},{3,2},{4,7},{5,4},{6,5},{7,6},{8,11},{9,8},{10,9... | collective-permute-start | bytes 122888 | tf_op jit(solution)/shard_map/ppermute | solution.py:367
  154.5 2.7 %copy-start.16 = (f32[40,256]{1,0:T(8,128)}, f32[40,256]{1,0:T(8,128)S(1)}, u32[]{:S(2)}) copy-start(f32[40,256]{1,0:T(8,128)S(1)} %collective-permute-done.18.l1) | copy-start | bytes 122884
  155.8 1.4 copy-start.17
  157.2 0.6 copy-start.18
Sparse Core Ops, SparseCore 0:
  9.1 34.6 all-gather.2
  46.0 92.2 all-gather.4

commit v3 on v2

--- a/solution.py
+++ b/solution.py
@@ -20,8 +20,8 @@
 VMEM = 56 * 1024 * 1024
 
 
-def params(**kw):
-    return pltpu.CompilerParams(vmem_limit_bytes=VMEM, **kw)
+def params(limit=VMEM):
+    return pltpu.CompilerParams(vmem_limit_bytes=limit)
 
 
 def dot(a, b, ca, cb):
@@ -299,14 +299,21 @@
     out_ref[ADAPTERS:, :] = own_ref[...]
     lane = iota((ROWS, 128), 1)
     found = jnp.zeros((ROWS, 128), F32)
-    for g in range(STEPS):
-        arrive(g)
-        turned = dot(probe_ref[...], held[g * PER : (g + 1) * PER].reshape(PER * B, WIDTH), 1, 1)
-        product = turned * bottles[:, g * PER * B : (g + 1) * PER * B].astype(F32)
-        for k in range(PER):
-            logit = jnp.sum(product[:, k * B : (k + 1) * B], axis=1, keepdims=True)
-            found = jnp.where(lane == ORDER[g * PER + k], logit, found)
+    turned = None
+    for g in range(STEPS + 1):
+        before = turned
+        if g < STEPS:
+            arrive(g)
+            turned = dot(probe_ref[...], held[g * PER : (g + 1) * PER].reshape(PER * B, WIDTH), 1, 1)
+        for i in range((g - 1) * PER, g * PER) if g else ():
+            k = i % PER
+            bottle = bottles[:, i * B : (i + 1) * B].astype(F32)
+            logit = jnp.sum(before[:, k * B : (k + 1) * B] * bottle, axis=1, keepdims=True)
+            found = jnp.where(lane == ORDER[i], logit, found)
     out_ref[0:ADAPTERS, :] = found.T[0:ADAPTERS, :]
+
+
+LESS = 48 * 1024 * 1024
 
 
 def logits_of(bottle, probe, own, up):
@@ -325,8 +332,12 @@
     )(bottle, probe, own, up)
 
 
-def join_kernel(bottle_ref, l0, l1, l2, l3, rank_ref, hid_ref, up_ref, out_ref, held, bottles, sems):
-    arrive = step_copies(up_ref, held, bottle_ref, bottles, sems)
+def join_kernel(bottles, l0, l1, l2, l3, rank_ref, hid_ref, up_ref, out_ref, held, sems):
+    copies = []
+    for g in range(STEPS):
+        some = pl.ds(g * PER, PER)
+        copies.append(pltpu.make_async_copy(up_ref.at[some], held.at[some], sems.at[g]))
+        copies[g].start()
     total = (l0[...] + l1[...]) + (l2[...] + l3[...])
     logits = (total[0:ADAPTERS] + total[ADAPTERS : ADAPTERS + 1]) * D ** (-0.5)
     chosen = rank_ref[...] >= 0.0
@@ -337,11 +348,11 @@
     total = hid_ref[...].astype(F32)
     for g in range(STEPS):
         mix = []
-        arrive(g)
         for i in range(g * PER, (g + 1) * PER):
             a = ORDER[i]
             bottle = bottles[:, i * B : (i + 1) * B].astype(F32)
             mix.append((bottle * share[:, a : a + 1]).astype(BF16))
+        copies[g].wait()
         up = held[g * PER : (g + 1) * PER].reshape(PER * B, WIDTH)
         total = total + dot(jnp.concatenate(mix, axis=1), up, 1, 0)
     out_ref[...] = total.astype(BF16)
@@ -351,14 +362,13 @@
     return pl.pallas_call(
         join_kernel,
         out_shape=jax.ShapeDtypeStruct((ROWS, WIDTH), BF16),
-        in_specs=[anywhere()] + [whole()] * 6 + [anywhere()],
+        in_specs=[whole()] * 7 + [anywhere()],
         out_specs=whole(),
         scratch_shapes=[
             pltpu.VMEM((ADAPTERS, B, WIDTH), BF16),
-            pltpu.VMEM((ROWS, ADAPTERS * B), BF16),
-            pltpu.SemaphoreType.DMA((2, STEPS)),
+            pltpu.SemaphoreType.DMA((STEPS,)),
         ],
-        compiler_params=params(),
+        compiler_params=params(LESS),
         name="join",
     )(bottle, *parts, rank, hidden, up)
 

time: 175 us -> 173 us (0.989)
  Pallas kernels: 57.4 us -> 55 us
    pallas_call x1, Pallas kernels: 9.94 us -> 7.44 us  [join(): pl.pallas_call(join_kernel, out_shape=jax.ShapeDtypeStruct((ROWS, WIDTH),...]
    unnamed x40 -> x42, local copies, waits for them, and re-layouts: 4.27 us -> 4.44 us
  transfers between devices with their start and end apart: 23 -> 23, of which waited for: 12 -> 11; matrix products, arithmetic and copies ran while one was open for 1% -> 1% of each run, Pallas kernels for 21% -> 22%
where the time goes in v3:
time: 173 us; the launch traced here: 172 us
  waiting for transfers between devices  61 us (35%)
  Pallas kernels  55 us (32%)
  starting transfers between devices  36.5 us (21%)
  between operations  13.6 us (8%)
  local copies, waits for them, and re-layouts  5.07 us (3%)
    ppermute x21, waiting for transfers between devices, shifted(): return lax.ppermute(x, axis, [(i, (i + s) % 4) for i in range(4)])  56.2 us
    ppermute x21, starting transfers between devices, shifted(): return lax.ppermute(x, axis, [(i, (i + s) % 4) for i in range(4)])  36.5 us
    pallas_call x1, Pallas kernels, logits_of(): pl.pallas_call(logits_kernel, out_shape=jax.ShapeDtypeStruct((ADAPTERS +...  10.3 us
    pallas_call x1, Pallas kernels, squeeze(): pl.pallas_call(squeeze_kernel, out_shape=[jax.ShapeDtypeStruct((8, CAP, B...  10.2 us
    pallas_call x1, Pallas kernels, join(): pl.pallas_call(join_kernel, out_shape=jax.ShapeDtypeStruct((ROWS, WIDTH),...  7.44 us
    pallas_call x1, Pallas kernels, probe_of(): pl.pallas_call(probe_kernel, out_shape=(jax.ShapeDtypeStruct((ROWS, WIDTH...  7.32 us
    pallas_call x1, Pallas kernels, query_parts(): pl.pallas_call(query_kernel, out_shape=[jax.ShapeDtypeStruct((ROWS, WIDTH...  6.35 us
    pallas_call x1, Pallas kernels, expand(): pl.pallas_call(expand_kernel, out_shape=jax.ShapeDtypeStruct((ROWS, ADAPT...  5.49 us
  transfers between devices with their start and end apart: 23, of which 11 were waited for; matrix products, arithmetic and copies ran while one was open for 1% of the time, Pallas kernels for 22%

profile of v3, /device:TPU:0, one launch (start us, length us, event | category | flops | bytes accessed | tf_op | source)
XLA Modules:
  0.0 172.4 jit_solution(17312687274263845466)
XLA Ops:
  6.5 0.7 all-gather.3.cloned.1.call-update
  7.3 0.0 all-gather.5.cloned.1.call-start
  7.3 2.1 %plan.1 = (bf16[288,1024]{1,0:T(8,128)(2,1)}, f32[32,256]{1,0:T(8,128)}, s32[32,128]{1,0:T(8,128)}) custom-call(s32[8,256]{1,0:T(8,128)} %bitcast.5, bf16[256,1024]{1,0:T(8,128)(2,1)} %hid_ref.5), custom_call_target="tpu_custom_call" | custom-call | tf_op jit(solution)/shard_map/plan/pallas_call | solution.py:67
  9.4 1.6 collective-permute-start
  11.0 2.7 %collective-permute-start.1 = (bf16[288,1024]{1,0:T(8,128)(2,1)}, bf16[288,1024]{1,0:T(8,128)(2,1)S(1)}, u32[]{:S(2)}, u32[]{:S(2)}) collective-permute-start(bf16[288,1024]{1,0:T(8,128)(2,1)} %get-tuple-element.45.ext_ref.refs_0_), channel_id=1, source_target_pairs={{0,16},{8,24},{16,0},{24,8},{1,17},{9,25},{17,1},{25,9},{2,18},{10... | collective-permute-start | bytes 1769480 | tf_op jit(solution)/shard_map/ppermute | solution.py:377
  13.7 1.4 collective-permute-start.2
  15.1 0.7 pad_add_fusion.pos_ref
  15.8 6.4 %query_parts.1 = (bf16[256,1024]{1,0:T(8,128)(2,1)}, bf16[256,1024]{1,0:T(8,128)(2,1)}, bf16[256,1024]{1,0:T(8,128)(2,1)}, bf16[256,1024]{1,0:T(8,128)(2,1)}) custom-call(s32[4]{0:T(128)} %pad_add_fusion.pos_ref, bf16[288,1024]{1,0:T(8,128)(2,1)} %get-tuple-element.45.ext_ref.refs_0_, bf16[1024,4096]{1,0:T(8,128)(2,1)} %weight_ref.2), custom_call_target="tpu_custom_call" | custom-call | tf_op jit(solution)/shard_map/query_parts/pallas_call | solution.py:121
  22.1 2.0 %collective-permute-start.3 = (bf16[256,1024]{1,0:T(8,128)(2,1)}, bf16[256,1024]{1,0:T(8,128)(2,1)S(1)}, u32[]{:S(2)}, u32[]{:S(2)}) collective-permute-start(bf16[256,1024]{1,0:T(8,128)(2,1)} %get-tuple-element.41), channel_id=1, source_target_pairs={{0,1},{1,2},{2,3},{3,0},{4,5},{5,6},{6,7},{7,4},{8,9},{9,10},{10,1... | collective-permute-start | bytes 1572872 | tf_op jit(solution)/shard_map/ppermute | solution.py:377
  24.1 2.2 %collective-permute-start.4 = (bf16[256,1024]{1,0:T(8,128)(2,1)}, bf16[256,1024]{1,0:T(8,128)(2,1)S(1)}, u32[]{:S(2)}, u32[]{:S(2)}) collective-permute-start(bf16[256,1024]{1,0:T(8,128)(2,1)} %get-tuple-element.42), channel_id=1, source_target_pairs={{0,3},{1,0},{2,1},{3,2},{4,7},{5,4},{6,5},{7,6},{8,11},{9,8},{10,9... | collective-permute-start | bytes 1572872 | tf_op jit(solution)/shard_map/ppermute | solution.py:377
  26.3 2.9 %spread.1.pick_ref = bf16[256,4096]{1,0:T(8,128)(2,1)} custom-call(f32[32,256]{1,0:T(8,128)} %get-tuple-element.44.rank_ref), custom_call_target="tpu_custom_call" | custom-call | tf_op jit(solution)/shard_map/spread/pallas_call | solution.py:91
  29.2 8.3 %collective-permute-done.3 = bf16[256,1024]{1,0:T(8,128)(2,1)S(1)} collective-permute-done((bf16[256,1024]{1,0:T(8,128)(2,1)}, bf16[256,1024]{1,0:T(8,128)(2,1)S(1)}, u32[]{:S(2)}, u32[]{:S(2)}) %collective-permute-start.3) | collective-permute-done | bytes 524320 | tf_op jit(solution)/shard_map/ppermute | solution.py:377
  37.5 0.0 collective-permute-done.4
  37.5 0.0 collective-permute-done.refs_1_
  37.6 2.0 %collective-permute-done.1.refs_2_ = bf16[288,1024]{1,0:T(8,128)(2,1)S(1)} collective-permute-done((bf16[288,1024]{1,0:T(8,128)(2,1)}, bf16[288,1024]{1,0:T(8,128)(2,1)S(1)}, u32[]{:S(2)}, u32[]{:S(2)}) %collective-permute-start.1) | collective-permute-done | bytes 589856 | tf_op jit(solution)/shard_map/ppermute | solution.py:377
  39.6 0.0 collective-permute-done.2.refs_3_
  39.6 4.1 %all-gather.3.cloned.1.call-done.refs_4_ = bf16[8,1024,256]{2,1,0:T(8,128)(2,1)} async-done(((bf16[1,1024,256]{2,1,0:T(8,128)(2,1)}), bf16[8,1024,256]{2,1,0:T(8,128)(2,1)}) %all-gather.3.cloned.1.call-update) | async-done | bytes 4194320 | tf_op jit(solution)/shard_map/all_gather | solution.py:400
  43.7 0.0 all-gather.5.cloned.1.call-update
  43.7 3.2 %collective-permute-start.11 = (bf16[256,1024]{1,0:T(8,128)(2,1)}, bf16[256,1024]{1,0:T(8,128)(2,1)S(1)}, u32[]{:S(2)}, u32[]{:S(2)}) collective-permute-start(bf16[256,1024]{1,0:T(8,128)(2,1)} %get-tuple-element.61), channel_id=1, source_target_pairs={{0,2},{1,3},{2,0},{3,1},{4,6},{5,7},{6,4},{7,5},{8,10},{9,11},{10,... | collective-permute-start | bytes 1572872 | tf_op jit(solution)/shard_map/ppermute | solution.py:377
  47.0 10.2 %squeeze.5 = (bf16[8,128,256]{2,1,0:T(8,128)(2,1)}, bf16[8,128,256]{2,1,0:T(8,128)(2,1)}, bf16[8,128,256]{2,1,0:T(8,128)(2,1)}, bf16[8,128,256]{2,1,0:T(8,128)(2,1)}) custom-call(s32[4]{0:T(128)} %pad_add_fusion.pos_ref, bf16[288,1024]{1,0:T(8,128)(2,1)} %get-tuple-element.45.ext_ref.refs_0_, bf16[288,1024]{1,0:T(8,128)(2,1)} %copy-done.6, ...), custom_call_target="tpu_custom_call" | custom-call | tf_op jit(solution)/shard_map/squeeze/pallas_call | solution.py:198
  57.1 1.5 collective-permute-start.5
  58.7 2.7 %collective-permute-start.6 = (bf16[8,128,256]{2,1,0:T(8,128)(2,1)}, bf16[8,128,256]{2,1,0:T(8,128)(2,1)S(1)}, u32[]{:S(2)}, u32[]{:S(2)}) collective-permute-start(bf16[8,128,256]{2,1,0:T(8,128)(2,1)} %get-tuple-element.52), channel_id=1, source_target_pairs={{0,16},{8,24},{16,0},{24,8},{1,17},{9,25},{17,1},{25,9},{2,18},{10... | collective-permute-start | bytes 1572872 | tf_op jit(solution)/shard_map/ppermute | solution.py:377
  61.4 1.5 collective-permute-start.7
  62.8 0.4 add_convert_fusion.q0
  63.2 0.7 collective-permute-start.12
  63.9 1.9 %collective-permute-start.13 = (bf16[256,1024]{1,0:T(8,128)(2,1)S(1)}, bf16[256,1024]{1,0:T(8,128)(2,1)S(1)}, u32[]{:S(2)}, u32[]{:S(2)}) collective-permute-start(bf16[256,1024]{1,0:T(8,128)(2,1)S(1)} %add_convert_fusion.q0), channel_id=1, source_target_pairs={{0,2},{1,3},{2,0},{3,1},{4,6},{5,7},{6,4},{7,5},{8,10},{9,11},{10,... | collective-permute-start | bytes 1572872 | tf_op jit(solution)/shard_map/ppermute | solution.py:377
  65.8 13.8 %collective-permute-done.5.refs_1_ = bf16[8,128,256]{2,1,0:T(8,128)(2,1)S(1)} collective-permute-done((bf16[8,128,256]{2,1,0:T(8,128)(2,1)}, bf16[8,128,256]{2,1,0:T(8,128)(2,1)S(1)}, u32[]{:S(2)}, u32[]{:S(2)}) %collective-permute-start.5) | collective-permute-done | bytes 524320 | tf_op jit(solution)/shard_map/ppermute | solution.py:377
  79.6 1.6 collective-permute-start.14
  81.2 0.6 slice_reduce_fusion.off_ref
  81.9 9.2 %collective-permute-done.6.refs_2_ = bf16[8,128,256]{2,1,0:T(8,128)(2,1)S(1)} collective-permute-done((bf16[8,128,256]{2,1,0:T(8,128)(2,1)}, bf16[8,128,256]{2,1,0:T(8,128)(2,1)S(1)}, u32[]{:S(2)}, u32[]{:S(2)}) %collective-permute-start.6) | collective-permute-done | bytes 524320 | tf_op jit(solution)/shard_map/ppermute | solution.py:377
  91.1 0.0 collective-permute-done.7.refs_3_
  91.1 0.8 copy-done.14
  91.9 0.3 copy-done.15
  92.2 3.0 %pack.1 = (bf16[640,256]{1,0:T(8,128)(2,1)}, bf16[640,256]{1,0:T(8,128)(2,1)}, bf16[640,256]{1,0:T(8,128)(2,1)}, bf16[640,256]{1,0:T(8,128)(2,1)}) custom-call(s32[4]{0:T(128)} %pad_add_fusion.pos_ref, s32[32]{0:T(128)} %slice_reduce_fusion.off_ref, bf16[8,128,256]{2,1,0:T(8,128)(2,1)} %get-tuple-element.50.refs_0_, bf16[8,128,256]{2,1,0:T(8,128)(2,1)} %copy-done.13, ...), custom_call_target="tpu_custom_call" | custom-call | tf_op jit(solution)/shard_map/pack/pallas_call | solution.py:230
  95.2 3.0 %collective-permute-start.10 = (bf16[640,256]{1,0:T(8,128)(2,1)}, bf16[640,256]{1,0:T(8,128)(2,1)S(1)}, u32[]{:S(2)}, u32[]{:S(2)}) collective-permute-start(bf16[640,256]{1,0:T(8,128)(2,1)} %get-tuple-element.57), channel_id=1, source_target_pairs={{0,3},{1,0},{2,1},{3,2},{4,7},{5,4},{6,5},{7,6},{8,11},{9,8},{10,9... | collective-permute-start | bytes 983048 | tf_op jit(solution)/shard_map/ppermute | solution.py:377
  98.2 0.0 collective-permute-start.8
  98.2 1.7 collective-permute-start.9
  99.9 0.0 collective-permute-done.14.q3
  99.9 0.8 copy-done.11
  100.7 0.8 copy-done.12
  101.5 7.3 %probe.1 = (bf16[256,1024]{1,0:T(8,128)(2,1)}, f32[8,256]{1,0:T(8,128)}) custom-call(s32[4]{0:T(128)} %pad_add_fusion.pos_ref, bf16[256,1024]{1,0:T(8,128)(2,1)} %copy-done.4, bf16[256,1024]{1,0:T(8,128)(2,1)} %copy-done.10, bf16[256,1024]{1,0:T(8,128)(2,1)} %copy-done.11, bf16[256,1024]{1,0:T(8,128)(2,1)} %copy-done.12, bf16[256,1024]{1,0:T(8,128)(2,1)} %hid_ref.5, ...), custom_call_target="tpu_custom_call" | custom-call | tf_op jit(solution)/shard_map/probe/pallas_call | solution.py:145
  108.8 3.6 %collective-permute-done.10 = bf16[640,256]{1,0:T(8,128)(2,1)S(1)} collective-permute-done((bf16[640,256]{1,0:T(8,128)(2,1)}, bf16[640,256]{1,0:T(8,128)(2,1)S(1)}, u32[]{:S(2)}, u32[]{:S(2)}) %collective-permute-start.10) | collective-permute-done | bytes 327712 | tf_op jit(solution)/shard_map/ppermute | solution.py:377
  112.5 3.3 %collective-permute-done.8 = bf16[640,256]{1,0:T(8,128)(2,1)S(1)} collective-permute-done((bf16[640,256]{1,0:T(8,128)(2,1)}, bf16[640,256]{1,0:T(8,128)(2,1)S(1)}, u32[]{:S(2)}, u32[]{:S(2)}) %collective-permute-start.8) | collective-permute-done | bytes 327712 | tf_op jit(solution)/shard_map/ppermute | solution.py:377
  115.8 0.0 collective-permute-done.9
  115.8 0.2 maximum_convert_fusion.g0
  116.0 0.0 copy-start.5
  116.0 0.1 collective-permute-start.15
  116.0 1.7 %collective-permute-start.16 = (bf16[640,256]{1,0:T(8,128)(2,1)S(1)}, bf16[640,256]{1,0:T(8,128)(2,1)S(1)}, u32[]{:S(2)}, u32[]{:S(2)}) collective-permute-start(bf16[640,256]{1,0:T(8,128)(2,1)S(1)} %maximum_convert_fusion.g0), channel_id=1, source_target_pairs={{0,2},{1,3},{2,0},{3,1},{4,6},{5,7},{6,4},{7,5},{8,10},{9,11},{10,... | collective-permute-start | bytes 983048 | tf_op jit(solution)/shard_map/ppermute | solution.py:377
  117.8 1.5 collective-permute-start.17
  119.3 12.4 %collective-permute-done.15.g1 = bf16[640,256]{1,0:T(8,128)(2,1)S(1)} collective-permute-done((bf16[640,256]{1,0:T(8,128)(2,1)S(1)}, bf16[640,256]{1,0:T(8,128)(2,1)S(1)}, u32[]{:S(2)}, u32[]{:S(2)}) %collective-permute-start.15) | collective-permute-done | bytes 327712 | tf_op jit(solution)/shard_map/ppermute | solution.py:377
  131.6 0.6 collective-permute-done.17.g3
  132.3 0.1 copy-done.16
  132.3 0.1 copy-done.17
  132.5 0.7 copy-done.18
  133.2 5.5 %expand.1.bottle_ref.bottles = bf16[256,8192]{1,0:T(8,128)(2,1)} custom-call(s32[4]{0:T(128)} %pad_add_fusion.pos_ref, s32[32]{0:T(128)} %slice_reduce_fusion.off_ref, bf16[640,256]{1,0:T(8,128)(2,1)} %copy-done.5, bf16[640,256]{1,0:T(8,128)(2,1)} %copy-done.16, bf16[640,256]{1,0:T(8,128)(2,1)} %copy-done.17, bf16[640,256]{1,0:T(8,128)(2,1)} %copy-done.18, ...), custom_call_target="tpu_custom_call" | custom-call | tf_op jit(solution)/shard_map/expand/pallas_call | solution.py:286
  138.7 10.3 %logits.1.l0 = f32[40,256]{1,0:T(8,128)} custom-call(bf16[256,8192]{1,0:T(8,128)(2,1)} %expand.1.bottle_ref.bottles, bf16[256,1024]{1,0:T(8,128)(2,1)} %get-tuple-element.68.probe_ref, f32[8,256]{1,0:T(8,128)} %get-tuple-element.69.own_ref, bf16[32,256,1024]{2,1,0:T(8,128)(2,1)} %all-gather.5.cloned.1.call-done.up_ref), custom_call_target="tpu_custom_call" | custom-call | tf_op jit(solution)/shard_map/logits/pallas_call | solution.py:320
  149.1 1.2 collective-permute-start.18
  150.3 2.9 %collective-permute-start.19 = (f32[40,256]{1,0:T(8,128)}, f32[40,256]{1,0:T(8,128)S(1)}, u32[]{:S(2)}, u32[]{:S(2)}) collective-permute-start(f32[40,256]{1,0:T(8,128)} %logits.1.l0), channel_id=1, source_target_pairs={{0,2},{1,3},{2,0},{3,1},{4,6},{5,7},{6,4},{7,5},{8,10},{9,11},{10,... | collective-permute-start | bytes 122888 | tf_op jit(solution)/shard_map/ppermute | solution.py:377
  153.1 1.4 collective-permute-start.20
  154.5 0.0 collective-permute-done.18.l1
  154.5 1.4 collective-permute-done.19.l2
  156.0 1.4 collective-permute-done.20.l3
  157.4 0.8 copy-done.2
  158.1 7.4 %join.1 = bf16[256,1024]{1,0:T(8,128)(2,1)} custom-call(bf16[256,8192]{1,0:T(8,128)(2,1)S(1)} %copy-done, f32[40,256]{1,0:T(8,128)S(1)} %copy-done.2, f32[40,256]{1,0:T(8,128)S(1)} %collective-permute-done.18.l1, f32[40,256]{1,0:T(8,128)S(1)} %collective-permute-done.19.l2, f32[40,256]{1,0:T(8,128)S(1)} %collective-permute-done.20.l3, ...), custom_call_target="tpu_custom_call" | custom-call | tf_op jit(solution)/shard_map/join/pallas_call | solution.py:362
  (39 shorter events, 0.1 us)
Async XLA Ops:
  6.5 37.2 %all-gather.3.cloned.1.call-start = ((), (), s32[]{:S(2)}) async-start(), calls=%async_computation | async-start | bytes 4718592 | tf_op jit(solution)/shard_map/all_gather | solution.py:400
  7.3 131.5 %all-gather.5.cloned.1.call-start = ((), (), s32[]{:S(2)}) async-start(), calls=%async_computation.1 | async-start | bytes 17301504 | tf_op jit(solution)/shard_map/all_gather | solution.py:407
  9.4 28.2 %collective-permute-start = (bf16[288,1024]{1,0:T(8,128)(2,1)}, bf16[288,1024]{1,0:T(8,128)(2,1)S(1)}, u32[]{:S(2)}, u32[]{:S(2)}) collective-permute-start(bf16[288,1024]{1,0:T(8,128)(2,1)} %get-tuple-element.45.ext_ref.refs_0_), channel_id=1, source_target_pairs={{0,8},{8,16},{16,24},{24,0},{1,9},{9,17},{17,25},{25,1},{2,10},{10... | collective-permute-start | bytes 1769480 | tf_op jit(solution)/shard_map/ppermute | solution.py:377
  11.0 28.6 %collective-permute-start.1 = (bf16[288,1024]{1,0:T(8,128)(2,1)}, bf16[288,1024]{1,0:T(8,128)(2,1)S(1)}, u32[]{:S(2)}, u32[]{:S(2)}) collective-permute-start(bf16[288,1024]{1,0:T(8,128)(2,1)} %get-tuple-element.45.ext_ref.refs_0_), channel_id=1, source_target_pairs={{0,16},{8,24},{16,0},{24,8},{1,17},{9,25},{17,1},{25,9},{2,18},{10... | collective-permute-start | bytes 1769480 | tf_op jit(solution)/shard_map/ppermute | solution.py:377
  13.7 25.9 %collective-permute-start.2 = (bf16[288,1024]{1,0:T(8,128)(2,1)}, bf16[288,1024]{1,0:T(8,128)(2,1)S(1)}, u32[]{:S(2)}, u32[]{:S(2)}) collective-permute-start(bf16[288,1024]{1,0:T(8,128)(2,1)} %get-tuple-element.45.ext_ref.refs_0_), channel_id=1, source_target_pairs={{0,24},{8,0},{16,8},{24,16},{1,25},{9,1},{17,9},{25,17},{2,26},{10... | collective-permute-start | bytes 1769480 | tf_op jit(solution)/shard_map/ppermute | solution.py:377
  15.8 65.5 %copy-start.20 = (s32[32,128]{1,0:T(8,128)S(1)}, s32[32,128]{1,0:T(8,128)}, u32[]{:S(2)}) copy-start(s32[32,128]{1,0:T(8,128)} %get-tuple-element.38) | copy-start | bytes 49156
  22.1 40.7 %copy-start.9 = (bf16[256,1024]{1,0:T(8,128)(2,1)S(1)}, bf16[256,1024]{1,0:T(8,128)(2,1)}, u32[]{:S(2)}) copy-start(bf16[256,1024]{1,0:T(8,128)(2,1)} %get-tuple-element.58) | copy-start | bytes 1572868
  22.1 15.4 %collective-permute-start.3 = (bf16[256,1024]{1,0:T(8,128)(2,1)}, bf16[256,1024]{1,0:T(8,128)(2,1)S(1)}, u32[]{:S(2)}, u32[]{:S(2)}) collective-permute-start(bf16[256,1024]{1,0:T(8,128)(2,1)} %get-tuple-element.41), channel_id=1, source_target_pairs={{0,1},{1,2},{2,3},{3,0},{4,5},{5,6},{6,7},{7,4},{8,9},{9,10},{10,1... | collective-permute-start | bytes 1572872 | tf_op jit(solution)/shard_map/ppermute | solution.py:377
  24.1 13.4 %collective-permute-start.4 = (bf16[256,1024]{1,0:T(8,128)(2,1)}, bf16[256,1024]{1,0:T(8,128)(2,1)S(1)}, u32[]{:S(2)}, u32[]{:S(2)}) collective-permute-start(bf16[256,1024]{1,0:T(8,128)(2,1)} %get-tuple-element.42), channel_id=1, source_target_pairs={{0,3},{1,0},{2,1},{3,2},{4,7},{5,4},{6,5},{7,6},{8,11},{9,8},{10,9... | collective-permute-start | bytes 1572872 | tf_op jit(solution)/shard_map/ppermute | solution.py:377
  37.6 9.4 %copy-start.6 = (bf16[288,1024]{1,0:T(8,128)(2,1)}, bf16[288,1024]{1,0:T(8,128)(2,1)S(1)}, u32[]{:S(2)}) copy-start(bf16[288,1024]{1,0:T(8,128)(2,1)S(1)} %collective-permute-done.refs_1_) | copy-start | bytes 1769476
  39.6 7.4 %copy-start.7 = (bf16[288,1024]{1,0:T(8,128)(2,1)}, bf16[288,1024]{1,0:T(8,128)(2,1)S(1)}, u32[]{:S(2)}) copy-start(bf16[288,1024]{1,0:T(8,128)(2,1)S(1)} %collective-permute-done.1.refs_2_) | copy-start | bytes 1769476
  39.6 7.4 %copy-start.8 = (bf16[288,1024]{1,0:T(8,128)(2,1)}, bf16[288,1024]{1,0:T(8,128)(2,1)S(1)}, u32[]{:S(2)}) copy-start(bf16[288,1024]{1,0:T(8,128)(2,1)S(1)} %collective-permute-done.2.refs_3_) | copy-start | bytes 1769476
  43.7 19.1 %collective-permute-start.11 = (bf16[256,1024]{1,0:T(8,128)(2,1)}, bf16[256,1024]{1,0:T(8,128)(2,1)S(1)}, u32[]{:S(2)}, u32[]{:S(2)}) collective-permute-start(bf16[256,1024]{1,0:T(8,128)(2,1)} %get-tuple-element.61), channel_id=1, source_target_pairs={{0,2},{1,3},{2,0},{3,1},{4,6},{5,7},{6,4},{7,5},{8,10},{9,11},{10,... | collective-permute-start | bytes 1572872 | tf_op jit(solution)/shard_map/ppermute | solution.py:377
  57.1 22.5 %collective-permute-start.5 = (bf16[8,128,256]{2,1,0:T(8,128)(2,1)}, bf16[8,128,256]{2,1,0:T(8,128)(2,1)S(1)}, u32[]{:S(2)}, u32[]{:S(2)}) collective-permute-start(bf16[8,128,256]{2,1,0:T(8,128)(2,1)} %get-tuple-element.51), channel_id=1, source_target_pairs={{0,8},{8,16},{16,24},{24,0},{1,9},{9,17},{17,25},{25,1},{2,10},{10... | collective-permute-start | bytes 1572872 | tf_op jit(solution)/shard_map/ppermute | solution.py:377
  58.7 32.4 %collective-permute-start.6 = (bf16[8,128,256]{2,1,0:T(8,128)(2,1)}, bf16[8,128,256]{2,1,0:T(8,128)(2,1)S(1)}, u32[]{:S(2)}, u32[]{:S(2)}) collective-permute-start(bf16[8,128,256]{2,1,0:T(8,128)(2,1)} %get-tuple-element.52), channel_id=1, source_target_pairs={{0,16},{8,24},{16,0},{24,8},{1,17},{9,25},{17,1},{25,9},{2,18},{10... | collective-permute-start | bytes 1572872 | tf_op jit(solution)/shard_map/ppermute | solution.py:377
  61.4 29.7 %collective-permute-start.7 = (bf16[8,128,256]{2,1,0:T(8,128)(2,1)}, bf16[8,128,256]{2,1,0:T(8,128)(2,1)S(1)}, u32[]{:S(2)}, u32[]{:S(2)}) collective-permute-start(bf16[8,128,256]{2,1,0:T(8,128)(2,1)} %get-tuple-element.53), channel_id=1, source_target_pairs={{0,24},{8,0},{16,8},{24,16},{1,25},{9,1},{17,9},{25,17},{2,26},{10... | collective-permute-start | bytes 1572872 | tf_op jit(solution)/shard_map/ppermute | solution.py:377
  63.2 36.7 %copy-start.4 = (bf16[256,1024]{1,0:T(8,128)(2,1)}, bf16[256,1024]{1,0:T(8,128)(2,1)S(1)}, u32[]{:S(2)}) copy-start(bf16[256,1024]{1,0:T(8,128)(2,1)S(1)} %add_convert_fusion.q0) | copy-start | bytes 1572868
  63.2 35.0 %collective-permute-start.12 = (bf16[256,1024]{1,0:T(8,128)(2,1)S(1)}, bf16[256,1024]{1,0:T(8,128)(2,1)S(1)}, u32[]{:S(2)}, u32[]{:S(2)}) collective-permute-start(bf16[256,1024]{1,0:T(8,128)(2,1)S(1)} %add_convert_fusion.q0), channel_id=1, source_target_pairs={{0,1},{1,2},{2,3},{3,0},{4,5},{5,6},{6,7},{7,4},{8,9},{9,10},{10,1... | collective-permute-start | bytes 1572872 | tf_op jit(solution)/shard_map/ppermute | solution.py:377
  63.9 36.0 %collective-permute-start.13 = (bf16[256,1024]{1,0:T(8,128)(2,1)S(1)}, bf16[256,1024]{1,0:T(8,128)(2,1)S(1)}, u32[]{:S(2)}, u32[]{:S(2)}) collective-permute-start(bf16[256,1024]{1,0:T(8,128)(2,1)S(1)} %add_convert_fusion.q0), channel_id=1, source_target_pairs={{0,2},{1,3},{2,0},{3,1},{4,6},{5,7},{6,4},{7,5},{8,10},{9,11},{10,... | collective-permute-start | bytes 1572872 | tf_op jit(solution)/shard_map/ppermute | solution.py:377
  79.6 11.5 %copy-start.13 = (bf16[8,128,256]{2,1,0:T(8,128)(2,1)}, bf16[8,128,256]{2,1,0:T(8,128)(2,1)S(1)}, u32[]{:S(2)}) copy-start(bf16[8,128,256]{2,1,0:T(8,128)(2,1)S(1)} %collective-permute-done.5.refs_1_) | copy-start | bytes 1572868
  79.6 20.3 %collective-permute-start.14 = (bf16[256,1024]{1,0:T(8,128)(2,1)S(1)}, bf16[256,1024]{1,0:T(8,128)(2,1)S(1)}, u32[]{:S(2)}, u32[]{:S(2)}) collective-permute-start(bf16[256,1024]{1,0:T(8,128)(2,1)S(1)} %add_convert_fusion.q0), channel_id=1, source_target_pairs={{0,3},{1,0},{2,1},{3,2},{4,7},{5,4},{6,5},{7,6},{8,11},{9,8},{10,9... | collective-permute-start | bytes 1572872 | tf_op jit(solution)/shard_map/ppermute | solution.py:377
  91.1 0.8 copy-start.14
  91.1 1.1 copy-start.15
  95.2 20.6 %copy-start.19 = (bf16[640,256]{1,0:T(8,128)(2,1)S(1)}, bf16[640,256]{1,0:T(8,128)(2,1)}, u32[]{:S(2)}) copy-start(bf16[640,256]{1,0:T(8,128)(2,1)} %get-tuple-element.63) | copy-start | bytes 983044
  95.2 17.3 %collective-permute-start.10 = (bf16[640,256]{1,0:T(8,128)(2,1)}, bf16[640,256]{1,0:T(8,128)(2,1)S(1)}, u32[]{:S(2)}, u32[]{:S(2)}) collective-permute-start(bf16[640,256]{1,0:T(8,128)(2,1)} %get-tuple-element.57), channel_id=1, source_target_pairs={{0,3},{1,0},{2,1},{3,2},{4,7},{5,4},{6,5},{7,6},{8,11},{9,8},{10,9... | collective-permute-start | bytes 983048 | tf_op jit(solution)/shard_map/ppermute | solution.py:377
  98.2 17.6 %collective-permute-start.8 = (bf16[640,256]{1,0:T(8,128)(2,1)}, bf16[640,256]{1,0:T(8,128)(2,1)S(1)}, u32[]{:S(2)}, u32[]{:S(2)}) collective-permute-start(bf16[640,256]{1,0:T(8,128)(2,1)} %get-tuple-element.55), channel_id=1, source_target_pairs={{0,1},{1,2},{2,3},{3,0},{4,5},{5,6},{6,7},{7,4},{8,9},{9,10},{10,1... | collective-permute-start | bytes 983048 | tf_op jit(solution)/shard_map/ppermute | solution.py:377
  98.2 1.7 %copy-start.10 = (bf16[256,1024]{1,0:T(8,128)(2,1)}, bf16[256,1024]{1,0:T(8,128)(2,1)S(1)}, u32[]{:S(2)}) copy-start(bf16[256,1024]{1,0:T(8,128)(2,1)S(1)} %collective-permute-done.12.q1) | copy-start | bytes 1572868
  98.2 17.6 %collective-permute-start.9 = (bf16[640,256]{1,0:T(8,128)(2,1)}, bf16[640,256]{1,0:T(8,128)(2,1)S(1)}, u32[]{:S(2)}, u32[]{:S(2)}) collective-permute-start(bf16[640,256]{1,0:T(8,128)(2,1)} %get-tuple-element.56), channel_id=1, source_target_pairs={{0,2},{1,3},{2,0},{3,1},{4,6},{5,7},{6,4},{7,5},{8,10},{9,11},{10,... | collective-permute-start | bytes 983048 | tf_op jit(solution)/shard_map/ppermute | solution.py:377
  99.9 0.8 copy-start.11
  100.7 0.8 copy-start.12
  116.0 16.3 %copy-start.5 = (bf16[640,256]{1,0:T(8,128)(2,1)}, bf16[640,256]{1,0:T(8,128)(2,1)S(1)}, u32[]{:S(2)}) copy-start(bf16[640,256]{1,0:T(8,128)(2,1)S(1)} %maximum_convert_fusion.g0) | copy-start | bytes 983044
  116.0 15.7 %collective-permute-start.15 = (bf16[640,256]{1,0:T(8,128)(2,1)S(1)}, bf16[640,256]{1,0:T(8,128)(2,1)S(1)}, u32[]{:S(2)}, u32[]{:S(2)}) collective-permute-start(bf16[640,256]{1,0:T(8,128)(2,1)S(1)} %maximum_convert_fusion.g0), channel_id=1, source_target_pairs={{0,1},{1,2},{2,3},{3,0},{4,5},{5,6},{6,7},{7,4},{8,9},{9,10},{10,1... | collective-permute-start | bytes 983048 | tf_op jit(solution)/shard_map/ppermute | solution.py:377
  116.0 15.6 %collective-permute-start.16 = (bf16[640,256]{1,0:T(8,128)(2,1)S(1)}, bf16[640,256]{1,0:T(8,128)(2,1)S(1)}, u32[]{:S(2)}, u32[]{:S(2)}) collective-permute-start(bf16[640,256]{1,0:T(8,128)(2,1)S(1)} %maximum_convert_fusion.g0), channel_id=1, source_target_pairs={{0,2},{1,3},{2,0},{3,1},{4,6},{5,7},{6,4},{7,5},{8,10},{9,11},{10,... | collective-permute-start | bytes 983048 | tf_op jit(solution)/shard_map/ppermute | solution.py:377
  117.8 14.5 %collective-permute-start.17 = (bf16[640,256]{1,0:T(8,128)(2,1)S(1)}, bf16[640,256]{1,0:T(8,128)(2,1)S(1)}, u32[]{:S(2)}, u32[]{:S(2)}) collective-permute-start(bf16[640,256]{1,0:T(8,128)(2,1)S(1)} %maximum_convert_fusion.g0), channel_id=1, source_target_pairs={{0,3},{1,0},{2,1},{3,2},{4,7},{5,4},{6,5},{7,6},{8,11},{9,8},{10,9... | collective-permute-start | bytes 983048 | tf_op jit(solution)/shard_map/ppermute | solution.py:377
  131.6 0.7 copy-start.16
  131.6 0.8 copy-start.17
  132.5 0.7 copy-start.18
  138.7 18.6 %copy-start = (bf16[256,8192]{1,0:T(8,128)(2,1)S(1)}, bf16[256,8192]{1,0:T(8,128)(2,1)}, u32[]{:S(2)}) copy-start(bf16[256,8192]{1,0:T(8,128)(2,1)} %expand.1.bottle_ref.bottles) | copy-start | bytes 12582916
  138.7 18.6 %copy-start.1 = (bf16[256,1024]{1,0:T(8,128)(2,1)S(1)}, bf16[256,1024]{1,0:T(8,128)(2,1)}, u32[]{:S(2)}) copy-start(bf16[256,1024]{1,0:T(8,128)(2,1)} %hid_ref.5) | copy-start | bytes 1572868
  138.7 18.6 %copy-start.3 = (f32[32,256]{1,0:T(8,128)S(1)}, f32[32,256]{1,0:T(8,128)}, u32[]{:S(2)}) copy-start(f32[32,256]{1,0:T(8,128)} %get-tuple-element.44.rank_ref) | copy-start | bytes 98308
  149.1 5.5 %collective-permute-start.18 = (f32[40,256]{1,0:T(8,128)}, f32[40,256]{1,0:T(8,128)S(1)}, u32[]{:S(2)}, u32[]{:S(2)}) collective-permute-start(f32[40,256]{1,0:T(8,128)} %logits.1.l0), channel_id=1, source_target_pairs={{0,1},{1,2},{2,3},{3,0},{4,5},{5,6},{6,7},{7,4},{8,9},{9,10},{10,1... | collective-permute-start | bytes 122888 | tf_op jit(solution)/shard_map/ppermute | solution.py:377
  150.3 5.7 %collective-permute-start.19 = (f32[40,256]{1,0:T(8,128)}, f32[40,256]{1,0:T(8,128)S(1)}, u32[]{:S(2)}, u32[]{:S(2)}) collective-permute-start(f32[40,256]{1,0:T(8,128)} %logits.1.l0), channel_id=1, source_target_pairs={{0,2},{1,3},{2,0},{3,1},{4,6},{5,7},{6,4},{7,5},{8,10},{9,11},{10,... | collective-permute-start | bytes 122888 | tf_op jit(solution)/shard_map/ppermute | solution.py:377
  153.1 4.2 %collective-permute-start.20 = (f32[40,256]{1,0:T(8,128)}, f32[40,256]{1,0:T(8,128)S(1)}, u32[]{:S(2)}, u32[]{:S(2)}) collective-permute-start(f32[40,256]{1,0:T(8,128)} %logits.1.l0), channel_id=1, source_target_pairs={{0,3},{1,0},{2,1},{3,2},{4,7},{5,4},{6,5},{7,6},{8,11},{9,8},{10,9... | collective-permute-start | bytes 122888 | tf_op jit(solution)/shard_map/ppermute | solution.py:377
  157.4 0.8 copy-start.2
Sparse Core Ops, SparseCore 0:
  9.1 34.5 all-gather.2
  46.0 92.3 all-gather.4

commit v4 on v3

--- a/solution.py
+++ b/solution.py
@@ -289,7 +289,7 @@
         in_specs=[smem(), smem()] + [whole()] * 5,
         out_specs=whole(),
         scratch_shapes=[pltpu.VMEM((BUF, B), BF16)],
-        compiler_params=params(),
+        compiler_params=params(24 * 1024 * 1024),
         name="expand",
     )(pos, off, *pieces, pick)
 

time: 173 us -> 173 us (level)
  Pallas kernels: 55 us -> 51.5 us
  waiting for transfers between devices: 61 us -> 63.3 us
    pallas_call x1, Pallas kernels: 5.49 us -> 1.89 us  [expand(): pl.pallas_call(expand_kernel, out_shape=jax.ShapeDtypeStruct((ROWS, ADAPT...]
    all_gather x1, waiting for transfers between devices: 0.01 us -> 2.31 us  [per_device(): up = lax.all_gather(up_weight, ('y', 'x', 'core'), axis=0, tiled=True)]
  transfers between devices with their start and end apart: 23 -> 23, of which waited for: 11 -> 13; matrix products, arithmetic and copies ran while one was open for 1% -> 1% of each run, Pallas kernels for 22% -> 20%
where the time goes in v4:
time: 173 us; the launch traced here: 172 us
  waiting for transfers between devices  63.3 us (37%)
  Pallas kernels  51.5 us (30%)
  starting transfers between devices  36.9 us (21%)
  between operations  13.6 us (8%)
  local copies, waits for them, and re-layouts  6.05 us (3%)
    ppermute x21, waiting for transfers between devices, shifted(): return lax.ppermute(x, axis, [(i, (i + s) % 4) for i in range(4)])  56.2 us
    ppermute x21, starting transfers between devices, shifted(): return lax.ppermute(x, axis, [(i, (i + s) % 4) for i in range(4)])  36.8 us
    pallas_call x1, Pallas kernels, logits_of(): pl.pallas_call(logits_kernel, out_shape=jax.ShapeDtypeStruct((ADAPTERS +...  10.3 us
    pallas_call x1, Pallas kernels, squeeze(): pl.pallas_call(squeeze_kernel, out_shape=[jax.ShapeDtypeStruct((8, CAP, B...  10.2 us
    pallas_call x1, Pallas kernels, join(): pl.pallas_call(join_kernel, out_shape=jax.ShapeDtypeStruct((ROWS, WIDTH),...  7.44 us
    pallas_call x1, Pallas kernels, probe_of(): pl.pallas_call(probe_kernel, out_shape=(jax.ShapeDtypeStruct((ROWS, WIDTH...  7.32 us
    pallas_call x1, Pallas kernels, query_parts(): pl.pallas_call(query_kernel, out_shape=[jax.ShapeDtypeStruct((ROWS, WIDTH...  6.35 us
    unnamed x42, local copies, waits for them, and re-layouts  5.43 us
  transfers between devices with their start and end apart: 23, of which 13 were waited for; matrix products, arithmetic and copies ran while one was open for 1% of the time, Pallas kernels for 20%

profile of v4, /device:TPU:0, one launch (start us, length us, event | category | flops | bytes accessed | tf_op | source)
XLA Modules:
  0.0 172.4 jit_solution(12092227142266477104)
XLA Ops:
  6.5 0.7 all-gather.3.cloned.1.call-update
  7.3 0.0 all-gather.5.cloned.1.call-start
  7.3 2.1 %plan.1 = (bf16[288,1024]{1,0:T(8,128)(2,1)}, f32[32,256]{1,0:T(8,128)}, s32[32,128]{1,0:T(8,128)}) custom-call(s32[8,256]{1,0:T(8,128)} %bitcast.5, bf16[256,1024]{1,0:T(8,128)(2,1)} %hid_ref.5), custom_call_target="tpu_custom_call" | custom-call | tf_op jit(solution)/shard_map/plan/pallas_call | solution.py:67
  9.4 1.6 collective-permute-start
  11.0 2.7 %collective-permute-start.1 = (bf16[288,1024]{1,0:T(8,128)(2,1)}, bf16[288,1024]{1,0:T(8,128)(2,1)S(1)}, u32[]{:S(2)}, u32[]{:S(2)}) collective-permute-start(bf16[288,1024]{1,0:T(8,128)(2,1)} %get-tuple-element.45.ext_ref.refs_0_), channel_id=1, source_target_pairs={{0,16},{8,24},{16,0},{24,8},{1,17},{9,25},{17,1},{25,9},{2,18},{10... | collective-permute-start | bytes 1769480 | tf_op jit(solution)/shard_map/ppermute | solution.py:377
  13.7 1.4 collective-permute-start.2
  15.1 0.7 pad_add_fusion.pos_ref
  15.8 6.4 %query_parts.1 = (bf16[256,1024]{1,0:T(8,128)(2,1)}, bf16[256,1024]{1,0:T(8,128)(2,1)}, bf16[256,1024]{1,0:T(8,128)(2,1)}, bf16[256,1024]{1,0:T(8,128)(2,1)}) custom-call(s32[4]{0:T(128)} %pad_add_fusion.pos_ref, bf16[288,1024]{1,0:T(8,128)(2,1)} %get-tuple-element.45.ext_ref.refs_0_, bf16[1024,4096]{1,0:T(8,128)(2,1)} %weight_ref.2), custom_call_target="tpu_custom_call" | custom-call | tf_op jit(solution)/shard_map/query_parts/pallas_call | solution.py:121
  22.1 2.0 %collective-permute-start.3 = (bf16[256,1024]{1,0:T(8,128)(2,1)}, bf16[256,1024]{1,0:T(8,128)(2,1)S(1)}, u32[]{:S(2)}, u32[]{:S(2)}) collective-permute-start(bf16[256,1024]{1,0:T(8,128)(2,1)} %get-tuple-element.41), channel_id=1, source_target_pairs={{0,1},{1,2},{2,3},{3,0},{4,5},{5,6},{6,7},{7,4},{8,9},{9,10},{10,1... | collective-permute-start | bytes 1572872 | tf_op jit(solution)/shard_map/ppermute | solution.py:377
  24.1 2.2 %collective-permute-start.4 = (bf16[256,1024]{1,0:T(8,128)(2,1)}, bf16[256,1024]{1,0:T(8,128)(2,1)S(1)}, u32[]{:S(2)}, u32[]{:S(2)}) collective-permute-start(bf16[256,1024]{1,0:T(8,128)(2,1)} %get-tuple-element.42), channel_id=1, source_target_pairs={{0,3},{1,0},{2,1},{3,2},{4,7},{5,4},{6,5},{7,6},{8,11},{9,8},{10,9... | collective-permute-start | bytes 1572872 | tf_op jit(solution)/shard_map/ppermute | solution.py:377
  26.3 2.9 %spread.1.pick_ref = bf16[256,4096]{1,0:T(8,128)(2,1)} custom-call(f32[32,256]{1,0:T(8,128)} %get-tuple-element.44.rank_ref), custom_call_target="tpu_custom_call" | custom-call | tf_op jit(solution)/shard_map/spread/pallas_call | solution.py:91
  29.2 8.3 %collective-permute-done.3 = bf16[256,1024]{1,0:T(8,128)(2,1)S(1)} collective-permute-done((bf16[256,1024]{1,0:T(8,128)(2,1)}, bf16[256,1024]{1,0:T(8,128)(2,1)S(1)}, u32[]{:S(2)}, u32[]{:S(2)}) %collective-permute-start.3) | collective-permute-done | bytes 524320 | tf_op jit(solution)/shard_map/ppermute | solution.py:377
  37.5 0.0 collective-permute-done.4
  37.5 0.0 collective-permute-done.refs_1_
  37.6 2.0 %collective-permute-done.1.refs_2_ = bf16[288,1024]{1,0:T(8,128)(2,1)S(1)} collective-permute-done((bf16[288,1024]{1,0:T(8,128)(2,1)}, bf16[288,1024]{1,0:T(8,128)(2,1)S(1)}, u32[]{:S(2)}, u32[]{:S(2)}) %collective-permute-start.1) | collective-permute-done | bytes 589856 | tf_op jit(solution)/shard_map/ppermute | solution.py:377
  39.6 0.0 collective-permute-done.2.refs_3_
  39.6 4.1 %all-gather.3.cloned.1.call-done.refs_4_ = bf16[8,1024,256]{2,1,0:T(8,128)(2,1)} async-done(((bf16[1,1024,256]{2,1,0:T(8,128)(2,1)}), bf16[8,1024,256]{2,1,0:T(8,128)(2,1)}) %all-gather.3.cloned.1.call-update) | async-done | bytes 4194320 | tf_op jit(solution)/shard_map/all_gather | solution.py:400
  43.7 0.0 all-gather.5.cloned.1.call-update
  43.7 3.2 %collective-permute-start.11 = (bf16[256,1024]{1,0:T(8,128)(2,1)}, bf16[256,1024]{1,0:T(8,128)(2,1)S(1)}, u32[]{:S(2)}, u32[]{:S(2)}) collective-permute-start(bf16[256,1024]{1,0:T(8,128)(2,1)} %get-tuple-element.61), channel_id=1, source_target_pairs={{0,2},{1,3},{2,0},{3,1},{4,6},{5,7},{6,4},{7,5},{8,10},{9,11},{10,... | collective-permute-start | bytes 1572872 | tf_op jit(solution)/shard_map/ppermute | solution.py:377
  47.0 10.2 %squeeze.5 = (bf16[8,128,256]{2,1,0:T(8,128)(2,1)}, bf16[8,128,256]{2,1,0:T(8,128)(2,1)}, bf16[8,128,256]{2,1,0:T(8,128)(2,1)}, bf16[8,128,256]{2,1,0:T(8,128)(2,1)}) custom-call(s32[4]{0:T(128)} %pad_add_fusion.pos_ref, bf16[288,1024]{1,0:T(8,128)(2,1)} %get-tuple-element.45.ext_ref.refs_0_, bf16[288,1024]{1,0:T(8,128)(2,1)} %copy-done.9, ...), custom_call_target="tpu_custom_call" | custom-call | tf_op jit(solution)/shard_map/squeeze/pallas_call | solution.py:198
  57.1 1.5 collective-permute-start.5
  58.7 2.7 %collective-permute-start.6 = (bf16[8,128,256]{2,1,0:T(8,128)(2,1)}, bf16[8,128,256]{2,1,0:T(8,128)(2,1)S(1)}, u32[]{:S(2)}, u32[]{:S(2)}) collective-permute-start(bf16[8,128,256]{2,1,0:T(8,128)(2,1)} %get-tuple-element.52), channel_id=1, source_target_pairs={{0,16},{8,24},{16,0},{24,8},{1,17},{9,25},{17,1},{25,9},{2,18},{10... | collective-permute-start | bytes 1572872 | tf_op jit(solution)/shard_map/ppermute | solution.py:377
  61.4 1.5 collective-permute-start.7
  62.8 0.0 collective-permute-done.11
  62.8 0.4 add_convert_fusion.q0
  63.2 0.7 collective-permute-start.12
  63.9 1.9 %collective-permute-start.13 = (bf16[256,1024]{1,0:T(8,128)(2,1)S(1)}, bf16[256,1024]{1,0:T(8,128)(2,1)S(1)}, u32[]{:S(2)}, u32[]{:S(2)}) collective-permute-start(bf16[256,1024]{1,0:T(8,128)(2,1)S(1)} %add_convert_fusion.q0), channel_id=1, source_target_pairs={{0,2},{1,3},{2,0},{3,1},{4,6},{5,7},{6,4},{7,5},{8,10},{9,11},{10,... | collective-permute-start | bytes 1572872 | tf_op jit(solution)/shard_map/ppermute | solution.py:377
  65.8 13.8 %collective-permute-done.5.refs_1_ = bf16[8,128,256]{2,1,0:T(8,128)(2,1)S(1)} collective-permute-done((bf16[8,128,256]{2,1,0:T(8,128)(2,1)}, bf16[8,128,256]{2,1,0:T(8,128)(2,1)S(1)}, u32[]{:S(2)}, u32[]{:S(2)}) %collective-permute-start.5) | collective-permute-done | bytes 524320 | tf_op jit(solution)/shard_map/ppermute | solution.py:377
  79.6 1.6 collective-permute-start.14
  81.2 0.6 slice_reduce_fusion.off_ref
  81.9 9.2 %collective-permute-done.6.refs_2_ = bf16[8,128,256]{2,1,0:T(8,128)(2,1)S(1)} collective-permute-done((bf16[8,128,256]{2,1,0:T(8,128)(2,1)}, bf16[8,128,256]{2,1,0:T(8,128)(2,1)S(1)}, u32[]{:S(2)}, u32[]{:S(2)}) %collective-permute-start.6) | collective-permute-done | bytes 524320 | tf_op jit(solution)/shard_map/ppermute | solution.py:377
  91.1 0.0 collective-permute-done.7.refs_3_
  91.1 0.8 copy-done.17
  91.9 0.3 copy-done.18
  92.2 3.0 %pack.1 = (bf16[640,256]{1,0:T(8,128)(2,1)}, bf16[640,256]{1,0:T(8,128)(2,1)}, bf16[640,256]{1,0:T(8,128)(2,1)}, bf16[640,256]{1,0:T(8,128)(2,1)}) custom-call(s32[4]{0:T(128)} %pad_add_fusion.pos_ref, s32[32]{0:T(128)} %slice_reduce_fusion.off_ref, bf16[8,128,256]{2,1,0:T(8,128)(2,1)} %get-tuple-element.50.refs_0_, bf16[8,128,256]{2,1,0:T(8,128)(2,1)} %copy-done.16, ...), custom_call_target="tpu_custom_call" | custom-call | tf_op jit(solution)/shard_map/pack/pallas_call | solution.py:230
  95.2 3.1 %collective-permute-start.10 = (bf16[640,256]{1,0:T(8,128)(2,1)}, bf16[640,256]{1,0:T(8,128)(2,1)S(1)}, u32[]{:S(2)}, u32[]{:S(2)}) collective-permute-start(bf16[640,256]{1,0:T(8,128)(2,1)} %get-tuple-element.57), channel_id=1, source_target_pairs={{0,3},{1,0},{2,1},{3,2},{4,7},{5,4},{6,5},{7,6},{8,11},{9,8},{10,9... | collective-permute-start | bytes 983048 | tf_op jit(solution)/shard_map/ppermute | solution.py:377
  98.2 0.0 collective-permute-start.8
  98.3 1.5 collective-permute-start.9
  99.8 0.0 collective-permute-done.13.q2
  99.8 0.0 collective-permute-done.14.q3
  99.8 0.8 copy-done.14
  100.6 0.8 copy-done.15
  101.4 7.3 %probe.1 = (bf16[256,1024]{1,0:T(8,128)(2,1)}, f32[8,256]{1,0:T(8,128)}) custom-call(s32[4]{0:T(128)} %pad_add_fusion.pos_ref, bf16[256,1024]{1,0:T(8,128)(2,1)} %copy-done.8, bf16[256,1024]{1,0:T(8,128)(2,1)} %copy-done.13, bf16[256,1024]{1,0:T(8,128)(2,1)} %copy-done.14, bf16[256,1024]{1,0:T(8,128)(2,1)} %copy-done.15, bf16[256,1024]{1,0:T(8,128)(2,1)} %hid_ref.5, ...), custom_call_target="tpu_custom_call" | custom-call | tf_op jit(solution)/shard_map/probe/pallas_call | solution.py:145
  108.8 3.8 %collective-permute-done.10 = bf16[640,256]{1,0:T(8,128)(2,1)S(1)} collective-permute-done((bf16[640,256]{1,0:T(8,128)(2,1)}, bf16[640,256]{1,0:T(8,128)(2,1)S(1)}, u32[]{:S(2)}, u32[]{:S(2)}) %collective-permute-start.10) | collective-permute-done | bytes 327712 | tf_op jit(solution)/shard_map/ppermute | solution.py:377
  112.5 3.3 %collective-permute-done.8 = bf16[640,256]{1,0:T(8,128)(2,1)S(1)} collective-permute-done((bf16[640,256]{1,0:T(8,128)(2,1)}, bf16[640,256]{1,0:T(8,128)(2,1)S(1)}, u32[]{:S(2)}, u32[]{:S(2)}) %collective-permute-start.8) | collective-permute-done | bytes 327712 | tf_op jit(solution)/shard_map/ppermute | solution.py:377
  115.8 0.0 collective-permute-done.9
  115.8 0.2 maximum_convert_fusion.g0
  116.0 0.1 collective-permute-start.15
  116.1 1.7 %collective-permute-start.16 = (bf16[640,256]{1,0:T(8,128)(2,1)S(1)}, bf16[640,256]{1,0:T(8,128)(2,1)S(1)}, u32[]{:S(2)}, u32[]{:S(2)}) collective-permute-start(bf16[640,256]{1,0:T(8,128)(2,1)S(1)} %maximum_convert_fusion.g0), channel_id=1, source_target_pairs={{0,2},{1,3},{2,0},{3,1},{4,6},{5,7},{6,4},{7,5},{8,10},{9,11},{10,... | collective-permute-start | bytes 983048 | tf_op jit(solution)/shard_map/ppermute | solution.py:377
  117.9 1.5 collective-permute-start.17
  119.4 7.2 %collective-permute-done.15.g1 = bf16[640,256]{1,0:T(8,128)(2,1)S(1)} collective-permute-done((bf16[640,256]{1,0:T(8,128)(2,1)S(1)}, bf16[640,256]{1,0:T(8,128)(2,1)S(1)}, u32[]{:S(2)}, u32[]{:S(2)}) %collective-permute-start.15) | collective-permute-done | bytes 327712 | tf_op jit(solution)/shard_map/ppermute | solution.py:377
  126.5 5.0 %collective-permute-done.16.g2 = bf16[640,256]{1,0:T(8,128)(2,1)S(1)} collective-permute-done((bf16[640,256]{1,0:T(8,128)(2,1)S(1)}, bf16[640,256]{1,0:T(8,128)(2,1)S(1)}, u32[]{:S(2)}, u32[]{:S(2)}) %collective-permute-start.16) | collective-permute-done | bytes 327712 | tf_op jit(solution)/shard_map/ppermute | solution.py:377
  131.5 0.6 collective-permute-done.17.g3
  132.2 1.9 %expand.1.bottle_ref.bottles = bf16[256,8192]{1,0:T(8,128)(2,1)S(1)} custom-call(s32[4]{0:T(128)S(1)} %copy-done.6, s32[32]{0:T(128)S(1)} %copy-done.7, bf16[640,256]{1,0:T(8,128)(2,1)S(1)} %maximum_convert_fusion.g0, bf16[640,256]{1,0:T(8,128)(2,1)S(1)} %collective-permute-done.15.g1, bf16[640,256]{1,0:T(8,128)(2,1)S(1)} %collective-permute-done.16.g2, ...), custom_call_target="tpu_custom_call" | custom-call | tf_op jit(solution)/shard_map/expand/pallas_call | solution.py:286
  134.1 1.9 %copy-done = bf16[256,8192]{1,0:T(8,128)(2,1)} copy-done((bf16[256,8192]{1,0:T(8,128)(2,1)}, bf16[256,8192]{1,0:T(8,128)(2,1)S(1)}, u32[]{:S(2)}) %copy-start) | copy-done | bytes 4194328
  136.0 2.3 %all-gather.5.cloned.1.call-done.up_ref = bf16[32,256,1024]{2,1,0:T(8,128)(2,1)} async-done(((bf16[1,256,1024]{2,1,0:T(8,128)(2,1)}), bf16[32,256,1024]{2,1,0:T(8,128)(2,1)}) %all-gather.5.cloned.1.call-update) | async-done | bytes 16777232 | tf_op jit(solution)/shard_map/all_gather | solution.py:407
  138.3 10.3 %logits.1.l0 = f32[40,256]{1,0:T(8,128)} custom-call(bf16[256,8192]{1,0:T(8,128)(2,1)} %copy-done, bf16[256,1024]{1,0:T(8,128)(2,1)} %get-tuple-element.68.probe_ref, f32[8,256]{1,0:T(8,128)} %get-tuple-element.69.own_ref, bf16[32,256,1024]{2,1,0:T(8,128)(2,1)} %all-gather.5.cloned.1.call-done.up_ref), custom_call_target="tpu_custom_call" | custom-call | tf_op jit(solution)/shard_map/logits/pallas_call | solution.py:320
  148.7 1.6 collective-permute-start.18
  150.3 2.9 %collective-permute-start.19 = (f32[40,256]{1,0:T(8,128)}, f32[40,256]{1,0:T(8,128)S(1)}, u32[]{:S(2)}, u32[]{:S(2)}) collective-permute-start(f32[40,256]{1,0:T(8,128)} %logits.1.l0), channel_id=1, source_target_pairs={{0,2},{1,3},{2,0},{3,1},{4,6},{5,7},{6,4},{7,5},{8,10},{9,11},{10,... | collective-permute-start | bytes 122888 | tf_op jit(solution)/shard_map/ppermute | solution.py:377
  153.1 1.4 collective-permute-start.20
  154.5 1.5 collective-permute-done.19.l2
  156.0 1.4 collective-permute-done.20.l3
  157.4 0.8 copy-done.4
  158.1 7.4 %join.1 = bf16[256,1024]{1,0:T(8,128)(2,1)} custom-call(bf16[256,8192]{1,0:T(8,128)(2,1)S(1)} %copy-done.1, f32[40,256]{1,0:T(8,128)S(1)} %copy-done.4, f32[40,256]{1,0:T(8,128)S(1)} %collective-permute-done.18.l1, f32[40,256]{1,0:T(8,128)S(1)} %collective-permute-done.19.l2, f32[40,256]{1,0:T(8,128)S(1)} %collective-permute-done.20.l3, ...), custom_call_target="tpu_custom_call" | custom-call | tf_op jit(solution)/shard_map/join/pallas_call | solution.py:362
  (39 shorter events, 0.1 us)
Async XLA Ops:
  6.5 37.2 %all-gather.3.cloned.1.call-start = ((), (), s32[]{:S(2)}) async-start(), calls=%async_computation | async-start | bytes 4718592 | tf_op jit(solution)/shard_map/all_gather | solution.py:400
  7.3 131.1 %all-gather.5.cloned.1.call-start = ((), (), s32[]{:S(2)}) async-start(), calls=%async_computation.1 | async-start | bytes 17301504 | tf_op jit(solution)/shard_map/all_gather | solution.py:407
  9.4 28.2 %collective-permute-start = (bf16[288,1024]{1,0:T(8,128)(2,1)}, bf16[288,1024]{1,0:T(8,128)(2,1)S(1)}, u32[]{:S(2)}, u32[]{:S(2)}) collective-permute-start(bf16[288,1024]{1,0:T(8,128)(2,1)} %get-tuple-element.45.ext_ref.refs_0_), channel_id=1, source_target_pairs={{0,8},{8,16},{16,24},{24,0},{1,9},{9,17},{17,25},{25,1},{2,10},{10... | collective-permute-start | bytes 1769480 | tf_op jit(solution)/shard_map/ppermute | solution.py:377
  11.0 28.6 %collective-permute-start.1 = (bf16[288,1024]{1,0:T(8,128)(2,1)}, bf16[288,1024]{1,0:T(8,128)(2,1)S(1)}, u32[]{:S(2)}, u32[]{:S(2)}) collective-permute-start(bf16[288,1024]{1,0:T(8,128)(2,1)} %get-tuple-element.45.ext_ref.refs_0_), channel_id=1, source_target_pairs={{0,16},{8,24},{16,0},{24,8},{1,17},{9,25},{17,1},{25,9},{2,18},{10... | collective-permute-start | bytes 1769480 | tf_op jit(solution)/shard_map/ppermute | solution.py:377
  13.7 25.9 %collective-permute-start.2 = (bf16[288,1024]{1,0:T(8,128)(2,1)}, bf16[288,1024]{1,0:T(8,128)(2,1)S(1)}, u32[]{:S(2)}, u32[]{:S(2)}) collective-permute-start(bf16[288,1024]{1,0:T(8,128)(2,1)} %get-tuple-element.45.ext_ref.refs_0_), channel_id=1, source_target_pairs={{0,24},{8,0},{16,8},{24,16},{1,25},{9,1},{17,9},{25,17},{2,26},{10... | collective-permute-start | bytes 1769480 | tf_op jit(solution)/shard_map/ppermute | solution.py:377
  15.8 65.5 %copy-start.20 = (s32[32,128]{1,0:T(8,128)S(1)}, s32[32,128]{1,0:T(8,128)}, u32[]{:S(2)}) copy-start(s32[32,128]{1,0:T(8,128)} %get-tuple-element.38) | copy-start | bytes 49156
  22.1 40.7 %copy-start.12 = (bf16[256,1024]{1,0:T(8,128)(2,1)S(1)}, bf16[256,1024]{1,0:T(8,128)(2,1)}, u32[]{:S(2)}) copy-start(bf16[256,1024]{1,0:T(8,128)(2,1)} %get-tuple-element.58) | copy-start | bytes 1572868
  22.1 15.4 %collective-permute-start.3 = (bf16[256,1024]{1,0:T(8,128)(2,1)}, bf16[256,1024]{1,0:T(8,128)(2,1)S(1)}, u32[]{:S(2)}, u32[]{:S(2)}) collective-permute-start(bf16[256,1024]{1,0:T(8,128)(2,1)} %get-tuple-element.41), channel_id=1, source_target_pairs={{0,1},{1,2},{2,3},{3,0},{4,5},{5,6},{6,7},{7,4},{8,9},{9,10},{10,1... | collective-permute-start | bytes 1572872 | tf_op jit(solution)/shard_map/ppermute | solution.py:377
  24.1 13.4 %collective-permute-start.4 = (bf16[256,1024]{1,0:T(8,128)(2,1)}, bf16[256,1024]{1,0:T(8,128)(2,1)S(1)}, u32[]{:S(2)}, u32[]{:S(2)}) collective-permute-start(bf16[256,1024]{1,0:T(8,128)(2,1)} %get-tuple-element.42), channel_id=1, source_target_pairs={{0,3},{1,0},{2,1},{3,2},{4,7},{5,4},{6,5},{7,6},{8,11},{9,8},{10,9... | collective-permute-start | bytes 1572872 | tf_op jit(solution)/shard_map/ppermute | solution.py:377
  37.6 9.4 %copy-start.9 = (bf16[288,1024]{1,0:T(8,128)(2,1)}, bf16[288,1024]{1,0:T(8,128)(2,1)S(1)}, u32[]{:S(2)}) copy-start(bf16[288,1024]{1,0:T(8,128)(2,1)S(1)} %collective-permute-done.refs_1_) | copy-start | bytes 1769476
  39.6 7.4 %copy-start.10 = (bf16[288,1024]{1,0:T(8,128)(2,1)}, bf16[288,1024]{1,0:T(8,128)(2,1)S(1)}, u32[]{:S(2)}) copy-start(bf16[288,1024]{1,0:T(8,128)(2,1)S(1)} %collective-permute-done.1.refs_2_) | copy-start | bytes 1769476
  39.6 7.4 %copy-start.11 = (bf16[288,1024]{1,0:T(8,128)(2,1)}, bf16[288,1024]{1,0:T(8,128)(2,1)S(1)}, u32[]{:S(2)}) copy-start(bf16[288,1024]{1,0:T(8,128)(2,1)S(1)} %collective-permute-done.2.refs_3_) | copy-start | bytes 1769476
  43.7 19.1 %collective-permute-start.11 = (bf16[256,1024]{1,0:T(8,128)(2,1)}, bf16[256,1024]{1,0:T(8,128)(2,1)S(1)}, u32[]{:S(2)}, u32[]{:S(2)}) collective-permute-start(bf16[256,1024]{1,0:T(8,128)(2,1)} %get-tuple-element.61), channel_id=1, source_target_pairs={{0,2},{1,3},{2,0},{3,1},{4,6},{5,7},{6,4},{7,5},{8,10},{9,11},{10,... | collective-permute-start | bytes 1572872 | tf_op jit(solution)/shard_map/ppermute | solution.py:377
  57.1 22.5 %collective-permute-start.5 = (bf16[8,128,256]{2,1,0:T(8,128)(2,1)}, bf16[8,128,256]{2,1,0:T(8,128)(2,1)S(1)}, u32[]{:S(2)}, u32[]{:S(2)}) collective-permute-start(bf16[8,128,256]{2,1,0:T(8,128)(2,1)} %get-tuple-element.51), channel_id=1, source_target_pairs={{0,8},{8,16},{16,24},{24,0},{1,9},{9,17},{17,25},{25,1},{2,10},{10... | collective-permute-start | bytes 1572872 | tf_op jit(solution)/shard_map/ppermute | solution.py:377
  58.7 32.4 %collective-permute-start.6 = (bf16[8,128,256]{2,1,0:T(8,128)(2,1)}, bf16[8,128,256]{2,1,0:T(8,128)(2,1)S(1)}, u32[]{:S(2)}, u32[]{:S(2)}) collective-permute-start(bf16[8,128,256]{2,1,0:T(8,128)(2,1)} %get-tuple-element.52), channel_id=1, source_target_pairs={{0,16},{8,24},{16,0},{24,8},{1,17},{9,25},{17,1},{25,9},{2,18},{10... | collective-permute-start | bytes 1572872 | tf_op jit(solution)/shard_map/ppermute | solution.py:377
  61.4 70.8 %copy-start.2 = (bf16[256,4096]{1,0:T(8,128)(2,1)S(1)}, bf16[256,4096]{1,0:T(8,128)(2,1)}, u32[]{:S(2)}) copy-start(bf16[256,4096]{1,0:T(8,128)(2,1)} %spread.1.pick_ref) | copy-start | bytes 6291460
  61.4 70.8 %copy-start.6 = (s32[4]{0:T(128)S(1)}, s32[4]{0:T(128)}, u32[]{:S(2)}) copy-start(s32[4]{0:T(128)} %pad_add_fusion.pos_ref) | copy-start | bytes 52
  61.4 29.7 %collective-permute-start.7 = (bf16[8,128,256]{2,1,0:T(8,128)(2,1)}, bf16[8,128,256]{2,1,0:T(8,128)(2,1)S(1)}, u32[]{:S(2)}, u32[]{:S(2)}) collective-permute-start(bf16[8,128,256]{2,1,0:T(8,128)(2,1)} %get-tuple-element.53), channel_id=1, source_target_pairs={{0,24},{8,0},{16,8},{24,16},{1,25},{9,1},{17,9},{25,17},{2,26},{10... | collective-permute-start | bytes 1572872 | tf_op jit(solution)/shard_map/ppermute | solution.py:377
  63.2 36.6 %copy-start.8 = (bf16[256,1024]{1,0:T(8,128)(2,1)}, bf16[256,1024]{1,0:T(8,128)(2,1)S(1)}, u32[]{:S(2)}) copy-start(bf16[256,1024]{1,0:T(8,128)(2,1)S(1)} %add_convert_fusion.q0) | copy-start | bytes 1572868
  63.2 35.0 %collective-permute-start.12 = (bf16[256,1024]{1,0:T(8,128)(2,1)S(1)}, bf16[256,1024]{1,0:T(8,128)(2,1)S(1)}, u32[]{:S(2)}, u32[]{:S(2)}) collective-permute-start(bf16[256,1024]{1,0:T(8,128)(2,1)S(1)} %add_convert_fusion.q0), channel_id=1, source_target_pairs={{0,1},{1,2},{2,3},{3,0},{4,5},{5,6},{6,7},{7,4},{8,9},{9,10},{10,1... | collective-permute-start | bytes 1572872 | tf_op jit(solution)/shard_map/ppermute | solution.py:377
  63.9 35.9 %collective-permute-start.13 = (bf16[256,1024]{1,0:T(8,128)(2,1)S(1)}, bf16[256,1024]{1,0:T(8,128)(2,1)S(1)}, u32[]{:S(2)}, u32[]{:S(2)}) collective-permute-start(bf16[256,1024]{1,0:T(8,128)(2,1)S(1)} %add_convert_fusion.q0), channel_id=1, source_target_pairs={{0,2},{1,3},{2,0},{3,1},{4,6},{5,7},{6,4},{7,5},{8,10},{9,11},{10,... | collective-permute-start | bytes 1572872 | tf_op jit(solution)/shard_map/ppermute | solution.py:377
  79.6 11.5 %copy-start.16 = (bf16[8,128,256]{2,1,0:T(8,128)(2,1)}, bf16[8,128,256]{2,1,0:T(8,128)(2,1)S(1)}, u32[]{:S(2)}) copy-start(bf16[8,128,256]{2,1,0:T(8,128)(2,1)S(1)} %collective-permute-done.5.refs_1_) | copy-start | bytes 1572868
  79.6 20.2 %collective-permute-start.14 = (bf16[256,1024]{1,0:T(8,128)(2,1)S(1)}, bf16[256,1024]{1,0:T(8,128)(2,1)S(1)}, u32[]{:S(2)}, u32[]{:S(2)}) collective-permute-start(bf16[256,1024]{1,0:T(8,128)(2,1)S(1)} %add_convert_fusion.q0), channel_id=1, source_target_pairs={{0,3},{1,0},{2,1},{3,2},{4,7},{5,4},{6,5},{7,6},{8,11},{9,8},{10,9... | collective-permute-start | bytes 1572872 | tf_op jit(solution)/shard_map/ppermute | solution.py:377
  81.9 50.3 %copy-start.7 = (s32[32]{0:T(128)S(1)}, s32[32]{0:T(128)}, u32[]{:S(2)}) copy-start(s32[32]{0:T(128)} %slice_reduce_fusion.off_ref) | copy-start | bytes 388
  91.1 0.8 copy-start.17
  91.1 1.1 copy-start.18
  95.2 20.7 %copy-start.19 = (bf16[640,256]{1,0:T(8,128)(2,1)S(1)}, bf16[640,256]{1,0:T(8,128)(2,1)}, u32[]{:S(2)}) copy-start(bf16[640,256]{1,0:T(8,128)(2,1)} %get-tuple-element.63) | copy-start | bytes 983044
  95.2 17.4 %collective-permute-start.10 = (bf16[640,256]{1,0:T(8,128)(2,1)}, bf16[640,256]{1,0:T(8,128)(2,1)S(1)}, u32[]{:S(2)}, u32[]{:S(2)}) collective-permute-start(bf16[640,256]{1,0:T(8,128)(2,1)} %get-tuple-element.57), channel_id=1, source_target_pairs={{0,3},{1,0},{2,1},{3,2},{4,7},{5,4},{6,5},{7,6},{8,11},{9,8},{10,9... | collective-permute-start | bytes 983048 | tf_op jit(solution)/shard_map/ppermute | solution.py:377
  98.2 17.6 %collective-permute-start.8 = (bf16[640,256]{1,0:T(8,128)(2,1)}, bf16[640,256]{1,0:T(8,128)(2,1)S(1)}, u32[]{:S(2)}, u32[]{:S(2)}) collective-permute-start(bf16[640,256]{1,0:T(8,128)(2,1)} %get-tuple-element.55), channel_id=1, source_target_pairs={{0,1},{1,2},{2,3},{3,0},{4,5},{5,6},{6,7},{7,4},{8,9},{9,10},{10,1... | collective-permute-start | bytes 983048 | tf_op jit(solution)/shard_map/ppermute | solution.py:377
  98.2 1.6 copy-start.13
  98.3 17.6 %collective-permute-start.9 = (bf16[640,256]{1,0:T(8,128)(2,1)}, bf16[640,256]{1,0:T(8,128)(2,1)S(1)}, u32[]{:S(2)}, u32[]{:S(2)}) collective-permute-start(bf16[640,256]{1,0:T(8,128)(2,1)} %get-tuple-element.56), channel_id=1, source_target_pairs={{0,2},{1,3},{2,0},{3,1},{4,6},{5,7},{6,4},{7,5},{8,10},{9,11},{10,... | collective-permute-start | bytes 983048 | tf_op jit(solution)/shard_map/ppermute | solution.py:377
  99.8 0.8 copy-start.14
  100.6 0.8 copy-start.15
  116.0 10.5 %collective-permute-start.15 = (bf16[640,256]{1,0:T(8,128)(2,1)S(1)}, bf16[640,256]{1,0:T(8,128)(2,1)S(1)}, u32[]{:S(2)}, u32[]{:S(2)}) collective-permute-start(bf16[640,256]{1,0:T(8,128)(2,1)S(1)} %maximum_convert_fusion.g0), channel_id=1, source_target_pairs={{0,1},{1,2},{2,3},{3,0},{4,5},{5,6},{6,7},{7,4},{8,9},{9,10},{10,1... | collective-permute-start | bytes 983048 | tf_op jit(solution)/shard_map/ppermute | solution.py:377
  116.1 15.4 %collective-permute-start.16 = (bf16[640,256]{1,0:T(8,128)(2,1)S(1)}, bf16[640,256]{1,0:T(8,128)(2,1)S(1)}, u32[]{:S(2)}, u32[]{:S(2)}) collective-permute-start(bf16[640,256]{1,0:T(8,128)(2,1)S(1)} %maximum_convert_fusion.g0), channel_id=1, source_target_pairs={{0,2},{1,3},{2,0},{3,1},{4,6},{5,7},{6,4},{7,5},{8,10},{9,11},{10,... | collective-permute-start | bytes 983048 | tf_op jit(solution)/shard_map/ppermute | solution.py:377
  117.9 14.3 %collective-permute-start.17 = (bf16[640,256]{1,0:T(8,128)(2,1)S(1)}, bf16[640,256]{1,0:T(8,128)(2,1)S(1)}, u32[]{:S(2)}, u32[]{:S(2)}) collective-permute-start(bf16[640,256]{1,0:T(8,128)(2,1)S(1)} %maximum_convert_fusion.g0), channel_id=1, source_target_pairs={{0,3},{1,0},{2,1},{3,2},{4,7},{5,4},{6,5},{7,6},{8,11},{9,8},{10,9... | collective-permute-start | bytes 983048 | tf_op jit(solution)/shard_map/ppermute | solution.py:377
  134.1 2.0 %copy-start = (bf16[256,8192]{1,0:T(8,128)(2,1)}, bf16[256,8192]{1,0:T(8,128)(2,1)S(1)}, u32[]{:S(2)}) copy-start(bf16[256,8192]{1,0:T(8,128)(2,1)S(1)} %expand.1.bottle_ref.bottles) | copy-start | bytes 12582916
  138.3 19.0 %copy-start.1 = (bf16[256,8192]{1,0:T(8,128)(2,1)S(1)}, bf16[256,8192]{1,0:T(8,128)(2,1)}, u32[]{:S(2)}) copy-start(bf16[256,8192]{1,0:T(8,128)(2,1)} %copy-done) | copy-start | bytes 12582916
  138.3 19.0 %copy-start.3 = (bf16[256,1024]{1,0:T(8,128)(2,1)S(1)}, bf16[256,1024]{1,0:T(8,128)(2,1)}, u32[]{:S(2)}) copy-start(bf16[256,1024]{1,0:T(8,128)(2,1)} %hid_ref.5) | copy-start | bytes 1572868
  138.3 19.0 %copy-start.5 = (f32[32,256]{1,0:T(8,128)S(1)}, f32[32,256]{1,0:T(8,128)}, u32[]{:S(2)}) copy-start(f32[32,256]{1,0:T(8,128)} %get-tuple-element.44.rank_ref) | copy-start | bytes 98308
  148.7 5.9 %collective-permute-start.18 = (f32[40,256]{1,0:T(8,128)}, f32[40,256]{1,0:T(8,128)S(1)}, u32[]{:S(2)}, u32[]{:S(2)}) collective-permute-start(f32[40,256]{1,0:T(8,128)} %logits.1.l0), channel_id=1, source_target_pairs={{0,1},{1,2},{2,3},{3,0},{4,5},{5,6},{6,7},{7,4},{8,9},{9,10},{10,1... | collective-permute-start | bytes 122888 | tf_op jit(solution)/shard_map/ppermute | solution.py:377
  150.3 5.7 %collective-permute-start.19 = (f32[40,256]{1,0:T(8,128)}, f32[40,256]{1,0:T(8,128)S(1)}, u32[]{:S(2)}, u32[]{:S(2)}) collective-permute-start(f32[40,256]{1,0:T(8,128)} %logits.1.l0), channel_id=1, source_target_pairs={{0,2},{1,3},{2,0},{3,1},{4,6},{5,7},{6,4},{7,5},{8,10},{9,11},{10,... | collective-permute-start | bytes 122888 | tf_op jit(solution)/shard_map/ppermute | solution.py:377
  153.1 4.2 %collective-permute-start.20 = (f32[40,256]{1,0:T(8,128)}, f32[40,256]{1,0:T(8,128)S(1)}, u32[]{:S(2)}, u32[]{:S(2)}) collective-permute-start(f32[40,256]{1,0:T(8,128)} %logits.1.l0), channel_id=1, source_target_pairs={{0,3},{1,0},{2,1},{3,2},{4,7},{5,4},{6,5},{7,6},{8,11},{9,8},{10,9... | collective-permute-start | bytes 122888 | tf_op jit(solution)/shard_map/ppermute | solution.py:377
  157.4 0.8 copy-start.4
Sparse Core Ops, SparseCore 0:
  9.1 34.5 all-gather.2
  46.0 92.3 all-gather.4
